TPU v7x, 256 devices: a whole 4x4x8 slice. The times are simulated.
256 devices in a mesh: shard: 32 (over y, z), cent: 8 (over x, core).
Axes of the slice: x: 4, y: 4, z: 8, core: 2. Of those that a mesh axis runs over, the one named last changes fastest.
Arguments:
- queries: bfloat16 [512, 32, 128], P('shard'), may hold values from -0.5 to 0.5
- centroids: bfloat16 [262144, 128], P('cent'), may hold values from -0.5 to 0.5
- passage_tokens: bfloat16 [3072, 128, 128], P('shard'), may hold values from -0.5 to 0.5
- live_token_count: int32 [3072], P('shard'), may hold values from 1 to 128
- passage_home: int32 [3072], replicated, may hold values from 0 to 3071, as said below
- candidates: int32 [512, 256], P('shard', 'cent'), may hold values from 0 to 3071, as said below
Outputs:
- probe_scores: float32 [512, 32, 4], P('shard')
- passage_scores: float32 [512, 256], P('shard', 'cent')
Inputs may be any that keep to these rules, and one draw needn't show every extreme that they name: Every passage id appears once; passage p is stored in row passage_home[p], which shard passage_home[p] // 96 holds. Among the candidates of one device (its 16 queries times its 32 columns), at most 32 are stored on any one shard. Ids may repeat.
All inputs are finite; a program needn't handle non-finite values.
Results may differ from a plain program's by a relative error of at most 0.0003.
Values may be sent and summed in bfloat16 or wider, within the bound.
No kernel may reach another device: no remote copies, remote signals or barrier semaphores. Data moves between devices by JAX's collectives and lax.ppermute only.
A program may use at most 128 MiB of HBM per device.

v0:
```python
import math

import jax
import jax.numpy as jnp
from jax import lax
from jax.sharding import PartitionSpec as P

NPROBE = 4


def merged(part, axis, combine):
    gathered = lax.all_gather(part, axis)

    def take(source):
        return lax.dynamic_index_in_dim(gathered, source, 0, False)

    return lax.fori_loop(
        1, lax.axis_size(axis), lambda source, state: combine(state, take(source)), take(0)
    )


def largest_values(values):
    columns = jnp.arange(values.shape[1], dtype=jnp.int32)[None, :]
    picked = []
    for rank in range(NPROBE):
        best = jnp.max(values, axis=1)
        where_best = jnp.argmax(values, axis=1)
        picked.append(best)
        values = jnp.where(columns == where_best[:, None], -jnp.inf, values)
    return jnp.stack(picked, axis=1)


def keep_top(first, second):
    return largest_values(jnp.concatenate([first, second], axis=1))


def local_probe(queries, centroids):
    emb_width = queries.shape[2]
    query_rows = queries.reshape(-1, emb_width)
    cent_total = centroids.shape[0]
    block_size = math.gcd(cent_total, 4096)
    blocks = centroids.reshape(cent_total // block_size, block_size, emb_width)
    start_top = jnp.full((query_rows.shape[0], NPROBE), -jnp.inf, jnp.float32)

    def advance(top_values, cent_block):
        scores = jnp.einsum("md,cd->mc", query_rows, cent_block, preferred_element_type=jnp.float32)
        return (keep_top(top_values, scores), None)

    top_values, _ = lax.scan(advance, start_top, blocks)
    return top_values


def score_block(query_tile_block, local_rows, passage_tokens, live_token_count):
    passage_row_matrix = passage_tokens[local_rows]
    lengths = live_token_count[local_rows]
    similarity_products = jnp.einsum(
        "mez,miz->mei", query_tile_block, passage_row_matrix, preferred_element_type=jnp.float32
    )
    in_length = (
        jnp.arange(passage_row_matrix.shape[1], dtype=jnp.int32)[None, None, :]
        < lengths[:, None, None]
    )
    similarity_products = jnp.where(in_length, similarity_products, -1e30)
    return jnp.sum(jnp.max(similarity_products, axis=2), axis=1)


def score_slots(query_blocks, local_rows, passage_tokens, live_token_count):
    total_slots = local_rows.shape[0]
    block_size = math.gcd(total_slots, 256)
    grouped_queries = query_blocks.reshape(
        (total_slots // block_size, block_size) + query_blocks.shape[1:]
    )
    gathered_row_groups = local_rows.reshape(total_slots // block_size, block_size)

    def one_group(inputs):
        return score_block(inputs[0], inputs[1], passage_tokens, live_token_count)

    return lax.map(one_group, (grouped_queries, gathered_row_groups)).reshape(total_slots)


def body(queries, centroids, passage_tokens, live_token_count, passage_home, candidates):
    query_count, query_tokens, emb_width = queries.shape
    shards = lax.axis_size("shard")
    stored_count = passage_tokens.shape[0]
    column_count = candidates.shape[1]
    pair_count = query_count * column_count
    capacity = 2 * pair_count // shards
    store_rows = jnp.take(passage_home, candidates.reshape(pair_count), axis=0)
    home_shard = store_rows // stored_count
    local_row = store_rows % stored_count
    onehot = (home_shard[:, None] == jnp.arange(shards, dtype=jnp.int32)[None, :]).astype(jnp.int32)
    slot_position_rank = jnp.sum((jnp.cumsum(onehot, axis=0) - onehot) * onehot, axis=1)
    send_slot = home_shard * capacity + slot_position_rank
    owner_query = jnp.repeat(jnp.arange(query_count, dtype=jnp.int32), column_count)
    send_rows = (
        jnp.zeros((shards * capacity,), jnp.int32)
        .at[send_slot]
        .set(local_row)
        .reshape(shards, capacity)
    )
    top_values = local_probe(queries, centroids)
    top_values = merged(top_values, "cent", keep_top)
    probe_scores = top_values.reshape(query_count, query_tokens, NPROBE)
    query_flat = queries.reshape(query_count, query_tokens * emb_width)
    send_queries = (
        jnp.zeros((shards * capacity, query_tokens * emb_width), queries.dtype)
        .at[send_slot]
        .set(query_flat[owner_query])
    )
    send_queries = send_queries.reshape(shards, capacity, query_tokens * emb_width)
    local_rows = lax.all_to_all(send_rows, "shard", split_axis=0, concat_axis=0, tiled=True)
    per_source = local_rows.shape[1]
    scores = score_slots(
        lax.all_to_all(send_queries, "shard", split_axis=0, concat_axis=0, tiled=True).reshape(
            -1, query_tokens, emb_width
        ),
        local_rows.reshape(-1),
        passage_tokens,
        live_token_count,
    )
    returned = lax.all_to_all(
        scores.reshape(shards, per_source), "shard", split_axis=0, concat_axis=0, tiled=True
    )
    passage_scores = returned.reshape(shards * capacity)[send_slot].reshape(
        query_count, column_count
    )
    return (probe_scores, passage_scores)


def solution(mesh):
    in_specs = (
        P("shard", None, None),
        P("cent", None),
        P("shard", None, None),
        P("shard"),
        P(),
        P("shard", "cent"),
    )
    out_specs = (P("shard", None, None), P("shard", "cent"))
    return jax.shard_map(body, mesh=mesh, in_specs=in_specs, out_specs=out_specs, check_vma=False)
```

profile of v0, /device:TPU:1, one launch (start us, length us, event | category | flops | bytes accessed | tf_op | source)
XLA Modules:
  0.0 347.2 jit_solution(17608009764768799329)
XLA Ops:
  3.0 3.1 gather_fusion.2
  10.9 12.0 %all-to-all-start = ((s32[32,1,32]{2,1,0:T(1,128)}), s32[32,1,32]{2,1,0:T(1,128)S(1)}, u32[]{:S(2)}, u32[]{:S(2)}) async-start(s32[32,1,32]{2,1,0:T(1,128)} %all_to_all.15), calls=%async_computation | async-start | bytes 32768 | tf_op jit(solution)/shard_map/all_to_all | solution.py:111
  24.0 4.4 %gather_fusion.3 = bf16[512,4096]{1,0:T(8,128)(2,1)} fusion(bf16[16,4096]{1,0:T(8,128)(2,1)S(1)} %bitcast.99, s32[1024]{0:T(1024)S(1)} %pad_clamp_fusion.2), kind=kCustom, calls=%fused_computation.3 | custom fusion | bytes 8390656 | tf_op jit(solution)/shard_map/gather | solution.py:108
  28.4 12.4 %scatter_custom_fusion.1 = bf16[1024,4096]{1,0:T(8,128)(2,1)} fusion(s32[512]{0:T(512)S(1)} %bitcast.124, bf16[512,4096]{1,0:T(8,128)(2,1)} %gather_fusion.3, bf16[]{:T(256)} %constant.139.clone.1), kind=kCustom, calls=%fused_computation.42 | custom fusion | bytes 8389120 | tf_op jit(solution)/shard_map/scatter | solution.py:108
  40.8 9.5 %all-to-all-start.1 = ((bf16[32,32,4096]{2,1,0:T(8,128)(2,1)}), bf16[32,32,4096]{2,1,0:T(8,128)(2,1)}, u32[]{:S(2)}, u32[]{:S(2)}) async-start(bf16[32,32,4096]{2,1,0:T(8,128)(2,1)} %bitcast.105), calls=%async_computation.1 | async-start | bytes 16777216 | tf_op jit(solution)/shard_map/all_to_all | solution.py:114
  50.3 137.4 %while.35 = (s32[]{:T(128)}, f32[512,4]{0,1:T(4,128)S(1)}, bf16[8,4096,128]{2,1,0:T(8,128)(2,1)}, bf16[512,128]{1,0:T(8,128)(2,1)S(1)}, s32[]{:T(128)}, /*index=5*/f32[]{:T(128)}) while((s32[]{:T(128)}, f32[512,4]{0,1:T(4,128)S(1)}, bf16[8,4096,128]{2,1,0:T(8,128)(2,1)}, bf16[512,128]{1,0:T(8,128)(2,1)S(1)}, s32[]{:T(128)}, ...), condition=%wide.region_7.8_spmd, body=%wide.region_0.7_spmd.sunk | while | flops 631326208 | bytes 43216456 | solution.py:49
  52.8 4.0 %iota_reduce_fusion.12 = (bf16[512]{0:T(512)(128)(2,1)}, s32[512]{0:T(512)S(1)}) fusion(f32[512,4096]{0,1:T(8,128)S(1)} %bitcast.100, f32[512,4]{0,1:T(4,128)S(1)} %get-tuple-element.339), kind=kLoop, calls=%fused_computation.13.clone.1 | loop fusion | flops 20987392 | bytes 8399872 | tf_op jit(solution)/shard_map/while/body/eval_jaxpr/reduce | solution.py:27
  56.8 3.5 %iota_reduce_fusion.13 = (f32[512]{0:T(512)S(1)}, s32[512]{0:T(512)S(1)}) fusion(f32[512,4096]{0,1:T(8,128)S(1)} %bitcast.101, f32[512,4]{0,1:T(4,128)S(1)} %get-tuple-element.339, s32[512]{0:T(512)S(1)} %get-tuple-element.310), kind=kLoop, calls=%fused_computation.12.clone.1 | loop fusion | flops 25185792 | bytes 8402944 | tf_op jit(solution)/shard_map/while/body/eval_jaxpr/reduce | solution.py:27
  60.4 4.1 %iota_reduce_fusion.14 = (f32[512]{0:T(512)S(1)}, s32[512]{0:T(512)S(1)}) fusion(s32[512]{0:T(512)S(1)} %get-tuple-element.311, f32[512,4096]{0,1:T(8,128)S(1)} %bitcast.102, f32[512,4]{0,1:T(4,128)S(1)} %get-tuple-element.339, s32[512]{0:T(512)S(1)} %get-tuple-element.310), kind=kLoop, calls=%fused_computation.10.clone.1 | loop fusion | flops 29384192 | bytes 8404992 | tf_op jit(solution)/shard_map/while/body/eval_jaxpr/reduce | solution.py:27
  64.5 3.0 select_reduce_fusion.6
  70.0 4.0 %iota_reduce_fusion.12 = (bf16[512]{0:T(512)(128)(2,1)}, s32[512]{0:T(512)S(1)}) fusion(f32[512,4096]{0,1:T(8,128)S(1)} %bitcast.100, f32[512,4]{0,1:T(4,128)S(1)} %get-tuple-element.339), kind=kLoop, calls=%fused_computation.13.clone.1 | loop fusion | flops 20987392 | bytes 8399872 | tf_op jit(solution)/shard_map/while/body/eval_jaxpr/reduce | solution.py:27
  74.0 3.5 %iota_reduce_fusion.13 = (f32[512]{0:T(512)S(1)}, s32[512]{0:T(512)S(1)}) fusion(f32[512,4096]{0,1:T(8,128)S(1)} %bitcast.101, f32[512,4]{0,1:T(4,128)S(1)} %get-tuple-element.339, s32[512]{0:T(512)S(1)} %get-tuple-element.310), kind=kLoop, calls=%fused_computation.12.clone.1 | loop fusion | flops 25185792 | bytes 8402944 | tf_op jit(solution)/shard_map/while/body/eval_jaxpr/reduce | solution.py:27
  77.6 4.1 %iota_reduce_fusion.14 = (f32[512]{0:T(512)S(1)}, s32[512]{0:T(512)S(1)}) fusion(s32[512]{0:T(512)S(1)} %get-tuple-element.311, f32[512,4096]{0,1:T(8,128)S(1)} %bitcast.102, f32[512,4]{0,1:T(4,128)S(1)} %get-tuple-element.339, s32[512]{0:T(512)S(1)} %get-tuple-element.310), kind=kLoop, calls=%fused_computation.10.clone.1 | loop fusion | flops 29384192 | bytes 8404992 | tf_op jit(solution)/shard_map/while/body/eval_jaxpr/reduce | solution.py:27
  81.6 3.0 select_reduce_fusion.6
  87.2 4.0 %iota_reduce_fusion.12 = (bf16[512]{0:T(512)(128)(2,1)}, s32[512]{0:T(512)S(1)}) fusion(f32[512,4096]{0,1:T(8,128)S(1)} %bitcast.100, f32[512,4]{0,1:T(4,128)S(1)} %get-tuple-element.339), kind=kLoop, calls=%fused_computation.13.clone.1 | loop fusion | flops 20987392 | bytes 8399872 | tf_op jit(solution)/shard_map/while/body/eval_jaxpr/reduce | solution.py:27
  91.2 3.5 %iota_reduce_fusion.13 = (f32[512]{0:T(512)S(1)}, s32[512]{0:T(512)S(1)}) fusion(f32[512,4096]{0,1:T(8,128)S(1)} %bitcast.101, f32[512,4]{0,1:T(4,128)S(1)} %get-tuple-element.339, s32[512]{0:T(512)S(1)} %get-tuple-element.310), kind=kLoop, calls=%fused_computation.12.clone.1 | loop fusion | flops 25185792 | bytes 8402944 | tf_op jit(solution)/shard_map/while/body/eval_jaxpr/reduce | solution.py:27
  94.7 4.1 %iota_reduce_fusion.14 = (f32[512]{0:T(512)S(1)}, s32[512]{0:T(512)S(1)}) fusion(s32[512]{0:T(512)S(1)} %get-tuple-element.311, f32[512,4096]{0,1:T(8,128)S(1)} %bitcast.102, f32[512,4]{0,1:T(4,128)S(1)} %get-tuple-element.339, s32[512]{0:T(512)S(1)} %get-tuple-element.310), kind=kLoop, calls=%fused_computation.10.clone.1 | loop fusion | flops 29384192 | bytes 8404992 | tf_op jit(solution)/shard_map/while/body/eval_jaxpr/reduce | solution.py:27
  98.8 3.0 select_reduce_fusion.6
  104.4 4.0 %iota_reduce_fusion.12 = (bf16[512]{0:T(512)(128)(2,1)}, s32[512]{0:T(512)S(1)}) fusion(f32[512,4096]{0,1:T(8,128)S(1)} %bitcast.100, f32[512,4]{0,1:T(4,128)S(1)} %get-tuple-element.339), kind=kLoop, calls=%fused_computation.13.clone.1 | loop fusion | flops 20987392 | bytes 8399872 | tf_op jit(solution)/shard_map/while/body/eval_jaxpr/reduce | solution.py:27
  108.4 3.5 %iota_reduce_fusion.13 = (f32[512]{0:T(512)S(1)}, s32[512]{0:T(512)S(1)}) fusion(f32[512,4096]{0,1:T(8,128)S(1)} %bitcast.101, f32[512,4]{0,1:T(4,128)S(1)} %get-tuple-element.339, s32[512]{0:T(512)S(1)} %get-tuple-element.310), kind=kLoop, calls=%fused_computation.12.clone.1 | loop fusion | flops 25185792 | bytes 8402944 | tf_op jit(solution)/shard_map/while/body/eval_jaxpr/reduce | solution.py:27
  111.9 4.1 %iota_reduce_fusion.14 = (f32[512]{0:T(512)S(1)}, s32[512]{0:T(512)S(1)}) fusion(s32[512]{0:T(512)S(1)} %get-tuple-element.311, f32[512,4096]{0,1:T(8,128)S(1)} %bitcast.102, f32[512,4]{0,1:T(4,128)S(1)} %get-tuple-element.339, s32[512]{0:T(512)S(1)} %get-tuple-element.310), kind=kLoop, calls=%fused_computation.10.clone.1 | loop fusion | flops 29384192 | bytes 8404992 | tf_op jit(solution)/shard_map/while/body/eval_jaxpr/reduce | solution.py:27
  121.5 4.0 %iota_reduce_fusion.12 = (bf16[512]{0:T(512)(128)(2,1)}, s32[512]{0:T(512)S(1)}) fusion(f32[512,4096]{0,1:T(8,128)S(1)} %bitcast.100, f32[512,4]{0,1:T(4,128)S(1)} %get-tuple-element.339), kind=kLoop, calls=%fused_computation.13.clone.1 | loop fusion | flops 20987392 | bytes 8399872 | tf_op jit(solution)/shard_map/while/body/eval_jaxpr/reduce | solution.py:27
  125.5 3.5 %iota_reduce_fusion.13 = (f32[512]{0:T(512)S(1)}, s32[512]{0:T(512)S(1)}) fusion(f32[512,4096]{0,1:T(8,128)S(1)} %bitcast.101, f32[512,4]{0,1:T(4,128)S(1)} %get-tuple-element.339, s32[512]{0:T(512)S(1)} %get-tuple-element.310), kind=kLoop, calls=%fused_computation.12.clone.1 | loop fusion | flops 25185792 | bytes 8402944 | tf_op jit(solution)/shard_map/while/body/eval_jaxpr/reduce | solution.py:27
  129.1 4.1 %iota_reduce_fusion.14 = (f32[512]{0:T(512)S(1)}, s32[512]{0:T(512)S(1)}) fusion(s32[512]{0:T(512)S(1)} %get-tuple-element.311, f32[512,4096]{0,1:T(8,128)S(1)} %bitcast.102, f32[512,4]{0,1:T(4,128)S(1)} %get-tuple-element.339, s32[512]{0:T(512)S(1)} %get-tuple-element.310), kind=kLoop, calls=%fused_computation.10.clone.1 | loop fusion | flops 29384192 | bytes 8404992 | tf_op jit(solution)/shard_map/while/body/eval_jaxpr/reduce | solution.py:27
  138.7 4.0 %iota_reduce_fusion.12 = (bf16[512]{0:T(512)(128)(2,1)}, s32[512]{0:T(512)S(1)}) fusion(f32[512,4096]{0,1:T(8,128)S(1)} %bitcast.100, f32[512,4]{0,1:T(4,128)S(1)} %get-tuple-element.339), kind=kLoop, calls=%fused_computation.13.clone.1 | loop fusion | flops 20987392 | bytes 8399872 | tf_op jit(solution)/shard_map/while/body/eval_jaxpr/reduce | solution.py:27
  142.7 3.5 %iota_reduce_fusion.13 = (f32[512]{0:T(512)S(1)}, s32[512]{0:T(512)S(1)}) fusion(f32[512,4096]{0,1:T(8,128)S(1)} %bitcast.101, f32[512,4]{0,1:T(4,128)S(1)} %get-tuple-element.339, s32[512]{0:T(512)S(1)} %get-tuple-element.310), kind=kLoop, calls=%fused_computation.12.clone.1 | loop fusion | flops 25185792 | bytes 8402944 | tf_op jit(solution)/shard_map/while/body/eval_jaxpr/reduce | solution.py:27
  146.3 4.1 %iota_reduce_fusion.14 = (f32[512]{0:T(512)S(1)}, s32[512]{0:T(512)S(1)}) fusion(s32[512]{0:T(512)S(1)} %get-tuple-element.311, f32[512,4096]{0,1:T(8,128)S(1)} %bitcast.102, f32[512,4]{0,1:T(4,128)S(1)} %get-tuple-element.339, s32[512]{0:T(512)S(1)} %get-tuple-element.310), kind=kLoop, calls=%fused_computation.10.clone.1 | loop fusion | flops 29384192 | bytes 8404992 | tf_op jit(solution)/shard_map/while/body/eval_jaxpr/reduce | solution.py:27
  155.9 4.0 %iota_reduce_fusion.12 = (bf16[512]{0:T(512)(128)(2,1)}, s32[512]{0:T(512)S(1)}) fusion(f32[512,4096]{0,1:T(8,128)S(1)} %bitcast.100, f32[512,4]{0,1:T(4,128)S(1)} %get-tuple-element.339), kind=kLoop, calls=%fused_computation.13.clone.1 | loop fusion | flops 20987392 | bytes 8399872 | tf_op jit(solution)/shard_map/while/body/eval_jaxpr/reduce | solution.py:27
  159.9 3.5 %iota_reduce_fusion.13 = (f32[512]{0:T(512)S(1)}, s32[512]{0:T(512)S(1)}) fusion(f32[512,4096]{0,1:T(8,128)S(1)} %bitcast.101, f32[512,4]{0,1:T(4,128)S(1)} %get-tuple-element.339, s32[512]{0:T(512)S(1)} %get-tuple-element.310), kind=kLoop, calls=%fused_computation.12.clone.1 | loop fusion | flops 25185792 | bytes 8402944 | tf_op jit(solution)/shard_map/while/body/eval_jaxpr/reduce | solution.py:27
  163.4 4.1 %iota_reduce_fusion.14 = (f32[512]{0:T(512)S(1)}, s32[512]{0:T(512)S(1)}) fusion(s32[512]{0:T(512)S(1)} %get-tuple-element.311, f32[512,4096]{0,1:T(8,128)S(1)} %bitcast.102, f32[512,4]{0,1:T(4,128)S(1)} %get-tuple-element.339, s32[512]{0:T(512)S(1)} %get-tuple-element.310), kind=kLoop, calls=%fused_computation.10.clone.1 | loop fusion | flops 29384192 | bytes 8404992 | tf_op jit(solution)/shard_map/while/body/eval_jaxpr/reduce | solution.py:27
  173.1 4.0 %iota_reduce_fusion.12 = (bf16[512]{0:T(512)(128)(2,1)}, s32[512]{0:T(512)S(1)}) fusion(f32[512,4096]{0,1:T(8,128)S(1)} %bitcast.100, f32[512,4]{0,1:T(4,128)S(1)} %get-tuple-element.339), kind=kLoop, calls=%fused_computation.13.clone.1 | loop fusion | flops 20987392 | bytes 8399872 | tf_op jit(solution)/shard_map/while/body/eval_jaxpr/reduce | solution.py:27
  177.1 3.5 %iota_reduce_fusion.13 = (f32[512]{0:T(512)S(1)}, s32[512]{0:T(512)S(1)}) fusion(f32[512,4096]{0,1:T(8,128)S(1)} %bitcast.101, f32[512,4]{0,1:T(4,128)S(1)} %get-tuple-element.339, s32[512]{0:T(512)S(1)} %get-tuple-element.310), kind=kLoop, calls=%fused_computation.12.clone.1 | loop fusion | flops 25185792 | bytes 8402944 | tf_op jit(solution)/shard_map/while/body/eval_jaxpr/reduce | solution.py:27
  180.6 4.1 %iota_reduce_fusion.14 = (f32[512]{0:T(512)S(1)}, s32[512]{0:T(512)S(1)}) fusion(s32[512]{0:T(512)S(1)} %get-tuple-element.311, f32[512,4096]{0,1:T(8,128)S(1)} %bitcast.102, f32[512,4]{0,1:T(4,128)S(1)} %get-tuple-element.339, s32[512]{0:T(512)S(1)} %get-tuple-element.310), kind=kLoop, calls=%fused_computation.10.clone.1 | loop fusion | flops 29384192 | bytes 8404992 | tf_op jit(solution)/shard_map/while/body/eval_jaxpr/reduce | solution.py:27
  187.7 14.6 %all-gather = f32[4096,4]{0,1:T(4,128)S(1)} all-gather(f32[512,4]{0,1:T(4,128)S(1)} %get-tuple-element.168), channel_id=2, replica_groups=mesh['shard'=32,'cent'=8] {'cent'}, dimensions={0}, use_global_device_ids=true | all-gather | bytes 73728 | tf_op jit(solution)/shard_map/all_gather | solution.py:12
  202.4 5.9 %while.36 = (s32[]{:T(128)}, f32[512,4]{0,1:T(4,128)S(1)}, f32[8,512,4]{1,2,0:T(4,128)S(1)}, s32[]{:T(128)}, s32[]{:T(128)}, /*index=5*/s32[]{:T(128)}, f32[]{:T(128)}) while((s32[]{:T(128)}, f32[512,4]{0,1:T(4,128)S(1)}, f32[8,512,4]{1,2,0:T(4,128)S(1)}, s32[]{:T(128)}, s32[]{:T(128)}, /*index=5*/s32[]{:T(128)}, f32[]{:T(128)}) %tuple.103), condition=%wide.region_15.16_spmd, body=%wide.region_8.15_spmd.sunk | while | flops 175621 | bytes 142463 | solution.py:17
  209.5 24.1 %all-to-all-done.1 = bf16[32,32,4096]{2,1,0:T(8,128)(2,1)} async-done(((bf16[32,32,4096]{2,1,0:T(8,128)(2,1)}), bf16[32,32,4096]{2,1,0:T(8,128)(2,1)}, u32[]{:S(2)}, u32[]{:S(2)}) %all-to-all-start.1) | async-done | bytes 8388640 | tf_op jit(solution)/shard_map/all_to_all | solution.py:114
  233.6 9.6 %copy.25 = bf16[128,8,32,128]{3,2,1,0:T(8,128)(2,1)} copy(bf16[128,8,32,128]{3,1,2,0:T(8,128)(2,1)} %bitcast.32) | data formatting | bytes 16777216
  243.2 77.4 %while.37 = (s32[]{:T(128)}, f32[4,256]{1,0:T(4,128)S(1)}, s32[4,256]{1,0:T(4,128)S(1)}, s32[96]{0:T(128)S(1)}, bf16[4,256,32,128]{3,2,1,0:T(8,128)(2,1)}, /*ind...) while((s32[]{:T(128)}, f32[4,256]{1,0:T(4,128)S(1)}, s32[4,256]{1,0:T(4,128)S(1)}, ...), condition=%wide.region_24.25_spmd, body=%wide.region_21.24_spmd.sunk | while | flops 270566912 | bytes 27410024 | solution.py:78
  243.2 8.6 %gather_fusion = bf16[256,128,128]{2,1,0:T(8,128)(2,1)} fusion(bf16[96,128,128]{2,1,0:T(8,128)(2,1)S(1)} %get-tuple-element.394, s32[1024]{0:T(1024)S(1)} %pad_clamp_fusion.5), kind=kCustom, calls=%fused_computation.1.clone.1 | custom fusion | bytes 16778240 | tf_op jit(solution)/shard_map/while/body/eval_jaxpr/gather | solution.py:54
  253.8 8.6 %select_reduce_fusion.8 = f32[256,32]{1,0:T(8,128)S(1)} fusion(bf16[256,128,128]{2,1,0:T(8,128)(2,1)} %gather_fusion, bf16[4,256,32,128]{3,2,1,0:T(8,128)(2,1)} %get-tuple-element.393, s32[]{:T(128)} %get-tuple-element.380, pred[256,128]{1,0:T(8,128)(4,1)S(1)} %iota_compare_fusion.10), kind=kOutput, calls=%fused_computation.35.clone.1 | convolution fusion | flops 270524416 | bytes 10551808 | tf_op jit(solution)/shard_map/while/body/eval_jaxpr/mez,miz->mei/dot_general | solution.py:56
  262.6 8.6 %gather_fusion = bf16[256,128,128]{2,1,0:T(8,128)(2,1)} fusion(bf16[96,128,128]{2,1,0:T(8,128)(2,1)S(1)} %get-tuple-element.394, s32[1024]{0:T(1024)S(1)} %pad_clamp_fusion.5), kind=kCustom, calls=%fused_computation.1.clone.1 | custom fusion | bytes 16778240 | tf_op jit(solution)/shard_map/while/body/eval_jaxpr/gather | solution.py:54
  273.1 8.6 %select_reduce_fusion.8 = f32[256,32]{1,0:T(8,128)S(1)} fusion(bf16[256,128,128]{2,1,0:T(8,128)(2,1)} %gather_fusion, bf16[4,256,32,128]{3,2,1,0:T(8,128)(2,1)} %get-tuple-element.393, s32[]{:T(128)} %get-tuple-element.380, pred[256,128]{1,0:T(8,128)(4,1)S(1)} %iota_compare_fusion.10), kind=kOutput, calls=%fused_computation.35.clone.1 | convolution fusion | flops 270524416 | bytes 10551808 | tf_op jit(solution)/shard_map/while/body/eval_jaxpr/mez,miz->mei/dot_general | solution.py:56
  281.9 8.6 %gather_fusion = bf16[256,128,128]{2,1,0:T(8,128)(2,1)} fusion(bf16[96,128,128]{2,1,0:T(8,128)(2,1)S(1)} %get-tuple-element.394, s32[1024]{0:T(1024)S(1)} %pad_clamp_fusion.5), kind=kCustom, calls=%fused_computation.1.clone.1 | custom fusion | bytes 16778240 | tf_op jit(solution)/shard_map/while/body/eval_jaxpr/gather | solution.py:54
  292.5 8.6 %select_reduce_fusion.8 = f32[256,32]{1,0:T(8,128)S(1)} fusion(bf16[256,128,128]{2,1,0:T(8,128)(2,1)} %gather_fusion, bf16[4,256,32,128]{3,2,1,0:T(8,128)(2,1)} %get-tuple-element.393, s32[]{:T(128)} %get-tuple-element.380, pred[256,128]{1,0:T(8,128)(4,1)S(1)} %iota_compare_fusion.10), kind=kOutput, calls=%fused_computation.35.clone.1 | convolution fusion | flops 270524416 | bytes 10551808 | tf_op jit(solution)/shard_map/while/body/eval_jaxpr/mez,miz->mei/dot_general | solution.py:56
  301.3 8.6 %gather_fusion = bf16[256,128,128]{2,1,0:T(8,128)(2,1)} fusion(bf16[96,128,128]{2,1,0:T(8,128)(2,1)S(1)} %get-tuple-element.394, s32[1024]{0:T(1024)S(1)} %pad_clamp_fusion.5), kind=kCustom, calls=%fused_computation.1.clone.1 | custom fusion | bytes 16778240 | tf_op jit(solution)/shard_map/while/body/eval_jaxpr/gather | solution.py:54
  311.8 8.6 %select_reduce_fusion.8 = f32[256,32]{1,0:T(8,128)S(1)} fusion(bf16[256,128,128]{2,1,0:T(8,128)(2,1)} %gather_fusion, bf16[4,256,32,128]{3,2,1,0:T(8,128)(2,1)} %get-tuple-element.393, s32[]{:T(128)} %get-tuple-element.380, pred[256,128]{1,0:T(8,128)(4,1)S(1)} %iota_compare_fusion.10), kind=kOutput, calls=%fused_computation.35.clone.1 | convolution fusion | flops 270524416 | bytes 10551808 | tf_op jit(solution)/shard_map/while/body/eval_jaxpr/mez,miz->mei/dot_general | solution.py:56
  321.3 13.1 %all-to-all-start.2 = ((f32[32,1,32]{2,1,0:T(1,128)}), f32[32,1,32]{2,1,0:T(1,128)S(1)}, u32[]{:S(2)}, u32[]{:S(2)}) async-start(f32[32,1,32]{2,1,0:T(1,128)} %all_to_all.18), calls=%async_computation.2 | async-start | bytes 32768 | tf_op jit(solution)/shard_map/all_to_all | solution.py:121
  335.1 7.9 %all-to-all-done.2 = f32[32,1,32]{2,1,0:T(1,128)S(1)} async-done(((f32[32,1,32]{2,1,0:T(1,128)}), f32[32,1,32]{2,1,0:T(1,128)S(1)}, u32[]{:S(2)}, u32[]{:S(2)}) %all-to-all-start.2) | async-done | bytes 4128 | tf_op jit(solution)/shard_map/all_to_all | solution.py:121
  (162 shorter events, 64.5 us)
Async XLA Ops:
  0.6 2.4 copy-start
  10.9 29.9 %all-to-all-start = ((s32[32,1,32]{2,1,0:T(1,128)}), s32[32,1,32]{2,1,0:T(1,128)S(1)}, u32[]{:S(2)}, u32[]{:S(2)}) async-start(s32[32,1,32]{2,1,0:T(1,128)} %all_to_all.15), calls=%async_computation | async-start | bytes 32768 | tf_op jit(solution)/shard_map/all_to_all | solution.py:111
  40.8 9.5 %copy-start.3 = (bf16[16,32,128]{2,1,0:T(8,128)(2,1)S(1)}, bf16[16,32,128]{2,1,0:T(8,128)(2,1)}, u32[]{:S(2)}) copy-start(bf16[16,32,128]{2,1,0:T(8,128)(2,1)} %param.12) | copy-start | bytes 393220
  40.8 192.8 %all-to-all-start.1 = ((bf16[32,32,4096]{2,1,0:T(8,128)(2,1)}), bf16[32,32,4096]{2,1,0:T(8,128)(2,1)}, u32[]{:S(2)}, u32[]{:S(2)}) async-start(bf16[32,32,4096]{2,1,0:T(8,128)(2,1)} %bitcast.105), calls=%async_computation.1 | async-start | bytes 16777216 | tf_op jit(solution)/shard_map/all_to_all | solution.py:114
  233.6 9.6 %copy-start.1 = (s32[96]{0:T(128)S(1)}, s32[96]{0:T(128)}, u32[]{:S(2)}) copy-start(s32[96]{0:T(128)} %param.15) | copy-start | bytes 1156
  233.6 9.6 %copy-start.2 = (bf16[96,128,128]{2,1,0:T(8,128)(2,1)S(1)}, bf16[96,128,128]{2,1,0:T(8,128)(2,1)}, u32[]{:S(2)}) copy-start(bf16[96,128,128]{2,1,0:T(8,128)(2,1)} %param.14) | copy-start | bytes 9437188
  321.3 21.7 %all-to-all-start.2 = ((f32[32,1,32]{2,1,0:T(1,128)}), f32[32,1,32]{2,1,0:T(1,128)S(1)}, u32[]{:S(2)}, u32[]{:S(2)}) async-start(f32[32,1,32]{2,1,0:T(1,128)} %all_to_all.18), calls=%async_computation.2 | async-start | bytes 32768 | tf_op jit(solution)/shard_map/all_to_all | solution.py:121
where the time goes:
time: 348 us; the launch traced here: 347 us
  other arithmetic  126 us (36%)
  local copies, waits for them, and re-layouts  83.7 us (24%)
  matrix products  54.2 us (16%)
  starting transfers between devices  34.6 us (10%)
  waiting for transfers between devices  32 us (9%)
  blocking collectives  14.6 us (4%)
    another operation x45, other arithmetic, largest_values(): where_best = jnp.argmax(values, axis=1)  97.8 us
    gather x4, local copies, waits for them, and re-layouts, score_block(): passage_row_matrix = passage_tokens[local_rows]  34.3 us
    dot_general x4, matrix products, score_block(): jnp.einsum('mez,miz->mei', query_tile_block, passage_row_matrix, preferre...  34.3 us
    reduce_max x52, other arithmetic, largest_values(): best = jnp.max(values, axis=1)  24.7 us
    all_to_all x1, waiting for transfers between devices, body(): lax.all_to_all(send_queries, 'shard', split_axis=0, concat_axis=0, tiled=...  24.1 us
    dot_general x8, matrix products, advance(): jnp.einsum('md,cd->mc', query_rows, cent_block, preferred_element_type=jn...  19.9 us
    all_gather x1, blocking collectives, merged(): gathered = lax.all_gather(part, axis)  14.6 us
    all_to_all x1, starting transfers between devices, body(): lax.all_to_all(scores.reshape(shards, per_source), 'shard', split_axis=0,...  13.1 us
  transfers between devices with their start and end apart: 3, of which 2 were waited for; matrix products, arithmetic and copies ran while one was open for 47% of the time, Pallas kernels for 0%

commit v1 on v0

v1 whole, which is shorter than its diff:
```python
import functools

import jax
import jax.numpy as jnp
from jax import lax
from jax.experimental import pallas as pl
from jax.experimental.pallas import tpu as pltpu
from jax.sharding import PartitionSpec as P

NPROBE = 4
LANES = 128
VMEM_LIMIT = 60 * 1024 * 1024
LEVELS = 3
GROUP = 16


def insert(running, x):
    out = []
    for rank, held in enumerate(running):
        out.append(jnp.maximum(held, x))
        if rank + 1 < len(running):
            x = jnp.minimum(held, x)
    return out


def streams(levels):
    return [2] * levels + [NPROBE]


def feed(xs, lists):
    for level in range(len(lists) - 1):
        half = len(xs) // 2
        losers = [jnp.minimum(a, b) for a, b in zip(xs[:half], xs[half:])]
        xs = [jnp.maximum(a, b) for a, b in zip(xs[:half], xs[half:])]
        for x in losers:
            lists[level] = insert(lists[level], x)
    for x in xs:
        lists[-1] = insert(lists[-1], x)


def merge_lists(a, b):
    m = [jnp.maximum(a[i], b[NPROBE - 1 - i]) for i in range(NPROBE)]
    for i, j in ((0, 2), (1, 3), (0, 1), (2, 3)):
        m[i], m[j] = jnp.maximum(m[i], m[j]), jnp.minimum(m[i], m[j])
    return m


def fold_sublanes(lists):
    for shift in (4, 2, 1):
        lists = merge_lists(lists, [pltpu.roll(t, shift, 0) for t in lists])
    return lists


def probe_kernel(q_ref, c_ref, o_ref, list_ref):
    step = pl.program_id(0)
    kept = streams(LEVELS)
    nq = q_ref.shape[0]

    @pl.when(step == 0)
    def _():
        list_ref[...] = jnp.full(list_ref.shape, -jnp.inf, jnp.float32)

    scores = lax.dot_general(
        c_ref[...], q_ref[...], (((1,), (1,)), ((), ())), preferred_element_type=jnp.float32
    )
    for col in range(0, nq, LANES):
        at = 0
        lists = []
        for k in kept:
            lists.append([list_ref[at + a, :, col : col + LANES] for a in range(k)])
            at += k
        for row in range(0, scores.shape[0], 8 * GROUP):
            feed([scores[row + 8 * r : row + 8 * r + 8, col : col + LANES] for r in range(GROUP)], lists)
        at = 0
        for held in lists:
            for a, t in enumerate(held):
                list_ref[at + a, :, col : col + LANES] = t
            at += len(held)

    @pl.when(step == pl.num_programs(0) - 1)
    def _():
        for tile in range(nq // LANES):
            at = 0
            lists = []
            for k in kept:
                lists.append([list_ref[at + a, :, tile * LANES : (tile + 1) * LANES] for a in range(k)])
                at += k
            top = lists[-1]
            for held in lists[:-1]:
                for x in held:
                    top = insert(top, x)
            top = fold_sublanes(top)
            for rank in range(NPROBE):
                row = rank * (nq // LANES) + tile
                o_ref[row : row + 1, :] = top[rank][0:1]


def probe(queries, centroids, block=4096):
    nq, dim = queries.shape
    total = centroids.shape[0]
    rows = NPROBE * nq // LANES
    return pl.pallas_call(
        probe_kernel,
        grid=(total // block,),
        in_specs=[pl.BlockSpec((nq, dim), lambda i: (0, 0)), pl.BlockSpec((block, dim), lambda i: (i, 0))],
        out_specs=pl.BlockSpec((rows, LANES), lambda i: (0, 0)),
        out_shape=jax.ShapeDtypeStruct((rows, LANES), jnp.float32),
        scratch_shapes=[pltpu.VMEM((sum(streams(LEVELS)), 8, nq), jnp.float32)],
        compiler_params=pltpu.CompilerParams(vmem_limit_bytes=VMEM_LIMIT),
        cost_estimate=pl.CostEstimate(
            flops=40 * nq * total * dim // 10, bytes_accessed=2 * total * dim, transcendentals=0
        ),
        name="probe",
    )(queries, centroids)


def prepare_kernel(count_ref, p_ref, home_ref, cand_ref, x_ref, shard_ref, local_ref):
    rows = lax.broadcasted_iota(jnp.int32, p_ref.shape[1:], 0)

    def one(p, carry):
        tokens = p_ref[p].astype(jnp.float32)
        x_ref[p] = jnp.where(rows < count_ref[p], tokens, tokens[0:1]).astype(x_ref.dtype)
        return carry

    lax.fori_loop(0, p_ref.shape[0], one, 0, unroll=2)
    nq, nk = cand_ref.shape
    cand = jnp.concatenate([cand_ref[...], jnp.zeros((nq, LANES - nk), jnp.int32)], axis=1)
    block, lane = cand // LANES, cand % LANES
    store = jnp.zeros((nq, LANES), jnp.int32)
    for b in range(home_ref.shape[0]):
        line = jnp.broadcast_to(home_ref[b : b + 1, :], (nq, LANES))
        store = jnp.where(block == b, jnp.take_along_axis(line, lane, axis=1), store)
    shard_ref[...] = store // p_ref.shape[0]
    local_ref[...] = store % p_ref.shape[0]


def prepare(counts, passages, home, candidates):
    nq = candidates.shape[0]
    index = jax.ShapeDtypeStruct((nq, LANES), jnp.int32)
    vmem = pl.BlockSpec(memory_space=pltpu.VMEM)
    return pl.pallas_call(
        prepare_kernel,
        in_specs=[pl.BlockSpec(memory_space=pltpu.SMEM), vmem, vmem, vmem],
        out_specs=[vmem, vmem, vmem],
        out_shape=[jax.ShapeDtypeStruct(passages.shape, passages.dtype), index, index],
        compiler_params=pltpu.CompilerParams(vmem_limit_bytes=VMEM_LIMIT),
        cost_estimate=pl.CostEstimate(flops=10**9, bytes_accessed=4 * passages.size, transcendentals=0),
        name="prepare",
    )(counts, passages, home.reshape(-1, LANES), candidates)


def maxsim_kernel(g_ref, x_ref, o_ref, best_ref, *, per, width, tokens):
    count, length, dim = x_ref.shape
    columns = g_ref.shape[0]

    def one(g, carry):
        at = pl.multiple_of(g * per, per)
        lhs = x_ref[pl.ds(at, per)].reshape(per * length, dim)
        for col in range(0, columns, width):
            dots = lax.dot_general(
                lhs, g_ref[col : col + width, :], (((1,), (1,)), ((), ())), preferred_element_type=jnp.float32
            )
            best = jnp.max(dots.reshape(per, length // 8, 8, width), axis=1)
            best_ref[pl.ds(at, per), col : col + width] = jnp.max(best, axis=1)
        return carry

    lax.fori_loop(0, count // per, one, 0)
    nq = o_ref.shape[0]
    owner = lax.broadcasted_iota(jnp.int32, (nq, columns), 1) // tokens
    pick = (owner == lax.broadcasted_iota(jnp.int32, (nq, columns), 0)).astype(jnp.bfloat16)
    rest = best_ref[...]
    total = jnp.zeros((nq, best_ref.shape[0]), jnp.float32)
    for _ in range(3):
        part = rest.astype(jnp.bfloat16)
        rest = rest - part.astype(jnp.float32)
        total += lax.dot_general(pick, part, (((1,), (1,)), ((), ())), preferred_element_type=jnp.float32)
    o_ref[...] = total


def maxsim(gathered, prepared, tokens):
    columns, dim = gathered.shape
    count, length, _ = prepared.shape
    nq = columns // tokens
    return pl.pallas_call(
        functools.partial(maxsim_kernel, per=16, width=512, tokens=tokens),
        out_shape=jax.ShapeDtypeStruct((nq, LANES), jnp.float32),
        scratch_shapes=[pltpu.VMEM((LANES, columns), jnp.float32)],
        compiler_params=pltpu.CompilerParams(vmem_limit_bytes=VMEM_LIMIT),
        cost_estimate=pl.CostEstimate(
            flops=2 * columns * count * length * dim, bytes_accessed=4 * prepared.size, transcendentals=0
        ),
        name="maxsim",
    )(gathered, prepared)


def finish_kernel(r_ref, shard_ref, local_ref, probe_ref, score_ref, *, shards, cents):
    lines = r_ref.shape[0] // cents
    half = shard_ref.shape[0] // 2
    nk = score_ref.shape[1]
    for j in range(2):
        home = shard_ref[pl.ds(j, half, stride=2), :]
        local = local_ref[pl.ds(j, half, stride=2), :]
        score = jnp.zeros(home.shape, jnp.float32)
        for s in range(shards):
            table = r_ref[pl.ds(2 * s + j, cents, stride=lines), :]
            score = jnp.where(home == s, jnp.take_along_axis(table, local, axis=1), score)
        score_ref[pl.ds(j, half, stride=2), :] = score[:, :nk]
    first = 2 * shards
    tiles = (lines - first) // NPROBE
    nt = probe_ref.shape[2]
    for tile in range(tiles):
        top = fold_sublanes(
            [r_ref[pl.ds(first + rank * tiles + tile, cents, stride=lines), :] for rank in range(NPROBE)]
        )
        four = jnp.concatenate([t[0:1] for t in top], axis=0)
        for i in range(LANES // nt):
            probe_ref[tile * (LANES // nt) + i] = four[:, i * nt : (i + 1) * nt]


def finish(received, shard_index, local_index, shards, cents, nq, nt, nk):
    return pl.pallas_call(
        functools.partial(finish_kernel, shards=shards, cents=cents),
        out_shape=[
            jax.ShapeDtypeStruct((nq, NPROBE, nt), jnp.float32),
            jax.ShapeDtypeStruct((nq, nk), jnp.float32),
        ],
        compiler_params=pltpu.CompilerParams(vmem_limit_bytes=VMEM_LIMIT),
        name="finish",
    )(received, shard_index, local_index)


def spread(block, copies):
    return jnp.broadcast_to(block[None], (copies,) + block.shape).reshape((-1,) + block.shape[1:])


def body(queries, centroids, passages, counts, home, candidates):
    nq, nt, dim = queries.shape
    nk = candidates.shape[1]
    shards, cents = lax.axis_size("shard"), lax.axis_size("cent")
    mine = nq // cents
    own = lax.dynamic_slice_in_dim(queries, lax.axis_index("cent") * mine, mine, 0).reshape(mine * nt, dim)
    gathered = lax.all_to_all(spread(own, shards), "shard", 0, 0, tiled=True)
    lists = probe(queries.reshape(nq * nt, dim), centroids)
    prepared, shard_index, local_index = prepare(counts, passages, home, candidates)
    table = maxsim(gathered, prepared, nt)
    returned = lax.all_to_all(table, "shard", 0, 0, tiled=True)
    final = spread(jnp.concatenate([returned, lists], axis=0), cents)
    received = lax.all_to_all(final, "cent", 0, 0, tiled=True)
    probe_scores, passage_scores = finish(received, shard_index, local_index, shards, cents, nq, nt, nk)
    return jnp.transpose(probe_scores, (0, 2, 1)), passage_scores


def solution(mesh):
    in_specs = (
        P("shard", None, None),
        P("cent", None),
        P("shard", None, None),
        P("shard"),
        P(),
        P("shard", "cent"),
    )
    out_specs = (P("shard", None, None), P("shard", "cent"))
    return jax.shard_map(body, mesh=mesh, in_specs=in_specs, out_specs=out_specs, check_vma=False)
```

time: 348 us -> 87.4 us (0.25)
  other arithmetic: 126 us -> 0.7 us
  local copies, waits for them, and re-layouts: 83.7 us -> 2.45 us
  matrix products: 54.2 us -> 0 us
  Pallas kernels: 0 us -> 40.5 us
  waiting for transfers between devices: 32 us -> 9.8 us
  starting transfers between devices: 34.6 us -> 19.5 us
    another operation x62 -> x0, other arithmetic: 99.2 us -> none  [the longest x45 97.8 us: largest_values(): where_best = jnp.argmax(values, axis=1)]
    dot_general x12 -> x0, matrix products: 54.2 us -> none  [the longest x4 34.3 us: score_block(): jnp.einsum('mez,miz->mei', query_tile_block, passage_row_matrix, preferre...]
    gather x11 -> x0, local copies, waits for them, and re-layouts: 51.6 us -> none  [the longest x4 34.3 us: score_block(): passage_row_matrix = passage_tokens[local_rows]]
    pallas_call x0 -> x4, Pallas kernels: none -> 40.5 us  [the longest x1 17.5 us: maxsim(): pl.pallas_call(functools.partial(maxsim_kernel, per=16, width=512, tokens...]
    reduce_max x52 -> x0, other arithmetic: 24.7 us -> none  [largest_values(): best = jnp.max(values, axis=1)]
    all_to_all x3 -> x2, waiting for transfers between devices: 32 us -> 9.8 us  [the longest x1 9.8 us: body(): gathered = lax.all_to_all(spread(own, shards), 'shard', 0, 0, tiled=True)]
    all_to_all x3 -> x2, starting transfers between devices: 34.6 us -> 19.5 us  [the longest x1 12 us: body(): gathered = lax.all_to_all(spread(own, shards), 'shard', 0, 0, tiled=True)]
    scatter x2 -> x0, local copies, waits for them, and re-layouts: 14.9 us -> none  [the longest x1 12.4 us: body(): send_queries = jnp.zeros((shards * capacity, query_tokens * emb_width), q...]
  transfers between devices with their start and end apart: 3 -> 2, of which waited for: 2 -> 1; matrix products, arithmetic and copies ran while one was open for 47% -> 0% of each run, Pallas kernels for 0% -> 24%
where the time goes in v1:
time: 87.4 us; the launch traced here: 86.9 us
  Pallas kernels  40.5 us (46%)
  starting transfers between devices  19.5 us (22%)
  blocking collectives  13.3 us (15%)
  waiting for transfers between devices  9.8 us (11%)
  local copies, waits for them, and re-layouts  2.45 us (3%)
    pallas_call x1, Pallas kernels, maxsim(): pl.pallas_call(functools.partial(maxsim_kernel, per=16, width=512, tokens...  17.5 us
    pallas_call x1, Pallas kernels, probe(): pl.pallas_call(probe_kernel, grid=(total // block,), in_specs=[pl.BlockSp...  16.7 us
    all_to_all x1, blocking collectives, body(): received = lax.all_to_all(final, 'cent', 0, 0, tiled=True)  13.3 us
    all_to_all x1, starting transfers between devices, body(): gathered = lax.all_to_all(spread(own, shards), 'shard', 0, 0, tiled=True)  12 us
    all_to_all x1, waiting for transfers between devices, body(): gathered = lax.all_to_all(spread(own, shards), 'shard', 0, 0, tiled=True)  9.8 us
    all_to_all x1, starting transfers between devices, body(): returned = lax.all_to_all(table, 'shard', 0, 0, tiled=True)  7.49 us
    pallas_call x1, Pallas kernels, prepare(): pl.pallas_call(prepare_kernel, in_specs=[pl.BlockSpec(memory_space=pltpu....  4.51 us
    pallas_call x1, Pallas kernels, finish(): pl.pallas_call(functools.partial(finish_kernel, shards=shards, cents=cent...  1.79 us
  transfers between devices with their start and end apart: 2, of which 1 were waited for; matrix products, arithmetic and copies ran while one was open for 0% of the time, Pallas kernels for 24%

profile of v1, /device:TPU:1, one launch (start us, length us, event | category | flops | bytes accessed | tf_op | source)
XLA Modules:
  0.0 86.9 jit_solution(3268390464013551848)
XLA Ops:
  0.6 0.7 constant_dynamic-slice_fusion
  1.4 0.9 %broadcast_in_dim.14 = bf16[32,64,128]{2,1,0:T(8,128)(2,1)} broadcast(bf16[64,128]{1,0:T(8,128)(2,1)S(1)} %bitcast.11), dimensions={1,2} | broadcast | bytes 540672 | tf_op jit(solution)/shard_map/broadcast_in_dim | solution.py:233
  2.3 12.0 %all-to-all-start = ((bf16[32,64,128]{2,1,0:T(8,128)(2,1)}), bf16[32,64,128]{2,1,0:T(8,128)(2,1)S(1)}, u32[]{:S(2)}, u32[]{:S(2)}) async-start(bf16[32,64,128]{2,1,0:T(8,128)(2,1)} %broadcast_in_dim.14), calls=%async_computation | async-start | bytes 1048576 | tf_op jit(solution)/shard_map/all_to_all | solution.py:242
  14.3 4.5 %prepare.1 = (bf16[96,128,128]{2,1,0:T(8,128)(2,1)}, s32[16,128]{1,0:T(8,128)}, s32[16,128]{1,0:T(8,128)}) custom-call(s32[96]{0:T(128)} %count_ref.1, bf16[96,128,128]{2,1,0:T(8,128)(2,1)} %p_ref.1, s32[24,128]{1,0:T(8,128)} %bitcast.15, s32[16,32]{1,0:T(8,128)} %cand_ref.1), custom_call_target="tpu_custom_call" | custom-call | flops 1000000000 | bytes 6291456 | tf_op jit(solution)/shard_map/prepare/pallas_call | solution.py:141
  18.8 9.8 %all-to-all-done = bf16[32,64,128]{2,1,0:T(8,128)(2,1)S(1)} async-done(((bf16[32,64,128]{2,1,0:T(8,128)(2,1)}), bf16[32,64,128]{2,1,0:T(8,128)(2,1)S(1)}, u32[]{:S(2)}, u32[]{:S(2)}) %all-to-all-start) | async-done | bytes 524320 | tf_op jit(solution)/shard_map/all_to_all | solution.py:242
  28.6 0.0 copy-start
  28.6 0.8 copy-done
  29.4 17.5 %maxsim.1 = f32[64,128]{1,0:T(8,128)} custom-call(bf16[2048,128]{1,0:T(8,128)(2,1)} %bitcast.9, bf16[96,128,128]{2,1,0:T(8,128)(2,1)} %get-tuple-element.7.x_ref), custom_call_target="tpu_custom_call" | custom-call | flops 6442450944 | bytes 6291456 | tf_op jit(solution)/shard_map/maxsim/pallas_call | solution.py:184
  46.9 7.5 %all-to-all-start.1 = ((f32[32,2,128]{2,1,0:T(2,128)}), f32[32,2,128]{2,1,0:T(2,128)S(1)}, u32[]{:S(2)}, u32[]{:S(2)}) async-start(f32[32,2,128]{2,1,0:T(2,128)} %bitcast.12), calls=%async_computation.1 | async-start | bytes 65536 | tf_op jit(solution)/shard_map/all_to_all | solution.py:246
  54.4 16.7 %probe.1 = f32[16,128]{1,0:T(8,128)} custom-call(bf16[512,128]{1,0:T(8,128)(2,1)} %bitcast.13, bf16[32768,128]{1,0:T(8,128)(2,1)} %c_ref.1), custom_call_target="tpu_custom_call" | custom-call | flops 8589934592 | bytes 8388608 | tf_op jit(solution)/shard_map/probe/pallas_call | solution.py:102
  71.1 0.0 all-to-all-done.1
  71.1 0.7 pad_maximum_fusion
  71.8 13.3 %all_to_all.28 = f32[8,80,128]{2,1,0:T(8,128)} all-to-all(f32[8,80,128]{2,1,0:T(8,128)S(1)} %broadcast_in_dim.15), channel_id=1, replica_groups=mesh['shard'=32,'cent'=8] {'cent'}, dimensions={0} | all-to-all | bytes 655360 | tf_op jit(solution)/shard_map/all_to_all | solution.py:248
  85.1 1.8 %finish.1 = (f32[16,4,32]{2,1,0:T(4,128)}, f32[16,32]{1,0:T(8,128)}) custom-call(f32[640,128]{1,0:T(8,128)} %bitcast.8, s32[16,128]{1,0:T(8,128)} %get-tuple-element.8.shard_ref, s32[16,128]{1,0:T(8,128)} %get-tuple-element.9.local_ref), custom_call_target="tpu_custom_call" | custom-call | tf_op jit(solution)/shard_map/finish/pallas_call | solution.py:221
  (1 shorter events, 0.0 us)
Async XLA Ops:
  2.3 26.4 %all-to-all-start = ((bf16[32,64,128]{2,1,0:T(8,128)(2,1)}), bf16[32,64,128]{2,1,0:T(8,128)(2,1)S(1)}, u32[]{:S(2)}, u32[]{:S(2)}) async-start(bf16[32,64,128]{2,1,0:T(8,128)(2,1)} %broadcast_in_dim.14), calls=%async_computation | async-start | bytes 1048576 | tf_op jit(solution)/shard_map/all_to_all | solution.py:242
  28.6 0.8 copy-start
  46.9 24.2 %all-to-all-start.1 = ((f32[32,2,128]{2,1,0:T(2,128)}), f32[32,2,128]{2,1,0:T(2,128)S(1)}, u32[]{:S(2)}, u32[]{:S(2)}) async-start(f32[32,2,128]{2,1,0:T(2,128)} %bitcast.12), calls=%async_computation.1 | async-start | bytes 65536 | tf_op jit(solution)/shard_map/all_to_all | solution.py:246

commit v2 on v1

--- a/solution.py
+++ b/solution.py
@@ -9,9 +9,12 @@
 
 NPROBE = 4
 LANES = 128
-VMEM_LIMIT = 60 * 1024 * 1024
+MIB = 1024 * 1024
 LEVELS = 3
 GROUP = 16
+ROWS = 16
+PER = 16
+FIRST = 5
 
 
 def insert(running, x):
@@ -51,7 +54,7 @@
     return lists
 
 
-def probe_kernel(q_ref, c_ref, o_ref, list_ref):
+def probe_kernel(q_ref, c_ref, before_ref, o_ref, list_ref):
     step = pl.program_id(0)
     kept = streams(LEVELS)
     nq = q_ref.shape[0]
@@ -90,39 +93,70 @@
                 for x in held:
                     top = insert(top, x)
             top = fold_sublanes(top)
-            for rank in range(NPROBE):
-                row = rank * (nq // LANES) + tile
-                o_ref[row : row + 1, :] = top[rank][0:1]
-
-
-def probe(queries, centroids, block=4096):
+            at_rows = [rank * (nq // LANES) + tile for rank in range(NPROBE)]
+            top = merge_lists([t[0:1] for t in top], [before_ref[row : row + 1, :] for row in at_rows])
+            for rank, row in enumerate(at_rows):
+                o_ref[row : row + 1, :] = top[rank]
+
+
+def probe(queries, centroids, before, first, steps, block=4096):
     nq, dim = queries.shape
-    total = centroids.shape[0]
+    total = steps * block
     rows = NPROBE * nq // LANES
     return pl.pallas_call(
         probe_kernel,
-        grid=(total // block,),
-        in_specs=[pl.BlockSpec((nq, dim), lambda i: (0, 0)), pl.BlockSpec((block, dim), lambda i: (i, 0))],
+        grid=(steps,),
+        in_specs=[
+            pl.BlockSpec((nq, dim), lambda i: (0, 0)),
+            pl.BlockSpec((block, dim), lambda i: (first + i, 0)),
+            pl.BlockSpec((rows, LANES), lambda i: (0, 0)),
+        ],
         out_specs=pl.BlockSpec((rows, LANES), lambda i: (0, 0)),
         out_shape=jax.ShapeDtypeStruct((rows, LANES), jnp.float32),
         scratch_shapes=[pltpu.VMEM((sum(streams(LEVELS)), 8, nq), jnp.float32)],
-        compiler_params=pltpu.CompilerParams(vmem_limit_bytes=VMEM_LIMIT),
+        compiler_params=pltpu.CompilerParams(vmem_limit_bytes=60 * MIB),
         cost_estimate=pl.CostEstimate(
-            flops=40 * nq * total * dim // 10, bytes_accessed=2 * total * dim, transcendentals=0
+            flops=4 * nq * total * dim, bytes_accessed=2 * total * dim, transcendentals=0
         ),
-        name="probe",
-    )(queries, centroids)
-
-
-def prepare_kernel(count_ref, p_ref, home_ref, cand_ref, x_ref, shard_ref, local_ref):
+        name=f"probe_{first}",
+    )(queries, centroids, before)
+
+
+def prepare_kernel(
+    count_ref, p_ref, home_ref, cand_ref, x_ref, shard_ref, local_ref, place_ref, tiles_ref, next_ref, sorted_ref
+):
+    total, length, _ = p_ref.shape
+    classes = length // ROWS
     rows = lax.broadcasted_iota(jnp.int32, p_ref.shape[1:], 0)
-
-    def one(p, carry):
+    lanes = lax.broadcasted_iota(jnp.int32, place_ref.shape, 1)
+
+    def tiles_of(p):
+        return (count_ref[p] + (ROWS - 1)) // ROWS
+
+    for k in range(classes + 1):
+        next_ref[k] = 0
+
+    def tally(p, carry):
+        k = classes - tiles_of(p) + 1
+        next_ref[k] = next_ref[k] + 1
+        return carry
+
+    lax.fori_loop(0, total, tally, 0)
+    for k in range(1, classes + 1):
+        next_ref[k] = next_ref[k] + next_ref[k - 1]
+
+    def one(p, places):
+        tiles = tiles_of(p)
+        at = next_ref[classes - tiles]
+        next_ref[classes - tiles] = at + 1
+        sorted_ref[at] = tiles
         tokens = p_ref[p].astype(jnp.float32)
-        x_ref[p] = jnp.where(rows < count_ref[p], tokens, tokens[0:1]).astype(x_ref.dtype)
-        return carry
-
-    lax.fori_loop(0, p_ref.shape[0], one, 0, unroll=2)
+        x_ref[at] = jnp.where(rows < count_ref[p], tokens, tokens[0:1]).astype(x_ref.dtype)
+        return jnp.where(lanes == p, at, places)
+
+    place_ref[...] = lax.fori_loop(0, total, one, jnp.zeros(place_ref.shape, jnp.int32))
+    for g in range(total // PER):
+        tiles_ref[g] = sorted_ref[g * PER]
     nq, nk = cand_ref.shape
     cand = jnp.concatenate([cand_ref[...], jnp.zeros((nq, LANES - nk), jnp.int32)], axis=1)
     block, lane = cand // LANES, cand % LANES
@@ -130,41 +164,57 @@
     for b in range(home_ref.shape[0]):
         line = jnp.broadcast_to(home_ref[b : b + 1, :], (nq, LANES))
         store = jnp.where(block == b, jnp.take_along_axis(line, lane, axis=1), store)
-    shard_ref[...] = store // p_ref.shape[0]
-    local_ref[...] = store % p_ref.shape[0]
+    shard_ref[...] = store // total
+    local_ref[...] = store % total
 
 
 def prepare(counts, passages, home, candidates):
     nq = candidates.shape[0]
+    total, length, _ = passages.shape
     index = jax.ShapeDtypeStruct((nq, LANES), jnp.int32)
     vmem = pl.BlockSpec(memory_space=pltpu.VMEM)
+    smem = pl.BlockSpec(memory_space=pltpu.SMEM)
     return pl.pallas_call(
         prepare_kernel,
-        in_specs=[pl.BlockSpec(memory_space=pltpu.SMEM), vmem, vmem, vmem],
-        out_specs=[vmem, vmem, vmem],
-        out_shape=[jax.ShapeDtypeStruct(passages.shape, passages.dtype), index, index],
-        compiler_params=pltpu.CompilerParams(vmem_limit_bytes=VMEM_LIMIT),
+        in_specs=[smem, vmem, vmem, vmem],
+        out_specs=[vmem, vmem, vmem, vmem, smem],
+        out_shape=[
+            jax.ShapeDtypeStruct(passages.shape, passages.dtype),
+            index,
+            index,
+            jax.ShapeDtypeStruct((8, LANES), jnp.int32),
+            jax.ShapeDtypeStruct((total // PER,), jnp.int32),
+        ],
+        scratch_shapes=[pltpu.SMEM((length // ROWS + 1,), jnp.int32), pltpu.SMEM((total,), jnp.int32)],
+        compiler_params=pltpu.CompilerParams(vmem_limit_bytes=60 * MIB),
         cost_estimate=pl.CostEstimate(flops=10**9, bytes_accessed=4 * passages.size, transcendentals=0),
         name="prepare",
     )(counts, passages, home.reshape(-1, LANES), candidates)
 
 
-def maxsim_kernel(g_ref, x_ref, o_ref, best_ref, *, per, width, tokens):
+def maxsim_kernel(tiles_ref, g_ref, x_ref, place_ref, o_ref, best_ref, *, width, tokens):
     count, length, dim = x_ref.shape
     columns = g_ref.shape[0]
+    best_ref[count:, :] = jnp.zeros((best_ref.shape[0] - count, columns), jnp.float32)
 
     def one(g, carry):
-        at = pl.multiple_of(g * per, per)
-        lhs = x_ref[pl.ds(at, per)].reshape(per * length, dim)
-        for col in range(0, columns, width):
-            dots = lax.dot_general(
-                lhs, g_ref[col : col + width, :], (((1,), (1,)), ((), ())), preferred_element_type=jnp.float32
-            )
-            best = jnp.max(dots.reshape(per, length // 8, 8, width), axis=1)
-            best_ref[pl.ds(at, per), col : col + width] = jnp.max(best, axis=1)
+        at = pl.multiple_of(g * PER, PER)
+        for tiles in range(1, length // ROWS + 1):
+            rows = tiles * ROWS
+
+            @pl.when(tiles_ref[g] == tiles)
+            def _(rows=rows):
+                lhs = x_ref[pl.ds(at, PER), :rows, :].reshape(PER * rows, dim)
+                for col in range(0, columns, width):
+                    dots = lax.dot_general(
+                        lhs, g_ref[col : col + width, :], (((1,), (1,)), ((), ())), preferred_element_type=jnp.float32
+                    )
+                    best = jnp.max(dots.reshape(PER, rows // 8, 8, width), axis=1)
+                    best_ref[pl.ds(at, PER), col : col + width] = jnp.max(best, axis=1)
+
         return carry
 
-    lax.fori_loop(0, count // per, one, 0)
+    lax.fori_loop(0, count // PER, one, 0)
     nq = o_ref.shape[0]
     owner = lax.broadcasted_iota(jnp.int32, (nq, columns), 1) // tokens
     pick = (owner == lax.broadcasted_iota(jnp.int32, (nq, columns), 0)).astype(jnp.bfloat16)
@@ -174,23 +224,27 @@
         part = rest.astype(jnp.bfloat16)
         rest = rest - part.astype(jnp.float32)
         total += lax.dot_general(pick, part, (((1,), (1,)), ((), ())), preferred_element_type=jnp.float32)
-    o_ref[...] = total
-
-
-def maxsim(gathered, prepared, tokens):
+    place = jnp.broadcast_to(place_ref[0:1, :], total.shape)
+    o_ref[...] = jnp.take_along_axis(total, place, axis=1)
+
+
+def maxsim(tiles, gathered, prepared, places, tokens):
     columns, dim = gathered.shape
     count, length, _ = prepared.shape
     nq = columns // tokens
+    vmem = pl.BlockSpec(memory_space=pltpu.VMEM)
     return pl.pallas_call(
-        functools.partial(maxsim_kernel, per=16, width=512, tokens=tokens),
+        functools.partial(maxsim_kernel, width=512, tokens=tokens),
+        in_specs=[pl.BlockSpec(memory_space=pltpu.SMEM), vmem, vmem, vmem],
+        out_specs=vmem,
         out_shape=jax.ShapeDtypeStruct((nq, LANES), jnp.float32),
         scratch_shapes=[pltpu.VMEM((LANES, columns), jnp.float32)],
-        compiler_params=pltpu.CompilerParams(vmem_limit_bytes=VMEM_LIMIT),
+        compiler_params=pltpu.CompilerParams(vmem_limit_bytes=24 * MIB),
         cost_estimate=pl.CostEstimate(
             flops=2 * columns * count * length * dim, bytes_accessed=4 * prepared.size, transcendentals=0
         ),
         name="maxsim",
-    )(gathered, prepared)
+    )(tiles, gathered, prepared, places)
 
 
 def finish_kernel(r_ref, shard_ref, local_ref, probe_ref, score_ref, *, shards, cents):
@@ -224,7 +278,7 @@
             jax.ShapeDtypeStruct((nq, NPROBE, nt), jnp.float32),
             jax.ShapeDtypeStruct((nq, nk), jnp.float32),
         ],
-        compiler_params=pltpu.CompilerParams(vmem_limit_bytes=VMEM_LIMIT),
+        compiler_params=pltpu.CompilerParams(vmem_limit_bytes=16 * MIB),
         name="finish",
     )(received, shard_index, local_index)
 
@@ -240,10 +294,15 @@
     mine = nq // cents
     own = lax.dynamic_slice_in_dim(queries, lax.axis_index("cent") * mine, mine, 0).reshape(mine * nt, dim)
     gathered = lax.all_to_all(spread(own, shards), "shard", 0, 0, tiled=True)
-    lists = probe(queries.reshape(nq * nt, dim), centroids)
-    prepared, shard_index, local_index = prepare(counts, passages, home, candidates)
-    table = maxsim(gathered, prepared, nt)
+    tokens = queries.reshape(nq * nt, dim)
+    blocks = centroids.shape[0] // 4096
+    lists = probe(tokens, centroids, jnp.full((NPROBE * nq * nt // LANES, LANES), -jnp.inf, jnp.float32), 0, FIRST)
+    prepared, shard_index, local_index, places, tiles = prepare(counts, passages, home, candidates)
+    gathered, lists = lax.optimization_barrier((gathered, lists))
+    table = maxsim(tiles, gathered, prepared, places, nt)
+    table, lists = lax.optimization_barrier((table, lists))
     returned = lax.all_to_all(table, "shard", 0, 0, tiled=True)
+    lists = probe(tokens, centroids, lists, FIRST, blocks - FIRST)
     final = spread(jnp.concatenate([returned, lists], axis=0), cents)
     received = lax.all_to_all(final, "cent", 0, 0, tiled=True)
     probe_scores, passage_scores = finish(received, shard_index, local_index, shards, cents, nq, nt, nk)

time: 87.4 us -> 80.9 us (0.926)
  waiting for transfers between devices: 9.8 us -> 1.3 us
  Pallas kernels: 40.5 us -> 37.9 us
  starting transfers between devices: 19.5 us -> 21.8 us
  local copies, waits for them, and re-layouts: 2.45 us -> 4.18 us
  blocking collectives: 13.3 us -> 14.3 us
    all_to_all x1, waiting for transfers between devices: 9.8 us -> 0.01 us  [body(): gathered = lax.all_to_all(spread(own, shards), 'shard', 0, 0, tiled=True)]
    all_to_all x1, starting transfers between devices: 7.49 us -> 9.77 us  [body(): returned = lax.all_to_all(table, 'shard', 0, 0, tiled=True)]
    pallas_call x3 -> x4, Pallas kernels: 38.7 us -> 37.1 us  [the longest x2 18.6 us: probe(): pl.pallas_call(probe_kernel, grid=(steps,), in_specs=[pl.BlockSpec((nq, d...]
    all_to_all x1, waiting for transfers between devices: 0.01 us -> 1.3 us  [body(): returned = lax.all_to_all(table, 'shard', 0, 0, tiled=True)]
    unnamed x2 -> x10, local copies, waits for them, and re-layouts: 0.79 us -> 1.9 us
    pallas_call x1, Pallas kernels: 1.79 us -> 0.8 us  [finish(): pl.pallas_call(functools.partial(finish_kernel, shards=shards, cents=cent...]
    all_to_all x1, blocking collectives: 13.3 us -> 14.3 us  [body(): received = lax.all_to_all(final, 'cent', 0, 0, tiled=True)]
  transfers between devices with their start and end apart: 2 -> 2, of which waited for: 1 -> 1; matrix products, arithmetic and copies ran while one was open for 0% -> 1% of each run, Pallas kernels for 24% -> 31%
where the time goes in v2:
time: 80.9 us; the launch traced here: 80.8 us
  Pallas kernels  37.9 us (47%)
  starting transfers between devices  21.8 us (27%)
  blocking collectives  14.3 us (18%)
  local copies, waits for them, and re-layouts  4.18 us (5%)
  waiting for transfers between devices  1.3 us (2%)
    pallas_call x2, Pallas kernels, probe(): pl.pallas_call(probe_kernel, grid=(steps,), in_specs=[pl.BlockSpec((nq, d...  18.6 us
    all_to_all x1, blocking collectives, body(): received = lax.all_to_all(final, 'cent', 0, 0, tiled=True)  14.3 us
    all_to_all x1, starting transfers between devices, body(): gathered = lax.all_to_all(spread(own, shards), 'shard', 0, 0, tiled=True)  12 us
    pallas_call x1, Pallas kernels, maxsim(): pl.pallas_call(functools.partial(maxsim_kernel, width=512, tokens=tokens)...  11.7 us
    all_to_all x1, starting transfers between devices, body(): returned = lax.all_to_all(table, 'shard', 0, 0, tiled=True)  9.77 us
    pallas_call x1, Pallas kernels, prepare(): pl.pallas_call(prepare_kernel, in_specs=[smem, vmem, vmem, vmem], out_spe...  6.81 us
    unnamed x10, local copies, waits for them, and re-layouts  1.9 us
  transfers between devices with their start and end apart: 2, of which 1 were waited for; matrix products, arithmetic and copies ran while one was open for 1% of the time, Pallas kernels for 31%

profile of v2, /device:TPU:1, one launch (start us, length us, event | category | flops | bytes accessed | tf_op | source)
XLA Modules:
  0.0 80.8 jit_solution(4280684163643039622)
XLA Ops:
  0.6 0.7 constant_dynamic-slice_fusion
  1.4 0.9 %broadcast_in_dim.17 = bf16[32,64,128]{2,1,0:T(8,128)(2,1)} broadcast(bf16[64,128]{1,0:T(8,128)(2,1)S(1)} %bitcast.11), dimensions={1,2} | broadcast | bytes 540672 | tf_op jit(solution)/shard_map/broadcast_in_dim | solution.py:287
  2.3 12.0 %all-to-all-start = ((bf16[32,64,128]{2,1,0:T(8,128)(2,1)}), bf16[32,64,128]{2,1,0:T(8,128)(2,1)S(1)}, u32[]{:S(2)}, u32[]{:S(2)}) async-start(bf16[32,64,128]{2,1,0:T(8,128)(2,1)} %broadcast_in_dim.17), calls=%async_computation | async-start | bytes 1048576 | tf_op jit(solution)/shard_map/all_to_all | solution.py:296
  14.3 6.8 %prepare.1 = (bf16[96,128,128]{2,1,0:T(8,128)(2,1)}, s32[16,128]{1,0:T(8,128)}, s32[16,128]{1,0:T(8,128)}, s32[8,128]{1,0:T(8,128)}, s32[6]{0:T(128)}) custom-call(s32[96]{0:T(128)} %count_ref.1, bf16[96,128,128]{2,1,0:T(8,128)(2,1)} %p_ref.1, s32[24,128]{1,0:T(8,128)} %bitcast.15, s32[16,32]{1,0:T(8,128)} %cand_ref.1), custom_call_target="tpu_custom_call" | custom-call | flops 1000000000 | bytes 6291456 | tf_op jit(solution)/shard_map/prepare/pallas_call | solution.py:177
  21.2 0.6 broadcast_in_dim.18.before_ref
  21.8 0.0 copy-start.3
  21.8 0.0 copy-start.4
  21.8 11.1 %probe_0.1.before_ref = f32[16,128]{1,0:T(8,128)} custom-call(bf16[512,128]{1,0:T(8,128)(2,1)} %bitcast.12, bf16[32768,128]{1,0:T(8,128)(2,1)} %c_ref.3, f32[16,128]{1,0:T(8,128)} %broadcast_in_dim.18.before_ref), custom_call_target="tpu_custom_call" | custom-call | flops 5368709120 | bytes 5242880 | tf_op jit(solution)/shard_map/probe_0/pallas_call | solution.py:106
  32.9 0.0 all-to-all-done
  32.9 0.0 copy-done.3
  32.9 0.0 copy-done.4
  32.9 0.0 copy-start.2
  32.9 1.9 %copy-done.2 = bf16[96,128,128]{2,1,0:T(8,128)(2,1)S(1)} copy-done((bf16[96,128,128]{2,1,0:T(8,128)(2,1)S(1)}, bf16[96,128,128]{2,1,0:T(8,128)(2,1)}, u32[]{:S(2)}) %copy-start.2) | copy-done | bytes 3145752
  34.8 11.7 %maxsim.1 = f32[64,128]{1,0:T(8,128)} custom-call(s32[6]{0:T(128)S(1)} %copy-done.4, bf16[2048,128]{1,0:T(8,128)(2,1)S(1)} %bitcast.9, bf16[96,128,128]{2,1,0:T(8,128)(2,1)S(1)} %copy-done.2, s32[8,128]{1,0:T(8,128)S(1)} %copy-done.3), custom_call_target="tpu_custom_call" | custom-call | flops 6442450944 | bytes 6291456 | tf_op jit(solution)/shard_map/maxsim/pallas_call | solution.py:236
  46.5 9.8 %all-to-all-start.1 = ((f32[32,2,128]{2,1,0:T(2,128)}), f32[32,2,128]{2,1,0:T(2,128)S(1)}, u32[]{:S(2)}, u32[]{:S(2)}) async-start(f32[32,2,128]{2,1,0:T(2,128)} %bitcast.4), calls=%async_computation.1 | async-start | bytes 65536 | tf_op jit(solution)/shard_map/all_to_all | solution.py:304
  56.3 0.0 copy-start
  56.3 0.0 copy-start.1
  56.3 7.4 %probe_5.1 = f32[16,128]{1,0:T(8,128)} custom-call(bf16[512,128]{1,0:T(8,128)(2,1)} %bitcast.13, bf16[32768,128]{1,0:T(8,128)(2,1)} %c_ref.3, f32[16,128]{1,0:T(8,128)} %probe_0.1.before_ref), custom_call_target="tpu_custom_call" | custom-call | flops 3221225472 | bytes 3145728 | tf_op jit(solution)/shard_map/probe_5/pallas_call | solution.py:106
  63.7 1.3 %all-to-all-done.1 = f32[32,2,128]{2,1,0:T(2,128)S(1)} async-done(((f32[32,2,128]{2,1,0:T(2,128)}), f32[32,2,128]{2,1,0:T(2,128)S(1)}, u32[]{:S(2)}, u32[]{:S(2)}) %all-to-all-start.1) | async-done | bytes 32800 | tf_op jit(solution)/shard_map/all_to_all | solution.py:304
  65.0 0.7 pad_maximum_fusion
  65.8 14.3 %all_to_all.29 = f32[8,80,128]{2,1,0:T(8,128)S(1)} all-to-all(f32[8,80,128]{2,1,0:T(8,128)S(1)} %broadcast_in_dim.19), channel_id=1, replica_groups=mesh['shard'=32,'cent'=8] {'cent'}, dimensions={0} | all-to-all | bytes 655360 | tf_op jit(solution)/shard_map/all_to_all | solution.py:307
  80.0 0.0 copy-done
  80.0 0.0 copy-done.1
  80.0 0.8 finish.1
  (1 shorter events, 0.0 us)
Async XLA Ops:
  2.3 30.6 %all-to-all-start = ((bf16[32,64,128]{2,1,0:T(8,128)(2,1)}), bf16[32,64,128]{2,1,0:T(8,128)(2,1)S(1)}, u32[]{:S(2)}, u32[]{:S(2)}) async-start(bf16[32,64,128]{2,1,0:T(8,128)(2,1)} %broadcast_in_dim.17), calls=%async_computation | async-start | bytes 1048576 | tf_op jit(solution)/shard_map/all_to_all | solution.py:296
  21.8 11.1 %copy-start.3 = (s32[8,128]{1,0:T(8,128)S(1)}, s32[8,128]{1,0:T(8,128)}, u32[]{:S(2)}) copy-start(s32[8,128]{1,0:T(8,128)} %get-tuple-element.16.place_ref) | copy-start | bytes 12292
  21.8 11.1 %copy-start.4 = (s32[6]{0:T(128)S(1)}, s32[6]{0:T(128)}, u32[]{:S(2)}) copy-start(s32[6]{0:T(128)} %get-tuple-element.13.tiles_ref) | copy-start | bytes 76
  32.9 1.9 %copy-start.2 = (bf16[96,128,128]{2,1,0:T(8,128)(2,1)S(1)}, bf16[96,128,128]{2,1,0:T(8,128)(2,1)}, u32[]{:S(2)}) copy-start(bf16[96,128,128]{2,1,0:T(8,128)(2,1)} %get-tuple-element.15.x_ref) | copy-start | bytes 9437188
  46.5 18.5 %all-to-all-start.1 = ((f32[32,2,128]{2,1,0:T(2,128)}), f32[32,2,128]{2,1,0:T(2,128)S(1)}, u32[]{:S(2)}, u32[]{:S(2)}) async-start(f32[32,2,128]{2,1,0:T(2,128)} %bitcast.4), calls=%async_computation.1 | async-start | bytes 65536 | tf_op jit(solution)/shard_map/all_to_all | solution.py:304
  56.3 23.8 %copy-start = (s32[16,128]{1,0:T(8,128)S(1)}, s32[16,128]{1,0:T(8,128)}, u32[]{:S(2)}) copy-start(s32[16,128]{1,0:T(8,128)} %get-tuple-element.20.shard_ref) | copy-start | bytes 24580
  56.3 23.8 %copy-start.1 = (s32[16,128]{1,0:T(8,128)S(1)}, s32[16,128]{1,0:T(8,128)}, u32[]{:S(2)}) copy-start(s32[16,128]{1,0:T(8,128)} %get-tuple-element.21.local_ref) | copy-start | bytes 24580

commit v3 on v2

--- a/solution.py
+++ b/solution.py
@@ -13,8 +13,9 @@
 LEVELS = 3
 GROUP = 16
 ROWS = 16
+CLASSES = 128 // ROWS
 PER = 16
-FIRST = 5
+FIRST = 6
 
 
 def insert(running, x):
@@ -54,7 +55,9 @@
     return lists
 
 
-def probe_kernel(q_ref, c_ref, before_ref, o_ref, list_ref):
+def probe_kernel(q_ref, c_ref, *refs):
+    before_ref = refs[0] if len(refs) > 2 else None
+    o_ref, list_ref = refs[-2:]
     step = pl.program_id(0)
     kept = streams(LEVELS)
     nq = q_ref.shape[0]
@@ -94,7 +97,9 @@
                     top = insert(top, x)
             top = fold_sublanes(top)
             at_rows = [rank * (nq // LANES) + tile for rank in range(NPROBE)]
-            top = merge_lists([t[0:1] for t in top], [before_ref[row : row + 1, :] for row in at_rows])
+            top = [t[0:1] for t in top]
+            if before_ref is not None:
+                top = merge_lists(top, [before_ref[row : row + 1, :] for row in at_rows])
             for rank, row in enumerate(at_rows):
                 o_ref[row : row + 1, :] = top[rank]
 
@@ -109,57 +114,51 @@
         in_specs=[
             pl.BlockSpec((nq, dim), lambda i: (0, 0)),
             pl.BlockSpec((block, dim), lambda i: (first + i, 0)),
-            pl.BlockSpec((rows, LANES), lambda i: (0, 0)),
-        ],
+        ]
+        + [pl.BlockSpec((rows, LANES), lambda i: (0, 0))] * len(before),
         out_specs=pl.BlockSpec((rows, LANES), lambda i: (0, 0)),
         out_shape=jax.ShapeDtypeStruct((rows, LANES), jnp.float32),
         scratch_shapes=[pltpu.VMEM((sum(streams(LEVELS)), 8, nq), jnp.float32)],
-        compiler_params=pltpu.CompilerParams(vmem_limit_bytes=60 * MIB),
+        compiler_params=pltpu.CompilerParams(vmem_limit_bytes=58 * MIB),
         cost_estimate=pl.CostEstimate(
             flops=4 * nq * total * dim, bytes_accessed=2 * total * dim, transcendentals=0
         ),
         name=f"probe_{first}",
-    )(queries, centroids, before)
-
-
-def prepare_kernel(
-    count_ref, p_ref, home_ref, cand_ref, x_ref, shard_ref, local_ref, place_ref, tiles_ref, next_ref, sorted_ref
-):
-    total, length, _ = p_ref.shape
-    classes = length // ROWS
-    rows = lax.broadcasted_iota(jnp.int32, p_ref.shape[1:], 0)
+    )(queries, centroids, *before)
+
+
+def prepare_kernel(count_ref, home_ref, cand_ref, shard_ref, local_ref, place_ref, order_ref, tiles_ref, next_ref):
+    total = order_ref.shape[0]
     lanes = lax.broadcasted_iota(jnp.int32, place_ref.shape, 1)
 
     def tiles_of(p):
-        return (count_ref[p] + (ROWS - 1)) // ROWS
-
-    for k in range(classes + 1):
+        return lax.shift_right_logical(count_ref[p] + (ROWS - 1), ROWS.bit_length() - 1)
+
+    for k in range(CLASSES + 1):
         next_ref[k] = 0
 
     def tally(p, carry):
-        k = classes - tiles_of(p) + 1
+        k = CLASSES + 1 - tiles_of(p)
         next_ref[k] = next_ref[k] + 1
         return carry
 
-    lax.fori_loop(0, total, tally, 0)
-    for k in range(1, classes + 1):
+    lax.fori_loop(0, total, tally, 0, unroll=8)
+    for k in range(1, CLASSES + 1):
         next_ref[k] = next_ref[k] + next_ref[k - 1]
 
     def one(p, places):
-        tiles = tiles_of(p)
-        at = next_ref[classes - tiles]
-        next_ref[classes - tiles] = at + 1
-        sorted_ref[at] = tiles
-        tokens = p_ref[p].astype(jnp.float32)
-        x_ref[at] = jnp.where(rows < count_ref[p], tokens, tokens[0:1]).astype(x_ref.dtype)
+        k = CLASSES - tiles_of(p)
+        at = next_ref[k]
+        next_ref[k] = at + 1
+        order_ref[at] = p
         return jnp.where(lanes == p, at, places)
 
-    place_ref[...] = lax.fori_loop(0, total, one, jnp.zeros(place_ref.shape, jnp.int32))
+    place_ref[...] = lax.fori_loop(0, total, one, jnp.zeros(place_ref.shape, jnp.int32), unroll=8)
     for g in range(total // PER):
-        tiles_ref[g] = sorted_ref[g * PER]
+        tiles_ref[g] = tiles_of(order_ref[g * PER])
     nq, nk = cand_ref.shape
     cand = jnp.concatenate([cand_ref[...], jnp.zeros((nq, LANES - nk), jnp.int32)], axis=1)
-    block, lane = cand // LANES, cand % LANES
+    block, lane = lax.shift_right_logical(cand, 7), jnp.bitwise_and(cand, LANES - 1)
     store = jnp.zeros((nq, LANES), jnp.int32)
     for b in range(home_ref.shape[0]):
         line = jnp.broadcast_to(home_ref[b : b + 1, :], (nq, LANES))
@@ -168,32 +167,32 @@
     local_ref[...] = store % total
 
 
-def prepare(counts, passages, home, candidates):
+def prepare(counts, home, candidates):
     nq = candidates.shape[0]
-    total, length, _ = passages.shape
+    total = counts.shape[0]
     index = jax.ShapeDtypeStruct((nq, LANES), jnp.int32)
     vmem = pl.BlockSpec(memory_space=pltpu.VMEM)
     smem = pl.BlockSpec(memory_space=pltpu.SMEM)
     return pl.pallas_call(
         prepare_kernel,
-        in_specs=[smem, vmem, vmem, vmem],
-        out_specs=[vmem, vmem, vmem, vmem, smem],
+        in_specs=[smem, vmem, vmem],
+        out_specs=[vmem, vmem, vmem, smem, smem],
         out_shape=[
-            jax.ShapeDtypeStruct(passages.shape, passages.dtype),
             index,
             index,
             jax.ShapeDtypeStruct((8, LANES), jnp.int32),
+            jax.ShapeDtypeStruct((total,), jnp.int32),
             jax.ShapeDtypeStruct((total // PER,), jnp.int32),
         ],
-        scratch_shapes=[pltpu.SMEM((length // ROWS + 1,), jnp.int32), pltpu.SMEM((total,), jnp.int32)],
-        compiler_params=pltpu.CompilerParams(vmem_limit_bytes=60 * MIB),
-        cost_estimate=pl.CostEstimate(flops=10**9, bytes_accessed=4 * passages.size, transcendentals=0),
+        scratch_shapes=[pltpu.SMEM((CLASSES + 1,), jnp.int32)],
+        compiler_params=pltpu.CompilerParams(vmem_limit_bytes=58 * MIB),
+        cost_estimate=pl.CostEstimate(flops=10**9, bytes_accessed=10**5, transcendentals=0),
         name="prepare",
-    )(counts, passages, home.reshape(-1, LANES), candidates)
-
-
-def maxsim_kernel(tiles_ref, g_ref, x_ref, place_ref, o_ref, best_ref, *, width, tokens):
-    count, length, dim = x_ref.shape
+    )(counts, home.reshape(-1, LANES), candidates)
+
+
+def maxsim_kernel(count_ref, order_ref, tiles_ref, g_ref, p_ref, place_ref, o_ref, best_ref, lhs_ref, *, width, tokens):
+    count, length, dim = p_ref.shape
     columns = g_ref.shape[0]
     best_ref[count:, :] = jnp.zeros((best_ref.shape[0] - count, columns), jnp.float32)
 
@@ -204,7 +203,13 @@
 
             @pl.when(tiles_ref[g] == tiles)
             def _(rows=rows):
-                lhs = x_ref[pl.ds(at, PER), :rows, :].reshape(PER * rows, dim)
+                index = lax.broadcasted_iota(jnp.int32, (rows, dim), 0)
+                for i in range(PER):
+                    p = order_ref[at + i]
+                    block = p_ref[p, :rows, :].astype(jnp.float32)
+                    block = jnp.where(index < count_ref[p], block, block[0:1])
+                    lhs_ref[i * rows : (i + 1) * rows, :] = block.astype(lhs_ref.dtype)
+                lhs = lhs_ref[: PER * rows, :]
                 for col in range(0, columns, width):
                     dots = lax.dot_general(
                         lhs, g_ref[col : col + width, :], (((1,), (1,)), ((), ())), preferred_element_type=jnp.float32
@@ -228,23 +233,24 @@
     o_ref[...] = jnp.take_along_axis(total, place, axis=1)
 
 
-def maxsim(tiles, gathered, prepared, places, tokens):
+def maxsim(counts, order, tiles, gathered, passages, places, tokens, width=512):
     columns, dim = gathered.shape
-    count, length, _ = prepared.shape
+    count, length, _ = passages.shape
     nq = columns // tokens
     vmem = pl.BlockSpec(memory_space=pltpu.VMEM)
-    return pl.pallas_call(
-        functools.partial(maxsim_kernel, width=512, tokens=tokens),
-        in_specs=[pl.BlockSpec(memory_space=pltpu.SMEM), vmem, vmem, vmem],
+    smem = pl.BlockSpec(memory_space=pltpu.SMEM)
+    return pl.pallas_call(
+        functools.partial(maxsim_kernel, width=width, tokens=tokens),
+        in_specs=[smem, smem, smem, vmem, vmem, vmem],
         out_specs=vmem,
         out_shape=jax.ShapeDtypeStruct((nq, LANES), jnp.float32),
-        scratch_shapes=[pltpu.VMEM((LANES, columns), jnp.float32)],
-        compiler_params=pltpu.CompilerParams(vmem_limit_bytes=24 * MIB),
+        scratch_shapes=[pltpu.VMEM((LANES, columns), jnp.float32), pltpu.VMEM((PER * length, dim), jnp.bfloat16)],
+        compiler_params=pltpu.CompilerParams(vmem_limit_bytes=40 * MIB),
         cost_estimate=pl.CostEstimate(
-            flops=2 * columns * count * length * dim, bytes_accessed=4 * prepared.size, transcendentals=0
+            flops=2 * columns * count * length * dim, bytes_accessed=2 * passages.size, transcendentals=0
         ),
         name="maxsim",
-    )(tiles, gathered, prepared, places)
+    )(counts, order, tiles, gathered, passages, places)
 
 
 def finish_kernel(r_ref, shard_ref, local_ref, probe_ref, score_ref, *, shards, cents):
@@ -283,8 +289,36 @@
     )(received, shard_index, local_index)
 
 
-def spread(block, copies):
-    return jnp.broadcast_to(block[None], (copies,) + block.shape).reshape((-1,) + block.shape[1:])
+def copies_kernel(at_ref, x_ref, o_ref):
+    rows = o_ref.shape[1]
+    block = x_ref[pl.ds(pl.multiple_of(at_ref[0] * rows, rows), rows), :]
+    for k in range(o_ref.shape[0]):
+        o_ref[k] = block
+
+
+def copies_of_part(x, at, rows, copies):
+    vmem = pl.BlockSpec(memory_space=pltpu.VMEM)
+    return pl.pallas_call(
+        copies_kernel,
+        in_specs=[pl.BlockSpec(memory_space=pltpu.SMEM), vmem],
+        out_specs=vmem,
+        out_shape=jax.ShapeDtypeStruct((copies, rows, x.shape[1]), x.dtype),
+        name="copies",
+    )(jnp.full((1,), at, jnp.int32), x)
+
+
+def joined_kernel(a_ref, b_ref, o_ref):
+    for k in range(o_ref.shape[0]):
+        o_ref[k, : a_ref.shape[0]] = a_ref[...]
+        o_ref[k, a_ref.shape[0] :] = b_ref[...]
+
+
+def copies_of_both(a, b, copies):
+    return pl.pallas_call(
+        joined_kernel,
+        out_shape=jax.ShapeDtypeStruct((copies, a.shape[0] + b.shape[0], a.shape[1]), a.dtype),
+        name="joined",
+    )(a, b)
 
 
 def body(queries, centroids, passages, counts, home, candidates):
@@ -292,19 +326,19 @@
     nk = candidates.shape[1]
     shards, cents = lax.axis_size("shard"), lax.axis_size("cent")
     mine = nq // cents
-    own = lax.dynamic_slice_in_dim(queries, lax.axis_index("cent") * mine, mine, 0).reshape(mine * nt, dim)
-    gathered = lax.all_to_all(spread(own, shards), "shard", 0, 0, tiled=True)
     tokens = queries.reshape(nq * nt, dim)
+    own = copies_of_part(tokens, lax.axis_index("cent"), mine * nt, shards)
+    gathered = lax.all_to_all(own.reshape(-1, dim), "shard", 0, 0, tiled=True)
     blocks = centroids.shape[0] // 4096
-    lists = probe(tokens, centroids, jnp.full((NPROBE * nq * nt // LANES, LANES), -jnp.inf, jnp.float32), 0, FIRST)
-    prepared, shard_index, local_index, places, tiles = prepare(counts, passages, home, candidates)
+    lists = probe(tokens, centroids, (), 0, FIRST)
+    shard_index, local_index, places, order, tiles = prepare(counts, home, candidates)
     gathered, lists = lax.optimization_barrier((gathered, lists))
-    table = maxsim(tiles, gathered, prepared, places, nt)
+    table = maxsim(counts, order, tiles, gathered, passages, places, nt)
     table, lists = lax.optimization_barrier((table, lists))
     returned = lax.all_to_all(table, "shard", 0, 0, tiled=True)
-    lists = probe(tokens, centroids, lists, FIRST, blocks - FIRST)
-    final = spread(jnp.concatenate([returned, lists], axis=0), cents)
-    received = lax.all_to_all(final, "cent", 0, 0, tiled=True)
+    lists = probe(tokens, centroids, (lists,), FIRST, blocks - FIRST)
+    final = copies_of_both(returned, lists, cents)
+    received = lax.all_to_all(final.reshape(-1, LANES), "cent", 0, 0, tiled=True)
     probe_scores, passage_scores = finish(received, shard_index, local_index, shards, cents, nq, nt, nk)
     return jnp.transpose(probe_scores, (0, 2, 1)), passage_scores
 

time: 80.9 us -> 80.1 us (level); the launches traced: 80.8 us -> 79.2 us
  waiting for transfers between devices: 1.3 us -> 3.18 us
  local copies, waits for them, and re-layouts: 4.18 us -> 2.53 us
  Pallas kernels: 37.9 us -> 36.9 us
    all_to_all x1, waiting for transfers between devices: 1.3 us -> 3.18 us  [body(): returned = lax.all_to_all(table, 'shard', 0, 0, tiled=True)]
    broadcast_in_dim x3 -> x0, local copies, waits for them, and re-layouts: 1.55 us -> none  [the longest x2 0.95 us: spread(): jnp.broadcast_to(block[None], (copies,) + block.shape)]
    pallas_call x2 -> x4, Pallas kernels: 18.5 us -> 17.5 us  [the longest x1 11.8 us: maxsim(): pl.pallas_call(functools.partial(maxsim_kernel, width=width, tokens=token...]
    unnamed x10 -> x16, local copies, waits for them, and re-layouts: 1.9 us -> 2.53 us
  transfers between devices with their start and end apart: 2 -> 2, of which waited for: 1 -> 1; matrix products, arithmetic and copies ran while one was open for 1% -> 0% of each run, Pallas kernels for 31% -> 27%
where the time goes in v3:
time: 80.1 us; the launch traced here: 79.2 us
  Pallas kernels  36.9 us (46%)
  starting transfers between devices  21.4 us (27%)
  blocking collectives  14.5 us (18%)
  waiting for transfers between devices  3.18 us (4%)
  local copies, waits for them, and re-layouts  2.53 us (3%)
    pallas_call x2, Pallas kernels, probe(): pl.pallas_call(probe_kernel, grid=(steps,), in_specs=[pl.BlockSpec((nq, d...  18.6 us
    all_to_all x1, blocking collectives, body(): lax.all_to_all(final.reshape(-1, LANES), 'cent', 0, 0, tiled=True)  14.5 us
    all_to_all x1, starting transfers between devices, body(): gathered = lax.all_to_all(own.reshape(-1, dim), 'shard', 0, 0, tiled=True)  12 us
    pallas_call x1, Pallas kernels, maxsim(): pl.pallas_call(functools.partial(maxsim_kernel, width=width, tokens=token...  11.8 us
    all_to_all x1, starting transfers between devices, body(): returned = lax.all_to_all(table, 'shard', 0, 0, tiled=True)  9.39 us
    all_to_all x1, waiting for transfers between devices, body(): returned = lax.all_to_all(table, 'shard', 0, 0, tiled=True)  3.18 us
    unnamed x16, local copies, waits for them, and re-layouts  2.53 us
    pallas_call x1, Pallas kernels, prepare(): pl.pallas_call(prepare_kernel, in_specs=[smem, vmem, vmem], out_specs=[vm...  2.43 us
  transfers between devices with their start and end apart: 2, of which 1 were waited for; matrix products, arithmetic and copies ran while one was open for 0% of the time, Pallas kernels for 27%

profile of v3, /device:TPU:1, one launch (start us, length us, event | category | flops | bytes accessed | tf_op | source)
XLA Modules:
  0.0 79.2 jit_solution(14889923815431375084)
XLA Ops:
  0.6 1.8 %copies.1 = bf16[32,64,128]{2,1,0:T(8,128)(2,1)} custom-call(s32[1]{0:T(128)} %bitcast.1.at_ref, bf16[512,128]{1,0:T(8,128)(2,1)} %bitcast.10), custom_call_target="tpu_custom_call" | custom-call | tf_op jit(solution)/shard_map/copies/pallas_call | solution.py:301
  2.5 12.0 %all-to-all-start = ((bf16[32,64,128]{2,1,0:T(8,128)(2,1)}), bf16[32,64,128]{2,1,0:T(8,128)(2,1)S(1)}, u32[]{:S(2)}, u32[]{:S(2)}) async-start(bf16[32,64,128]{2,1,0:T(8,128)(2,1)} %copies.1), calls=%async_computation | async-start | bytes 1048576 | tf_op jit(solution)/shard_map/all_to_all | solution.py:331
  14.5 2.4 %prepare.1 = (s32[16,128]{1,0:T(8,128)}, s32[16,128]{1,0:T(8,128)}, s32[8,128]{1,0:T(8,128)}, s32[96]{0:T(128)}, s32[6]{0:T(128)}) custom-call(s32[96]{0:T(128)} %count_ref.3, s32[24,128]{1,0:T(8,128)} %bitcast.15, s32[16,32]{1,0:T(8,128)} %cand_ref.1), custom_call_target="tpu_custom_call" | custom-call | flops 1000000000 | bytes 100000 | tf_op jit(solution)/shard_map/prepare/pallas_call | solution.py:176
  16.9 0.0 copy-start.3
  16.9 0.0 copy-start.4
  17.0 0.0 copy-start.5
  17.0 0.0 copy-start.6
  17.0 13.0 %probe_0.1.refs_0_ = f32[16,128]{1,0:T(8,128)} custom-call(bf16[512,128]{1,0:T(8,128)(2,1)} %bitcast.11, bf16[32768,128]{1,0:T(8,128)(2,1)} %c_ref.3), custom_call_target="tpu_custom_call" | custom-call | flops 6442450944 | bytes 6291456 | tf_op jit(solution)/shard_map/probe_0/pallas_call | solution.py:111
  30.0 0.0 all-to-all-done
  30.0 0.0 copy-done.3
  30.0 0.0 copy-done.4
  30.0 0.0 copy-done.5
  30.0 0.0 copy-done.6
  30.0 0.0 copy-start.2
  30.0 1.9 %copy-done.2 = bf16[96,128,128]{2,1,0:T(8,128)(2,1)S(1)} copy-done((bf16[96,128,128]{2,1,0:T(8,128)(2,1)S(1)}, bf16[96,128,128]{2,1,0:T(8,128)(2,1)}, u32[]{:S(2)}) %copy-start.2) | copy-done | bytes 3145752
  31.9 11.8 %maxsim.1 = f32[64,128]{1,0:T(8,128)} custom-call(s32[96]{0:T(128)S(1)} %copy-done.3, s32[96]{0:T(128)S(1)} %copy-done.5, s32[6]{0:T(128)S(1)} %copy-done.6, bf16[2048,128]{1,0:T(8,128)(2,1)S(1)} %bitcast.9, bf16[96,128,128]{2,1,0:T(8,128)(2,1)S(1)} %copy-done.2, s32[8,128]{1,0:T(8,128)S(1)} %copy-done.4), custom_call_target="tpu_custom_call" | custom-call | flops 6442450944 | bytes 3145728 | tf_op jit(solution)/shard_map/maxsim/pallas_call | solution.py:242
  43.7 0.0 copy-start
  43.7 0.0 copy-start.1
  43.7 9.4 %all-to-all-start.1 = ((f32[32,2,128]{2,1,0:T(2,128)}), f32[32,2,128]{2,1,0:T(2,128)S(1)}, u32[]{:S(2)}, u32[]{:S(2)}) async-start(f32[32,2,128]{2,1,0:T(2,128)} %bitcast.4), calls=%async_computation.1 | async-start | bytes 65536 | tf_op jit(solution)/shard_map/all_to_all | solution.py:338
  53.1 5.6 %probe_6.1.b_ref = f32[16,128]{1,0:T(8,128)} custom-call(bf16[512,128]{1,0:T(8,128)(2,1)} %bitcast.12, bf16[32768,128]{1,0:T(8,128)(2,1)} %c_ref.3, f32[16,128]{1,0:T(8,128)} %probe_0.1.refs_0_), custom_call_target="tpu_custom_call" | custom-call | flops 2147483648 | bytes 2097152 | tf_op jit(solution)/shard_map/probe_6/pallas_call | solution.py:111
  58.7 3.2 %all-to-all-done.1 = f32[32,2,128]{2,1,0:T(2,128)S(1)} async-done(((f32[32,2,128]{2,1,0:T(2,128)}), f32[32,2,128]{2,1,0:T(2,128)S(1)}, u32[]{:S(2)}, u32[]{:S(2)}) %all-to-all-start.1) | async-done | bytes 32800 | tf_op jit(solution)/shard_map/all_to_all | solution.py:338
  61.8 0.0 copy-start.7
  61.8 0.6 copy-done.7
  62.4 1.5 %joined.1 = f32[8,80,128]{2,1,0:T(8,128)} custom-call(f32[64,128]{1,0:T(8,128)} %bitcast.13, f32[16,128]{1,0:T(8,128)} %probe_6.1.b_ref), custom_call_target="tpu_custom_call" | custom-call | tf_op jit(solution)/shard_map/joined/pallas_call | solution.py:317
  63.9 14.5 %all_to_all.28 = f32[8,80,128]{2,1,0:T(8,128)S(1)} all-to-all(f32[8,80,128]{2,1,0:T(8,128)} %joined.1), channel_id=1, replica_groups=mesh['shard'=32,'cent'=8] {'cent'}, dimensions={0} | all-to-all | bytes 655360 | tf_op jit(solution)/shard_map/all_to_all | solution.py:341
  78.4 0.0 copy-done
  78.4 0.0 copy-done.1
  78.4 0.8 %finish.1 = (f32[16,4,32]{2,1,0:T(4,128)}, f32[16,32]{1,0:T(8,128)}) custom-call(f32[640,128]{1,0:T(8,128)S(1)} %bitcast.8, s32[16,128]{1,0:T(8,128)S(1)} %copy-done, s32[16,128]{1,0:T(8,128)S(1)} %copy-done.1), custom_call_target="tpu_custom_call" | custom-call | tf_op jit(solution)/shard_map/finish/pallas_call | solution.py:281
Async XLA Ops:
  2.5 27.5 %all-to-all-start = ((bf16[32,64,128]{2,1,0:T(8,128)(2,1)}), bf16[32,64,128]{2,1,0:T(8,128)(2,1)S(1)}, u32[]{:S(2)}, u32[]{:S(2)}) async-start(bf16[32,64,128]{2,1,0:T(8,128)(2,1)} %copies.1), calls=%async_computation | async-start | bytes 1048576 | tf_op jit(solution)/shard_map/all_to_all | solution.py:331
  16.9 13.0 %copy-start.3 = (s32[96]{0:T(128)S(1)}, s32[96]{0:T(128)}, u32[]{:S(2)}) copy-start(s32[96]{0:T(128)} %count_ref.3) | copy-start | bytes 1156
  16.9 13.0 %copy-start.4 = (s32[8,128]{1,0:T(8,128)S(1)}, s32[8,128]{1,0:T(8,128)}, u32[]{:S(2)}) copy-start(s32[8,128]{1,0:T(8,128)} %get-tuple-element.16.place_ref) | copy-start | bytes 12292
  17.0 13.0 %copy-start.5 = (s32[96]{0:T(128)S(1)}, s32[96]{0:T(128)}, u32[]{:S(2)}) copy-start(s32[96]{0:T(128)} %get-tuple-element.13.order_ref) | copy-start | bytes 1156
  17.0 13.0 %copy-start.6 = (s32[6]{0:T(128)S(1)}, s32[6]{0:T(128)}, u32[]{:S(2)}) copy-start(s32[6]{0:T(128)} %get-tuple-element.14.tiles_ref) | copy-start | bytes 76
  30.0 1.9 %copy-start.2 = (bf16[96,128,128]{2,1,0:T(8,128)(2,1)S(1)}, bf16[96,128,128]{2,1,0:T(8,128)(2,1)}, u32[]{:S(2)}) copy-start(bf16[96,128,128]{2,1,0:T(8,128)(2,1)} %p_ref.1) | copy-start | bytes 9437188
  43.7 34.7 %copy-start = (s32[16,128]{1,0:T(8,128)S(1)}, s32[16,128]{1,0:T(8,128)}, u32[]{:S(2)}) copy-start(s32[16,128]{1,0:T(8,128)} %get-tuple-element.20.shard_ref) | copy-start | bytes 24580
  43.7 34.7 %copy-start.1 = (s32[16,128]{1,0:T(8,128)S(1)}, s32[16,128]{1,0:T(8,128)}, u32[]{:S(2)}) copy-start(s32[16,128]{1,0:T(8,128)} %get-tuple-element.21.local_ref) | copy-start | bytes 24580
  43.7 18.2 %all-to-all-start.1 = ((f32[32,2,128]{2,1,0:T(2,128)}), f32[32,2,128]{2,1,0:T(2,128)S(1)}, u32[]{:S(2)}, u32[]{:S(2)}) async-start(f32[32,2,128]{2,1,0:T(2,128)} %bitcast.4), calls=%async_computation.1 | async-start | bytes 65536 | tf_op jit(solution)/shard_map/all_to_all | solution.py:338
  61.8 0.6 copy-start.7

commit v4 on v3

--- a/solution.py
+++ b/solution.py
@@ -15,7 +15,7 @@
 ROWS = 16
 CLASSES = 128 // ROWS
 PER = 16
-FIRST = 6
+FIRST = 7
 
 
 def insert(running, x):
@@ -119,7 +119,7 @@
         out_specs=pl.BlockSpec((rows, LANES), lambda i: (0, 0)),
         out_shape=jax.ShapeDtypeStruct((rows, LANES), jnp.float32),
         scratch_shapes=[pltpu.VMEM((sum(streams(LEVELS)), 8, nq), jnp.float32)],
-        compiler_params=pltpu.CompilerParams(vmem_limit_bytes=58 * MIB),
+        compiler_params=pltpu.CompilerParams(vmem_limit_bytes=24 * MIB),
         cost_estimate=pl.CostEstimate(
             flops=4 * nq * total * dim, bytes_accessed=2 * total * dim, transcendentals=0
         ),
@@ -289,36 +289,8 @@
     )(received, shard_index, local_index)
 
 
-def copies_kernel(at_ref, x_ref, o_ref):
-    rows = o_ref.shape[1]
-    block = x_ref[pl.ds(pl.multiple_of(at_ref[0] * rows, rows), rows), :]
-    for k in range(o_ref.shape[0]):
-        o_ref[k] = block
-
-
-def copies_of_part(x, at, rows, copies):
-    vmem = pl.BlockSpec(memory_space=pltpu.VMEM)
-    return pl.pallas_call(
-        copies_kernel,
-        in_specs=[pl.BlockSpec(memory_space=pltpu.SMEM), vmem],
-        out_specs=vmem,
-        out_shape=jax.ShapeDtypeStruct((copies, rows, x.shape[1]), x.dtype),
-        name="copies",
-    )(jnp.full((1,), at, jnp.int32), x)
-
-
-def joined_kernel(a_ref, b_ref, o_ref):
-    for k in range(o_ref.shape[0]):
-        o_ref[k, : a_ref.shape[0]] = a_ref[...]
-        o_ref[k, a_ref.shape[0] :] = b_ref[...]
-
-
-def copies_of_both(a, b, copies):
-    return pl.pallas_call(
-        joined_kernel,
-        out_shape=jax.ShapeDtypeStruct((copies, a.shape[0] + b.shape[0], a.shape[1]), a.dtype),
-        name="joined",
-    )(a, b)
+def spread(block, copies):
+    return jnp.broadcast_to(block[None], (copies,) + block.shape).reshape((-1,) + block.shape[1:])
 
 
 def body(queries, centroids, passages, counts, home, candidates):
@@ -327,9 +299,10 @@
     shards, cents = lax.axis_size("shard"), lax.axis_size("cent")
     mine = nq // cents
     tokens = queries.reshape(nq * nt, dim)
-    own = copies_of_part(tokens, lax.axis_index("cent"), mine * nt, shards)
-    gathered = lax.all_to_all(own.reshape(-1, dim), "shard", 0, 0, tiled=True)
+    own = lax.dynamic_slice_in_dim(tokens, lax.axis_index("cent") * mine * nt, mine * nt, 0)
+    gathered = lax.all_to_all(spread(own, shards), "shard", 0, 0, tiled=True)
     blocks = centroids.shape[0] // 4096
+    centroids = pltpu.with_memory_space_constraint(centroids, pltpu.HBM)
     lists = probe(tokens, centroids, (), 0, FIRST)
     shard_index, local_index, places, order, tiles = prepare(counts, home, candidates)
     gathered, lists = lax.optimization_barrier((gathered, lists))
@@ -337,8 +310,8 @@
     table, lists = lax.optimization_barrier((table, lists))
     returned = lax.all_to_all(table, "shard", 0, 0, tiled=True)
     lists = probe(tokens, centroids, (lists,), FIRST, blocks - FIRST)
-    final = copies_of_both(returned, lists, cents)
-    received = lax.all_to_all(final.reshape(-1, LANES), "cent", 0, 0, tiled=True)
+    final = spread(jnp.concatenate([returned, lists], axis=0), cents)
+    received = lax.all_to_all(final, "cent", 0, 0, tiled=True)
     probe_scores, passage_scores = finish(received, shard_index, local_index, shards, cents, nq, nt, nk)
     return jnp.transpose(probe_scores, (0, 2, 1)), passage_scores
 

time: 80.1 us -> 79.6 us (level)
  Pallas kernels: 36.9 us -> 31.8 us
  waiting for transfers between devices: 3.18 us -> 5.64 us
  local copies, waits for them, and re-layouts: 2.53 us -> 4.47 us
    pallas_call x2 -> x0, Pallas kernels: 3.32 us -> none  [the longest x1 1.82 us: copies_of_part(): pl.pallas_call(copies_kernel, in_specs=[pl.BlockSpec(memory_space=pltpu.S...]
    all_to_all x1, waiting for transfers between devices: 3.18 us -> 5.63 us  [body(): returned = lax.all_to_all(table, 'shard', 0, 0, tiled=True)]
    pallas_call x2, Pallas kernels: 18.6 us -> 17.3 us  [probe(): pl.pallas_call(probe_kernel, grid=(steps,), in_specs=[pl.BlockSpec((nq, d...]
    broadcast_in_dim x0 -> x2, local copies, waits for them, and re-layouts: none -> 0.94 us  [spread(): jnp.broadcast_to(block[None], (copies,) + block.shape)]
    unnamed x16 -> x18, local copies, waits for them, and re-layouts: 2.53 us -> 2.81 us
  transfers between devices with their start and end apart: 2 -> 2, of which waited for: 1 -> 1; matrix products, arithmetic and copies ran while one was open for 0% -> 0% of each run, Pallas kernels for 27% -> 25%
where the time goes in v4:
time: 79.6 us; the launch traced here: 78.8 us
  Pallas kernels  31.8 us (40%)
  starting transfers between devices  22 us (28%)
  blocking collectives  14.3 us (18%)
  waiting for transfers between devices  5.64 us (7%)
  local copies, waits for them, and re-layouts  4.47 us (6%)
    pallas_call x2, Pallas kernels, probe(): pl.pallas_call(probe_kernel, grid=(steps,), in_specs=[pl.BlockSpec((nq, d...  17.3 us
    all_to_all x1, blocking collectives, body(): received = lax.all_to_all(final, 'cent', 0, 0, tiled=True)  14.3 us
    all_to_all x1, starting transfers between devices, body(): gathered = lax.all_to_all(spread(own, shards), 'shard', 0, 0, tiled=True)  12 us
    pallas_call x1, Pallas kernels, maxsim(): pl.pallas_call(functools.partial(maxsim_kernel, width=width, tokens=token...  11.2 us
    all_to_all x1, starting transfers between devices, body(): returned = lax.all_to_all(table, 'shard', 0, 0, tiled=True)  9.92 us
    all_to_all x1, waiting for transfers between devices, body(): returned = lax.all_to_all(table, 'shard', 0, 0, tiled=True)  5.63 us
    unnamed x18, local copies, waits for them, and re-layouts  2.81 us
    pallas_call x1, Pallas kernels, prepare(): pl.pallas_call(prepare_kernel, in_specs=[smem, vmem, vmem], out_specs=[vm...  2.44 us
  transfers between devices with their start and end apart: 2, of which 1 were waited for; matrix products, arithmetic and copies ran while one was open for 0% of the time, Pallas kernels for 25%

profile of v4, /device:TPU:1, one launch (start us, length us, event | category | flops | bytes accessed | tf_op | source)
XLA Modules:
  0.0 78.8 jit_solution(15134149979572552748)
XLA Ops:
  0.6 0.7 constant_dynamic-slice_fusion
  1.4 0.9 %broadcast_in_dim.4 = bf16[32,64,128]{2,1,0:T(8,128)(2,1)} broadcast(bf16[64,128]{1,0:T(8,128)(2,1)S(1)} %constant_dynamic-slice_fusion), dimensions={1,2} | broadcast | bytes 540672 | tf_op jit(solution)/shard_map/broadcast_in_dim | solution.py:293
  2.3 12.0 %all-to-all-start = ((bf16[32,64,128]{2,1,0:T(8,128)(2,1)}), bf16[32,64,128]{2,1,0:T(8,128)(2,1)S(1)}, u32[]{:S(2)}, u32[]{:S(2)}) async-start(bf16[32,64,128]{2,1,0:T(8,128)(2,1)} %broadcast_in_dim.4), calls=%async_computation | async-start | bytes 1048576 | tf_op jit(solution)/shard_map/all_to_all | solution.py:303
  14.3 2.4 %prepare.1 = (s32[16,128]{1,0:T(8,128)}, s32[16,128]{1,0:T(8,128)}, s32[8,128]{1,0:T(8,128)}, s32[96]{0:T(128)}, s32[6]{0:T(128)}) custom-call(s32[96]{0:T(128)} %count_ref.3, s32[24,128]{1,0:T(8,128)} %bitcast.14, s32[16,32]{1,0:T(8,128)} %cand_ref.1), custom_call_target="tpu_custom_call" | custom-call | flops 1000000000 | bytes 100000 | tf_op jit(solution)/shard_map/prepare/pallas_call | solution.py:176
  16.8 0.0 copy-start
  16.8 0.9 %copy-done = bf16[16,32,128]{2,1,0:T(8,128)(2,1)S(1)} copy-done((bf16[16,32,128]{2,1,0:T(8,128)(2,1)S(1)}, bf16[16,32,128]{2,1,0:T(8,128)(2,1)}, u32[]{:S(2)}) %copy-start) | copy-done | bytes 131096
  17.7 0.0 copy-start.5
  17.7 0.0 copy-start.6
  17.7 0.0 copy-start.7
  17.7 0.0 copy-start.8
  17.7 14.2 %probe_0.1.refs_0_ = f32[16,128]{1,0:T(8,128)S(1)} custom-call(bf16[512,128]{1,0:T(8,128)(2,1)S(1)} %bitcast.10, bf16[32768,128]{1,0:T(8,128)(2,1)} %c_ref.3), custom_call_target="tpu_custom_call" | custom-call | flops 7516192768 | bytes 7340032 | tf_op jit(solution)/shard_map/probe_0/pallas_call | solution.py:111
  31.9 0.0 all-to-all-done
  31.9 0.0 copy-done.5
  31.9 0.0 copy-done.6
  31.9 0.0 copy-done.7
  31.9 0.0 copy-done.8
  31.9 0.0 copy-start.4
  31.9 1.9 %copy-done.4 = bf16[96,128,128]{2,1,0:T(8,128)(2,1)S(1)} copy-done((bf16[96,128,128]{2,1,0:T(8,128)(2,1)S(1)}, bf16[96,128,128]{2,1,0:T(8,128)(2,1)}, u32[]{:S(2)}) %copy-start.4) | copy-done | bytes 3145752
  33.8 0.0 copy-start.1
  33.8 11.2 %maxsim.1 = f32[64,128]{1,0:T(8,128)} custom-call(s32[96]{0:T(128)S(1)} %copy-done.5, s32[96]{0:T(128)S(1)} %copy-done.7, s32[6]{0:T(128)S(1)} %copy-done.8, bf16[2048,128]{1,0:T(8,128)(2,1)S(1)} %bitcast.8, bf16[96,128,128]{2,1,0:T(8,128)(2,1)S(1)} %copy-done.4, s32[8,128]{1,0:T(8,128)S(1)} %copy-done.6), custom_call_target="tpu_custom_call" | custom-call | flops 6442450944 | bytes 3145728 | tf_op jit(solution)/shard_map/maxsim/pallas_call | solution.py:242
  45.0 0.0 copy-start.2
  45.0 0.0 copy-start.3
  45.0 9.9 %all-to-all-start.1 = ((f32[32,2,128]{2,1,0:T(2,128)}), f32[32,2,128]{2,1,0:T(2,128)S(1)}, u32[]{:S(2)}, u32[]{:S(2)}) async-start(f32[32,2,128]{2,1,0:T(2,128)} %bitcast.3), calls=%async_computation.1 | async-start | bytes 65536 | tf_op jit(solution)/shard_map/all_to_all | solution.py:311
  55.0 0.0 copy-done.1
  55.0 3.1 %probe_7.1 = f32[16,128]{1,0:T(8,128)S(1)} custom-call(bf16[512,128]{1,0:T(8,128)(2,1)S(1)} %bitcast.11, bf16[32768,128]{1,0:T(8,128)(2,1)} %c_ref.3, f32[16,128]{1,0:T(8,128)S(1)} %probe_0.1.refs_0_), custom_call_target="tpu_custom_call" | custom-call | flops 1073741824 | bytes 1048576 | tf_op jit(solution)/shard_map/probe_7/pallas_call | solution.py:111
  58.1 5.6 %all-to-all-done.1 = f32[32,2,128]{2,1,0:T(2,128)S(1)} async-done(((f32[32,2,128]{2,1,0:T(2,128)}), f32[32,2,128]{2,1,0:T(2,128)S(1)}, u32[]{:S(2)}, u32[]{:S(2)}) %all-to-all-start.1) | async-done | bytes 32800 | tf_op jit(solution)/shard_map/all_to_all | solution.py:311
  63.8 14.3 %all_to_all.29 = f32[8,80,128]{2,1,0:T(8,128)S(1)} all-to-all(f32[8,80,128]{2,1,0:T(8,128)S(1)} %broadcast_in_dim.5), channel_id=1, replica_groups=mesh['shard'=32,'cent'=8] {'cent'}, dimensions={0} | all-to-all | bytes 655360 | tf_op jit(solution)/shard_map/all_to_all | solution.py:314
  78.0 0.0 copy-done.2
  78.0 0.0 copy-done.3
  78.0 0.8 %finish.1 = (f32[16,4,32]{2,1,0:T(4,128)}, f32[16,32]{1,0:T(8,128)}) custom-call(f32[640,128]{1,0:T(8,128)S(1)} %bitcast.7, s32[16,128]{1,0:T(8,128)S(1)} %copy-done.2, s32[16,128]{1,0:T(8,128)S(1)} %copy-done.3), custom_call_target="tpu_custom_call" | custom-call | tf_op jit(solution)/shard_map/finish/pallas_call | solution.py:281
  (2 shorter events, 0.0 us)
Async XLA Ops:
  2.3 29.6 %all-to-all-start = ((bf16[32,64,128]{2,1,0:T(8,128)(2,1)}), bf16[32,64,128]{2,1,0:T(8,128)(2,1)S(1)}, u32[]{:S(2)}, u32[]{:S(2)}) async-start(bf16[32,64,128]{2,1,0:T(8,128)(2,1)} %broadcast_in_dim.4), calls=%async_computation | async-start | bytes 1048576 | tf_op jit(solution)/shard_map/all_to_all | solution.py:303
  16.8 0.9 %copy-start = (bf16[16,32,128]{2,1,0:T(8,128)(2,1)S(1)}, bf16[16,32,128]{2,1,0:T(8,128)(2,1)}, u32[]{:S(2)}) copy-start(bf16[16,32,128]{2,1,0:T(8,128)(2,1)} %param.6) | copy-start | bytes 393220
  17.7 14.2 %copy-start.5 = (s32[96]{0:T(128)S(1)}, s32[96]{0:T(128)}, u32[]{:S(2)}) copy-start(s32[96]{0:T(128)} %count_ref.3) | copy-start | bytes 1156
  17.7 14.2 %copy-start.6 = (s32[8,128]{1,0:T(8,128)S(1)}, s32[8,128]{1,0:T(8,128)}, u32[]{:S(2)}) copy-start(s32[8,128]{1,0:T(8,128)} %get-tuple-element.16.place_ref) | copy-start | bytes 12292
  17.7 14.2 %copy-start.7 = (s32[96]{0:T(128)S(1)}, s32[96]{0:T(128)}, u32[]{:S(2)}) copy-start(s32[96]{0:T(128)} %get-tuple-element.13.order_ref) | copy-start | bytes 1156
  17.7 14.2 %copy-start.8 = (s32[6]{0:T(128)S(1)}, s32[6]{0:T(128)}, u32[]{:S(2)}) copy-start(s32[6]{0:T(128)} %get-tuple-element.14.tiles_ref) | copy-start | bytes 76
  31.9 1.9 %copy-start.4 = (bf16[96,128,128]{2,1,0:T(8,128)(2,1)S(1)}, bf16[96,128,128]{2,1,0:T(8,128)(2,1)}, u32[]{:S(2)}) copy-start(bf16[96,128,128]{2,1,0:T(8,128)(2,1)} %p_ref.1) | copy-start | bytes 9437188
  33.8 21.2 %copy-start.1 = (bf16[16,32,128]{2,1,0:T(8,128)(2,1)S(1)}, bf16[16,32,128]{2,1,0:T(8,128)(2,1)}, u32[]{:S(2)}) copy-start(bf16[16,32,128]{2,1,0:T(8,128)(2,1)} %param.6) | copy-start | bytes 393220
  45.0 33.0 %copy-start.2 = (s32[16,128]{1,0:T(8,128)S(1)}, s32[16,128]{1,0:T(8,128)}, u32[]{:S(2)}) copy-start(s32[16,128]{1,0:T(8,128)} %get-tuple-element.20.shard_ref) | copy-start | bytes 24580
  45.0 33.0 %copy-start.3 = (s32[16,128]{1,0:T(8,128)S(1)}, s32[16,128]{1,0:T(8,128)}, u32[]{:S(2)}) copy-start(s32[16,128]{1,0:T(8,128)} %get-tuple-element.21.local_ref) | copy-start | bytes 24580
  45.0 18.7 %all-to-all-start.1 = ((f32[32,2,128]{2,1,0:T(2,128)}), f32[32,2,128]{2,1,0:T(2,128)S(1)}, u32[]{:S(2)}, u32[]{:S(2)}) async-start(f32[32,2,128]{2,1,0:T(2,128)} %bitcast.3), calls=%async_computation.1 | async-start | bytes 65536 | tf_op jit(solution)/shard_map/all_to_all | solution.py:311

commit v5 on v4

v5 whole, which is shorter than its diff:
```python
import functools

import jax
import jax.numpy as jnp
from jax import lax
from jax.experimental import pallas as pl
from jax.experimental.pallas import tpu as pltpu
from jax.sharding import PartitionSpec as P

NPROBE = 4
LANES = 128
MIB = 1024 * 1024
LEVELS = 3
GROUP = 16
ROWS = 16
PER = 16
SENT = 256


def insert(running, x):
    out = []
    for rank, held in enumerate(running):
        out.append(jnp.maximum(held, x))
        if rank + 1 < len(running):
            x = jnp.minimum(held, x)
    return out


def streams(levels):
    return [2] * levels + [NPROBE]


def feed(xs, lists):
    for level in range(len(lists) - 1):
        half = len(xs) // 2
        losers = [jnp.minimum(a, b) for a, b in zip(xs[:half], xs[half:])]
        xs = [jnp.maximum(a, b) for a, b in zip(xs[:half], xs[half:])]
        for x in losers:
            lists[level] = insert(lists[level], x)
    for x in xs:
        lists[-1] = insert(lists[-1], x)


def merge_lists(a, b):
    m = [jnp.maximum(a[i], b[NPROBE - 1 - i]) for i in range(NPROBE)]
    for i, j in ((0, 2), (1, 3), (0, 1), (2, 3)):
        m[i], m[j] = jnp.maximum(m[i], m[j]), jnp.minimum(m[i], m[j])
    return m


def fold_sublanes(lists):
    for shift in (4, 2, 1):
        lists = merge_lists(lists, [pltpu.roll(t, shift, 0) for t in lists])
    return lists


def probe_kernel(q_ref, c_ref, o_ref, list_ref):
    step = pl.program_id(0)
    kept = streams(LEVELS)
    nq = q_ref.shape[0]

    def held_lists(col):
        at, lists = 0, []
        for k in kept:
            lists.append([list_ref[at + a, :, col : col + LANES] for a in range(k)])
            at += k
        return lists

    @pl.when(step == 0)
    def _():
        list_ref[...] = jnp.full(list_ref.shape, -jnp.inf, jnp.float32)
        o_ref[...] = jnp.zeros(o_ref.shape, jnp.float32)

    scores = lax.dot_general(
        c_ref[...], q_ref[...], (((1,), (1,)), ((), ())), preferred_element_type=jnp.float32
    )
    for col in range(0, nq, LANES):
        lists = held_lists(col)
        for row in range(0, scores.shape[0], 8 * GROUP):
            feed([scores[row + 8 * r : row + 8 * r + 8, col : col + LANES] for r in range(GROUP)], lists)
        for at, t in enumerate(sum(lists, [])):
            list_ref[at, :, col : col + LANES] = t

    @pl.when(step == pl.num_programs(0) - 1)
    def _():
        for tile in range(nq // LANES):
            lists = held_lists(tile * LANES)
            top = lists[-1]
            for x in sum(lists[:-1], []):
                top = insert(top, x)
            top = fold_sublanes(top)
            for rank in range(NPROBE):
                row = rank * (nq // LANES) + tile
                o_ref[row : row + 1, :] = top[rank][0:1]


def probe(queries, centroids, rows, block=4096):
    nq, dim = queries.shape
    total = centroids.shape[0]
    return pl.pallas_call(
        probe_kernel,
        grid=(total // block,),
        in_specs=[pl.BlockSpec((nq, dim), lambda i: (0, 0)), pl.BlockSpec((block, dim), lambda i: (i, 0))],
        out_specs=pl.BlockSpec((rows, LANES), lambda i: (0, 0)),
        out_shape=jax.ShapeDtypeStruct((rows, LANES), jnp.float32),
        scratch_shapes=[pltpu.VMEM((sum(streams(LEVELS)), 8, nq), jnp.float32)],
        compiler_params=pltpu.CompilerParams(vmem_limit_bytes=58 * MIB),
        cost_estimate=pl.CostEstimate(
            flops=4 * nq * total * dim, bytes_accessed=2 * total * dim, transcendentals=0
        ),
        name="probe",
    )(queries, centroids)


def prepare_kernel(count_ref, home_ref, cand_ref, shard_ref, local_ref, place_ref, order_ref, tiles_ref):
    total = count_ref.shape[1]
    counts = jnp.concatenate([count_ref[...], jnp.full((1, LANES - total), 1 - ROWS, jnp.int32)], axis=1)
    tiles = lax.shift_right_arithmetic(counts + (ROWS - 1), ROWS.bit_length() - 1)
    lane = lax.broadcasted_iota(jnp.int32, (LANES, LANES), 1).astype(jnp.float32)
    tiles_across = jnp.broadcast_to(tiles.astype(jnp.float32), (LANES, LANES))
    across = tiles_across * LANES - lane
    down = across.T
    place_across = jnp.sum(jnp.where(down > across, 1.0, 0.0), axis=0, keepdims=True)
    place_down = jnp.sum(jnp.where(across > down, 1.0, 0.0), axis=1, keepdims=True)
    stands = place_down == lane
    order = jnp.sum(jnp.where(stands, lane.T, 0.0), axis=0, keepdims=True)
    sorted_tiles = jnp.sum(jnp.where(stands, tiles_across.T, 0.0), axis=0, keepdims=True)
    place_ref[...] = jnp.broadcast_to(place_across, place_ref.shape).astype(jnp.int32)
    order_ref[...] = order.astype(jnp.int32)
    tiles_ref[...] = sorted_tiles.astype(jnp.int32)
    nq, nk = cand_ref.shape
    cand = jnp.concatenate([cand_ref[...], jnp.zeros((nq, LANES - nk), jnp.int32)], axis=1)
    block, at = lax.shift_right_logical(cand, 7), jnp.bitwise_and(cand, LANES - 1)
    store = jnp.zeros((nq, LANES), jnp.int32)
    for b in range(home_ref.shape[0]):
        line = jnp.broadcast_to(home_ref[b : b + 1, :], (nq, LANES))
        store = jnp.where(block == b, jnp.take_along_axis(line, at, axis=1), store)
    shard_ref[...] = store // total
    local_ref[...] = store % total


def prepare(counts, home, candidates):
    nq = candidates.shape[0]
    index = jax.ShapeDtypeStruct((nq, LANES), jnp.int32)
    line = jax.ShapeDtypeStruct((1, LANES), jnp.int32)
    return pl.pallas_call(
        prepare_kernel,
        out_shape=[index, index, jax.ShapeDtypeStruct((8, LANES), jnp.int32), line, line],
        compiler_params=pltpu.CompilerParams(vmem_limit_bytes=58 * MIB),
        cost_estimate=pl.CostEstimate(flops=10**8, bytes_accessed=10**5, transcendentals=0),
        name="prepare",
    )(counts.reshape(1, -1), home.reshape(-1, LANES), candidates)


def maxsim_kernel(
    count_ref, order_ref, tiles_ref, g_ref, p_ref, place_ref, o_ref, best_ref, lhs_ref, table_ref, *, width, tokens, mine
):
    count, length, dim = p_ref.shape
    columns = g_ref.shape[0]
    best_ref[count:, :] = jnp.zeros((best_ref.shape[0] - count, columns), jnp.float32)

    def one(g, carry):
        at = pl.multiple_of(g * PER, PER)
        for tiles in range(1, length // ROWS + 1):
            rows = tiles * ROWS

            @pl.when(tiles_ref[0, at] == tiles)
            def _(rows=rows):
                index = lax.broadcasted_iota(jnp.int32, (rows, dim), 0)
                for i in range(PER):
                    p = order_ref[0, at + i]
                    block = p_ref[p, :rows, :].astype(jnp.float32)
                    block = jnp.where(index < count_ref[p], block, block[0:1])
                    lhs_ref[i * rows : (i + 1) * rows, :] = block.astype(lhs_ref.dtype)
                lhs = lhs_ref[: PER * rows, :]
                for col in range(0, columns, width):
                    dots = lax.dot_general(
                        lhs, g_ref[col : col + width, :], (((1,), (1,)), ((), ())), preferred_element_type=jnp.float32
                    )
                    best = jnp.max(dots.reshape(PER, rows // 8, 8, width), axis=1)
                    best_ref[pl.ds(at, PER), col : col + width] = jnp.max(best, axis=1)

        return carry

    lax.fori_loop(0, count // PER, one, 0)
    nq = columns // tokens
    owner = lax.broadcasted_iota(jnp.int32, (nq, columns), 1) // tokens
    pick = (owner == lax.broadcasted_iota(jnp.int32, (nq, columns), 0)).astype(jnp.bfloat16)
    rest = best_ref[...]
    total = jnp.zeros((nq, best_ref.shape[0]), jnp.float32)
    for _ in range(3):
        part = rest.astype(jnp.bfloat16)
        rest = rest - part.astype(jnp.float32)
        total += lax.dot_general(pick, part, (((1,), (1,)), ((), ())), preferred_element_type=jnp.float32)
    place = jnp.broadcast_to(place_ref[0:1, :], total.shape)
    table_ref[...] = jnp.take_along_axis(total, place, axis=1)
    copies = o_ref.shape[0] // nq
    for j in range(mine):
        lines = table_ref[pl.ds(j, nq // mine, stride=mine), :]
        for k in range(copies):
            o_ref[pl.ds(k * mine + j, nq // mine, stride=copies * mine), :] = lines


def maxsim(counts, order, tiles, gathered, passages, places, tokens, mine, copies, width=512):
    columns, dim = gathered.shape
    count, length, _ = passages.shape
    nq = columns // tokens
    vmem = pl.BlockSpec(memory_space=pltpu.VMEM)
    smem = pl.BlockSpec(memory_space=pltpu.SMEM)
    return pl.pallas_call(
        functools.partial(maxsim_kernel, width=width, tokens=tokens, mine=mine),
        in_specs=[smem, smem, smem, vmem, vmem, vmem],
        out_specs=vmem,
        out_shape=jax.ShapeDtypeStruct((copies * nq, LANES), jnp.float32),
        scratch_shapes=[
            pltpu.VMEM((LANES, columns), jnp.float32),
            pltpu.VMEM((PER * length, dim), jnp.bfloat16),
            pltpu.VMEM((nq, LANES), jnp.float32),
        ],
        compiler_params=pltpu.CompilerParams(vmem_limit_bytes=40 * MIB),
        cost_estimate=pl.CostEstimate(
            flops=2 * columns * count * length * dim, bytes_accessed=2 * passages.size, transcendentals=0
        ),
        name="maxsim",
    )(counts, order, tiles, gathered, passages, places)


def merge_kernel(r_ref, o_ref):
    tiles = r_ref.shape[1] // NPROBE
    nt = o_ref.shape[2]
    for tile in range(tiles):
        top = fold_sublanes([r_ref[:, rank * tiles + tile, :] for rank in range(NPROBE)])
        four = jnp.concatenate([t[0:1] for t in top], axis=0)
        for i in range(LANES // nt):
            o_ref[tile * (LANES // nt) + i] = four[:, i * nt : (i + 1) * nt]


def merge(received, rows, nq, nt):
    cents = received.shape[0]
    return pl.pallas_call(
        merge_kernel,
        grid=(1,),
        in_specs=[pl.BlockSpec((cents, rows, LANES), lambda i: (0, 0, 0))],
        out_specs=pl.BlockSpec((nq, NPROBE, nt), lambda i: (0, 0, 0)),
        out_shape=jax.ShapeDtypeStruct((nq, NPROBE, nt), jnp.float32),
        compiler_params=pltpu.CompilerParams(vmem_limit_bytes=16 * MIB),
        name="merge",
    )(received)


def lookup_kernel(r_ref, shard_ref, local_ref, o_ref):
    nq, nk = o_ref.shape
    home, local = shard_ref[...], local_ref[...]
    score = jnp.zeros(home.shape, jnp.float32)
    for s in range(r_ref.shape[0] // nq):
        table = r_ref[s * nq : (s + 1) * nq, :]
        score = jnp.where(home == s, jnp.take_along_axis(table, local, axis=1), score)
    o_ref[...] = score[:, :nk]


def lookup(received, shard_index, local_index, nq, nk):
    return pl.pallas_call(
        lookup_kernel,
        out_shape=jax.ShapeDtypeStruct((nq, nk), jnp.float32),
        compiler_params=pltpu.CompilerParams(vmem_limit_bytes=16 * MIB),
        name="lookup",
    )(received, shard_index, local_index)


def spread(block, copies):
    return jnp.broadcast_to(block[None], (copies,) + block.shape).reshape((-1,) + block.shape[1:])


def body(queries, centroids, passages, counts, home, candidates):
    nq, nt, dim = queries.shape
    nk = candidates.shape[1]
    shards, cents = lax.axis_size("shard"), lax.axis_size("cent")
    mine = nq // cents
    tokens = queries.reshape(nq * nt, dim)
    own = lax.dynamic_slice_in_dim(tokens, lax.axis_index("cent") * mine * nt, mine * nt, 0)
    gathered = lax.all_to_all(spread(own, shards), "shard", 0, 0, tiled=True)
    rows = NPROBE * nq * nt // LANES
    lists = probe(tokens, centroids, SENT)
    shard_index, local_index, places, order, tiles = prepare(counts, home, candidates)
    gathered, lists, places, order, tiles = lax.optimization_barrier((gathered, lists, places, order, tiles))
    received = pltpu.with_memory_space_constraint(lax.all_gather(lists, "cent"), pltpu.HBM)
    table = maxsim(counts, order, tiles, gathered, passages, places, nt, mine, cents)
    returned = lax.all_to_all(table, ("shard", "cent"), 0, 0, tiled=True)
    probe_scores = merge(received, rows, nq, nt)
    returned, probe_scores = lax.optimization_barrier((returned, probe_scores))
    passage_scores = lookup(returned, shard_index, local_index, nq, nk)
    return jnp.transpose(probe_scores, (0, 2, 1)), passage_scores


def solution(mesh):
    in_specs = (
        P("shard", None, None),
        P("cent", None),
        P("shard", None, None),
        P("shard"),
        P(),
        P("shard", "cent"),
    )
    out_specs = (P("shard", None, None), P("shard", "cent"))
    return jax.shard_map(body, mesh=mesh, in_specs=in_specs, out_specs=out_specs, check_vma=False)
```

time: 79.6 us -> 90.3 us (1.13)
  blocking collectives: 14.3 us -> 0 us
  between operations: 0.75 us -> 14.1 us
  waiting for transfers between devices: 5.64 us -> 13.9 us
  starting transfers between devices: 22 us -> 24.7 us
  Pallas kernels: 31.8 us -> 33.2 us
  local copies, waits for them, and re-layouts: 4.47 us -> 3.54 us
    all_to_all x1 -> x0, blocking collectives: 14.3 us -> none  [body(): received = lax.all_to_all(final, 'cent', 0, 0, tiled=True)]
    all_to_all x1, waiting for transfers between devices: 5.63 us -> 12.9 us  [body(): returned = lax.all_to_all(table, ('shard', 'cent'), 0, 0, tiled=True)]
    all_to_all x1, starting transfers between devices: 9.92 us -> 12.6 us  [body(): returned = lax.all_to_all(table, ('shard', 'cent'), 0, 0, tiled=True)]
    pallas_call x1, Pallas kernels: 11.2 us -> 12.5 us  [maxsim(): pl.pallas_call(functools.partial(maxsim_kernel, width=width, tokens=token...]
    all_gather x0 -> x1, waiting for transfers between devices: none -> 0.96 us  [body(): lax.all_gather(lists, 'cent')]
    unnamed x18 -> x14, local copies, waits for them, and re-layouts: 2.81 us -> 1.91 us
  transfers between devices with their start and end apart: 2 -> 3, of which waited for: 1 -> 2; matrix products, arithmetic and copies ran while one was open for 0% -> 0% of each run, Pallas kernels for 25% -> 36%
where the time goes in v5:
time: 90.3 us; the launch traced here: 89.4 us
  Pallas kernels  33.2 us (37%)
  starting transfers between devices  24.7 us (27%)
  between operations  14.1 us (16%)
  waiting for transfers between devices  13.9 us (15%)
  local copies, waits for them, and re-layouts  3.54 us (4%)
    pallas_call x1, Pallas kernels, probe(): pl.pallas_call(probe_kernel, grid=(total // block,), in_specs=[pl.BlockSp...  16.7 us
    all_to_all x1, waiting for transfers between devices, body(): returned = lax.all_to_all(table, ('shard', 'cent'), 0, 0, tiled=True)  12.9 us
    all_to_all x1, starting transfers between devices, body(): returned = lax.all_to_all(table, ('shard', 'cent'), 0, 0, tiled=True)  12.6 us
    pallas_call x1, Pallas kernels, maxsim(): pl.pallas_call(functools.partial(maxsim_kernel, width=width, tokens=token...  12.5 us
    all_to_all x1, starting transfers between devices, body(): gathered = lax.all_to_all(spread(own, shards), 'shard', 0, 0, tiled=True)  12 us
    unnamed x14, local copies, waits for them, and re-layouts  1.91 us
  transfers between devices with their start and end apart: 3, of which 2 were waited for; matrix products, arithmetic and copies ran while one was open for 0% of the time, Pallas kernels for 36%

profile of v5, /device:TPU:1, one launch (start us, length us, event | category | flops | bytes accessed | tf_op | source)
XLA Modules:
  0.0 89.4 jit_solution(3927686320238378193)
XLA Ops:
  7.2 0.7 constant_dynamic-slice_fusion
  7.9 0.9 %broadcast_in_dim.2 = bf16[32,64,128]{2,1,0:T(8,128)(2,1)} broadcast(bf16[64,128]{1,0:T(8,128)(2,1)S(1)} %constant_dynamic-slice_fusion), dimensions={1,2} | broadcast | bytes 540672 | tf_op jit(solution)/shard_map/broadcast_in_dim | solution.py:271
  8.8 12.0 %all-to-all-start = ((bf16[32,64,128]{2,1,0:T(8,128)(2,1)}), bf16[32,64,128]{2,1,0:T(8,128)(2,1)S(1)}, u32[]{:S(2)}, u32[]{:S(2)}) async-start(bf16[32,64,128]{2,1,0:T(8,128)(2,1)} %broadcast_in_dim.2), calls=%async_computation | async-start | bytes 1048576 | tf_op jit(solution)/shard_map/all_to_all | solution.py:281
  20.8 0.0 all-gather.3.cloned.1.call-start
  20.9 1.6 %prepare.1 = (s32[16,128]{1,0:T(8,128)}, s32[16,128]{1,0:T(8,128)}, s32[8,128]{1,0:T(8,128)}, s32[1,128]{1,0:T(1,128)}, s32[1,128]{1,0:T(1,128)}) custom-call(s32[1,96]{1,0:T(1,128)} %bitcast.10, s32[24,128]{1,0:T(8,128)} %bitcast.15, s32[16,32]{1,0:T(8,128)} %cand_ref.1), custom_call_target="tpu_custom_call" | custom-call | flops 100000000 | bytes 100000 | tf_op jit(solution)/shard_map/prepare/pallas_call | solution.py:146
  22.5 0.0 copy-start.3
  22.5 0.0 copy-start.4
  22.5 0.0 copy-start.5
  22.5 0.0 copy-start.6
  22.5 16.7 %probe.1 = f32[256,128]{1,0:T(8,128)} custom-call(bf16[512,128]{1,0:T(8,128)(2,1)} %bitcast.14, bf16[32768,128]{1,0:T(8,128)(2,1)} %c_ref.1), custom_call_target="tpu_custom_call" | custom-call | flops 8589934592 | bytes 8388608 | tf_op jit(solution)/shard_map/probe/pallas_call | solution.py:100
  39.3 0.0 all-to-all-done
  39.3 0.0 all-gather.3.cloned.1.call-update
  39.3 0.0 copy-done.3
  39.3 0.0 copy-done.4
  39.3 0.0 copy-done.5
  39.3 0.0 copy-done.6
  39.3 0.0 copy-start.2
  39.3 1.9 %copy-done.2 = bf16[96,128,128]{2,1,0:T(8,128)(2,1)S(1)} copy-done((bf16[96,128,128]{2,1,0:T(8,128)(2,1)S(1)}, bf16[96,128,128]{2,1,0:T(8,128)(2,1)}, u32[]{:S(2)}) %copy-start.2) | copy-done | bytes 3145752
  41.2 0.0 copy-start
  41.2 0.0 copy-start.1
  41.2 12.5 %maxsim.1 = f32[512,128]{1,0:T(8,128)} custom-call(s32[96]{0:T(128)S(1)} %copy-done.3, s32[1,128]{1,0:T(1,128)S(1)} %copy-done.5, s32[1,128]{1,0:T(1,128)S(1)} %copy-done.6, bf16[2048,128]{1,0:T(8,128)(2,1)S(1)} %bitcast.9, bf16[96,128,128]{2,1,0:T(8,128)(2,1)S(1)} %copy-done.2, s32[8,128]{1,0:T(8,128)S(1)} %copy-done.4), custom_call_target="tpu_custom_call" | custom-call | flops 6442450944 | bytes 3145728 | tf_op jit(solution)/shard_map/maxsim/pallas_call | solution.py:210
  53.7 12.6 %all-to-all-start.1 = ((f32[256,2,128]{2,1,0:T(2,128)}), f32[256,2,128]{2,1,0:T(2,128)S(1)}, u32[]{:S(2)}, u32[]{:S(2)}) async-start(f32[256,2,128]{2,1,0:T(2,128)} %bitcast.4), calls=%async_computation.1 | async-start | bytes 524288 | tf_op jit(solution)/shard_map/all_to_all | solution.py:288
  66.3 1.0 %all-gather.3.cloned.1.call-done = f32[2048,128]{1,0:T(8,128)} async-done(((f32[256,128]{1,0:T(8,128)}), f32[2048,128]{1,0:T(8,128)}) %all-gather.3.cloned.1.call-update) | async-done | bytes 1048592 | tf_op jit(solution)/shard_map/all_gather | solution.py:286
  67.3 1.6 %merge.1 = f32[16,4,32]{2,1,0:T(4,128)} custom-call(f32[8,256,128]{2,1,0:T(8,128)} %bitcast.11), custom_call_target="tpu_custom_call" | custom-call | tf_op jit(solution)/shard_map/merge/pallas_call | solution.py:240
  68.9 12.9 %all-to-all-done.1 = f32[256,2,128]{2,1,0:T(2,128)S(1)} async-done(((f32[256,2,128]{2,1,0:T(2,128)}), f32[256,2,128]{2,1,0:T(2,128)S(1)}, u32[]{:S(2)}, u32[]{:S(2)}) %all-to-all-start.1) | async-done | bytes 262176 | tf_op jit(solution)/shard_map/all_to_all | solution.py:288
  81.8 0.0 copy-done
  81.8 0.0 copy-done.1
  81.8 0.7 lookup.1
Async XLA Ops:
  8.8 30.5 %all-to-all-start = ((bf16[32,64,128]{2,1,0:T(8,128)(2,1)}), bf16[32,64,128]{2,1,0:T(8,128)(2,1)S(1)}, u32[]{:S(2)}, u32[]{:S(2)}) async-start(bf16[32,64,128]{2,1,0:T(8,128)(2,1)} %broadcast_in_dim.2), calls=%async_computation | async-start | bytes 1048576 | tf_op jit(solution)/shard_map/all_to_all | solution.py:281
  20.8 46.5 %all-gather.3.cloned.1.call-start = ((), (), s32[]{:S(2)}) async-start(), calls=%async_computation.2 | async-start | bytes 1179648 | tf_op jit(solution)/shard_map/all_gather | solution.py:286
  22.5 16.8 %copy-start.3 = (s32[96]{0:T(128)S(1)}, s32[96]{0:T(128)}, u32[]{:S(2)}) copy-start(s32[96]{0:T(128)} %count_ref.1) | copy-start | bytes 1156
  22.5 16.8 %copy-start.4 = (s32[8,128]{1,0:T(8,128)S(1)}, s32[8,128]{1,0:T(8,128)}, u32[]{:S(2)}) copy-start(s32[8,128]{1,0:T(8,128)} %get-tuple-element.20.place_ref) | copy-start | bytes 12292
  22.5 16.8 %copy-start.5 = (s32[1,128]{1,0:T(1,128)S(1)}, s32[1,128]{1,0:T(1,128)}, u32[]{:S(2)}) copy-start(s32[1,128]{1,0:T(1,128)} %get-tuple-element.17.order_ref) | copy-start | bytes 1540
  22.5 16.8 %copy-start.6 = (s32[1,128]{1,0:T(1,128)S(1)}, s32[1,128]{1,0:T(1,128)}, u32[]{:S(2)}) copy-start(s32[1,128]{1,0:T(1,128)} %get-tuple-element.18.tiles_ref) | copy-start | bytes 1540
  39.3 1.9 %copy-start.2 = (bf16[96,128,128]{2,1,0:T(8,128)(2,1)S(1)}, bf16[96,128,128]{2,1,0:T(8,128)(2,1)}, u32[]{:S(2)}) copy-start(bf16[96,128,128]{2,1,0:T(8,128)(2,1)} %p_ref.1) | copy-start | bytes 9437188
  41.2 40.6 %copy-start = (s32[16,128]{1,0:T(8,128)S(1)}, s32[16,128]{1,0:T(8,128)}, u32[]{:S(2)}) copy-start(s32[16,128]{1,0:T(8,128)} %get-tuple-element.24.shard_ref) | copy-start | bytes 24580
  41.2 40.6 %copy-start.1 = (s32[16,128]{1,0:T(8,128)S(1)}, s32[16,128]{1,0:T(8,128)}, u32[]{:S(2)}) copy-start(s32[16,128]{1,0:T(8,128)} %get-tuple-element.25.local_ref) | copy-start | bytes 24580
  53.7 28.1 %all-to-all-start.1 = ((f32[256,2,128]{2,1,0:T(2,128)}), f32[256,2,128]{2,1,0:T(2,128)S(1)}, u32[]{:S(2)}, u32[]{:S(2)}) async-start(f32[256,2,128]{2,1,0:T(2,128)} %bitcast.4), calls=%async_computation.1 | async-start | bytes 524288 | tf_op jit(solution)/shard_map/all_to_all | solution.py:288
Sparse Core Ops, SparseCore 0:
  39.4 27.8 all-gather.2

commit v6 on v4

--- a/solution.py
+++ b/solution.py
@@ -12,8 +12,7 @@
 MIB = 1024 * 1024
 LEVELS = 3
 GROUP = 16
-ROWS = 16
-CLASSES = 128 // ROWS
+ROWS = 32
 PER = 16
 FIRST = 7
 
@@ -127,68 +126,44 @@
     )(queries, centroids, *before)
 
 
-def prepare_kernel(count_ref, home_ref, cand_ref, shard_ref, local_ref, place_ref, order_ref, tiles_ref, next_ref):
-    total = order_ref.shape[0]
-    lanes = lax.broadcasted_iota(jnp.int32, place_ref.shape, 1)
-
-    def tiles_of(p):
-        return lax.shift_right_logical(count_ref[p] + (ROWS - 1), ROWS.bit_length() - 1)
-
-    for k in range(CLASSES + 1):
-        next_ref[k] = 0
-
-    def tally(p, carry):
-        k = CLASSES + 1 - tiles_of(p)
-        next_ref[k] = next_ref[k] + 1
-        return carry
-
-    lax.fori_loop(0, total, tally, 0, unroll=8)
-    for k in range(1, CLASSES + 1):
-        next_ref[k] = next_ref[k] + next_ref[k - 1]
-
-    def one(p, places):
-        k = CLASSES - tiles_of(p)
-        at = next_ref[k]
-        next_ref[k] = at + 1
-        order_ref[at] = p
-        return jnp.where(lanes == p, at, places)
-
-    place_ref[...] = lax.fori_loop(0, total, one, jnp.zeros(place_ref.shape, jnp.int32), unroll=8)
-    for g in range(total // PER):
-        tiles_ref[g] = tiles_of(order_ref[g * PER])
+def prepare_kernel(count_ref, home_ref, cand_ref, shard_ref, local_ref, place_ref, order_ref, tiles_ref):
+    total = count_ref.shape[1]
+    counts = jnp.concatenate([count_ref[...], jnp.full((1, LANES - total), 1 - ROWS, jnp.int32)], axis=1)
+    tiles = lax.shift_right_arithmetic(counts + (ROWS - 1), ROWS.bit_length() - 1)
+    lane = lax.broadcasted_iota(jnp.int32, (LANES, LANES), 1).astype(jnp.float32)
+    tiles_across = jnp.broadcast_to(tiles.astype(jnp.float32), (LANES, LANES))
+    across = tiles_across * LANES - lane
+    down = across.T
+    place_across = jnp.sum(jnp.where(down > across, 1.0, 0.0), axis=0, keepdims=True)
+    place_down = jnp.sum(jnp.where(across > down, 1.0, 0.0), axis=1, keepdims=True)
+    stands = place_down == lane
+    order = jnp.sum(jnp.where(stands, lane.T, 0.0), axis=0, keepdims=True)
+    sorted_tiles = jnp.sum(jnp.where(stands, tiles_across.T, 0.0), axis=0, keepdims=True)
+    place_ref[...] = jnp.broadcast_to(place_across, place_ref.shape).astype(jnp.int32)
+    order_ref[...] = order.astype(jnp.int32)
+    tiles_ref[...] = sorted_tiles.astype(jnp.int32)
     nq, nk = cand_ref.shape
     cand = jnp.concatenate([cand_ref[...], jnp.zeros((nq, LANES - nk), jnp.int32)], axis=1)
-    block, lane = lax.shift_right_logical(cand, 7), jnp.bitwise_and(cand, LANES - 1)
+    block, at = lax.shift_right_logical(cand, 7), jnp.bitwise_and(cand, LANES - 1)
     store = jnp.zeros((nq, LANES), jnp.int32)
     for b in range(home_ref.shape[0]):
         line = jnp.broadcast_to(home_ref[b : b + 1, :], (nq, LANES))
-        store = jnp.where(block == b, jnp.take_along_axis(line, lane, axis=1), store)
+        store = jnp.where(block == b, jnp.take_along_axis(line, at, axis=1), store)
     shard_ref[...] = store // total
     local_ref[...] = store % total
 
 
 def prepare(counts, home, candidates):
     nq = candidates.shape[0]
-    total = counts.shape[0]
     index = jax.ShapeDtypeStruct((nq, LANES), jnp.int32)
-    vmem = pl.BlockSpec(memory_space=pltpu.VMEM)
-    smem = pl.BlockSpec(memory_space=pltpu.SMEM)
+    line = jax.ShapeDtypeStruct((1, LANES), jnp.int32)
     return pl.pallas_call(
         prepare_kernel,
-        in_specs=[smem, vmem, vmem],
-        out_specs=[vmem, vmem, vmem, smem, smem],
-        out_shape=[
-            index,
-            index,
-            jax.ShapeDtypeStruct((8, LANES), jnp.int32),
-            jax.ShapeDtypeStruct((total,), jnp.int32),
-            jax.ShapeDtypeStruct((total // PER,), jnp.int32),
-        ],
-        scratch_shapes=[pltpu.SMEM((CLASSES + 1,), jnp.int32)],
+        out_shape=[index, index, jax.ShapeDtypeStruct((8, LANES), jnp.int32), line, line],
         compiler_params=pltpu.CompilerParams(vmem_limit_bytes=58 * MIB),
-        cost_estimate=pl.CostEstimate(flops=10**9, bytes_accessed=10**5, transcendentals=0),
+        cost_estimate=pl.CostEstimate(flops=10**8, bytes_accessed=10**5, transcendentals=0),
         name="prepare",
-    )(counts, home.reshape(-1, LANES), candidates)
+    )(counts.reshape(1, -1), home.reshape(-1, LANES), candidates)
 
 
 def maxsim_kernel(count_ref, order_ref, tiles_ref, g_ref, p_ref, place_ref, o_ref, best_ref, lhs_ref, *, width, tokens):
@@ -201,11 +176,11 @@
         for tiles in range(1, length // ROWS + 1):
             rows = tiles * ROWS
 
-            @pl.when(tiles_ref[g] == tiles)
+            @pl.when(tiles_ref[0, at] == tiles)
             def _(rows=rows):
                 index = lax.broadcasted_iota(jnp.int32, (rows, dim), 0)
                 for i in range(PER):
-                    p = order_ref[at + i]
+                    p = order_ref[0, at + i]
                     block = p_ref[p, :rows, :].astype(jnp.float32)
                     block = jnp.where(index < count_ref[p], block, block[0:1])
                     lhs_ref[i * rows : (i + 1) * rows, :] = block.astype(lhs_ref.dtype)
@@ -305,7 +280,7 @@
     centroids = pltpu.with_memory_space_constraint(centroids, pltpu.HBM)
     lists = probe(tokens, centroids, (), 0, FIRST)
     shard_index, local_index, places, order, tiles = prepare(counts, home, candidates)
-    gathered, lists = lax.optimization_barrier((gathered, lists))
+    gathered, lists, places, order, tiles = lax.optimization_barrier((gathered, lists, places, order, tiles))
     table = maxsim(counts, order, tiles, gathered, passages, places, nt)
     table, lists = lax.optimization_barrier((table, lists))
     returned = lax.all_to_all(table, "shard", 0, 0, tiled=True)

time: 79.6 us -> 79.2 us (level)
    pallas_call x1, Pallas kernels: 11.2 us -> 12.5 us  [maxsim(): pl.pallas_call(functools.partial(maxsim_kernel, width=width, tokens=token...]
    pallas_call x1, Pallas kernels: 2.44 us -> 1.61 us  [prepare(): pl.pallas_call(prepare_kernel, out_shape=[index, index, jax.ShapeDtypeStr...]
  transfers between devices with their start and end apart: 2 -> 2, of which waited for: 1 -> 1; matrix products, arithmetic and copies ran while one was open for 0% -> 0% of each run, Pallas kernels for 25% -> 24%
where the time goes in v6:
time: 79.2 us; the launch traced here: 78.7 us
  Pallas kernels  32.2 us (41%)
  starting transfers between devices  21.4 us (27%)
  blocking collectives  14.3 us (18%)
  waiting for transfers between devices  5.64 us (7%)
  local copies, waits for them, and re-layouts  4.47 us (6%)
    pallas_call x2, Pallas kernels, probe(): pl.pallas_call(probe_kernel, grid=(steps,), in_specs=[pl.BlockSpec((nq, d...  17.3 us
    all_to_all x1, blocking collectives, body(): received = lax.all_to_all(final, 'cent', 0, 0, tiled=True)  14.3 us
    pallas_call x1, Pallas kernels, maxsim(): pl.pallas_call(functools.partial(maxsim_kernel, width=width, tokens=token...  12.5 us
    all_to_all x1, starting transfers between devices, body(): gathered = lax.all_to_all(spread(own, shards), 'shard', 0, 0, tiled=True)  12 us
    all_to_all x1, starting transfers between devices, body(): returned = lax.all_to_all(table, 'shard', 0, 0, tiled=True)  9.36 us
    all_to_all x1, waiting for transfers between devices, body(): returned = lax.all_to_all(table, 'shard', 0, 0, tiled=True)  5.64 us
    unnamed x18, local copies, waits for them, and re-layouts  2.81 us
    pallas_call x1, Pallas kernels, prepare(): pl.pallas_call(prepare_kernel, out_shape=[index, index, jax.ShapeDtypeStr...  1.61 us
  transfers between devices with their start and end apart: 2, of which 1 were waited for; matrix products, arithmetic and copies ran while one was open for 0% of the time, Pallas kernels for 24%

profile of v6, /device:TPU:1, one launch (start us, length us, event | category | flops | bytes accessed | tf_op | source)
XLA Modules:
  0.0 78.7 jit_solution(14305597969607388811)
XLA Ops:
  0.6 0.7 constant_dynamic-slice_fusion
  1.4 0.9 %broadcast_in_dim.4 = bf16[32,64,128]{2,1,0:T(8,128)(2,1)} broadcast(bf16[64,128]{1,0:T(8,128)(2,1)S(1)} %constant_dynamic-slice_fusion), dimensions={1,2} | broadcast | bytes 540672 | tf_op jit(solution)/shard_map/broadcast_in_dim | solution.py:268
  2.3 12.0 %all-to-all-start = ((bf16[32,64,128]{2,1,0:T(8,128)(2,1)}), bf16[32,64,128]{2,1,0:T(8,128)(2,1)S(1)}, u32[]{:S(2)}, u32[]{:S(2)}) async-start(bf16[32,64,128]{2,1,0:T(8,128)(2,1)} %broadcast_in_dim.4), calls=%async_computation | async-start | bytes 1048576 | tf_op jit(solution)/shard_map/all_to_all | solution.py:278
  14.3 1.6 %prepare.1 = (s32[16,128]{1,0:T(8,128)}, s32[16,128]{1,0:T(8,128)}, s32[8,128]{1,0:T(8,128)}, s32[1,128]{1,0:T(1,128)}, s32[1,128]{1,0:T(1,128)}) custom-call(s32[1,96]{1,0:T(1,128)} %bitcast.13, s32[24,128]{1,0:T(8,128)} %bitcast.16, s32[16,32]{1,0:T(8,128)} %cand_ref.1), custom_call_target="tpu_custom_call" | custom-call | flops 100000000 | bytes 100000 | tf_op jit(solution)/shard_map/prepare/pallas_call | solution.py:160
  15.9 0.0 copy-start
  15.9 0.9 %copy-done = bf16[16,32,128]{2,1,0:T(8,128)(2,1)S(1)} copy-done((bf16[16,32,128]{2,1,0:T(8,128)(2,1)S(1)}, bf16[16,32,128]{2,1,0:T(8,128)(2,1)}, u32[]{:S(2)}) %copy-start) | copy-done | bytes 131096
  16.8 0.0 copy-start.5
  16.8 0.0 copy-start.6
  16.8 0.0 copy-start.7
  16.8 0.0 copy-start.8
  16.8 14.2 %probe_0.1.refs_0_ = f32[16,128]{1,0:T(8,128)S(1)} custom-call(bf16[512,128]{1,0:T(8,128)(2,1)S(1)} %bitcast.11, bf16[32768,128]{1,0:T(8,128)(2,1)} %c_ref.3), custom_call_target="tpu_custom_call" | custom-call | flops 7516192768 | bytes 7340032 | tf_op jit(solution)/shard_map/probe_0/pallas_call | solution.py:110
  31.0 0.0 all-to-all-done
  31.0 0.0 copy-done.5
  31.1 0.0 copy-done.6
  31.1 0.0 copy-done.7
  31.1 0.0 copy-done.8
  31.1 0.0 copy-start.4
  31.1 1.9 %copy-done.4 = bf16[96,128,128]{2,1,0:T(8,128)(2,1)S(1)} copy-done((bf16[96,128,128]{2,1,0:T(8,128)(2,1)S(1)}, bf16[96,128,128]{2,1,0:T(8,128)(2,1)}, u32[]{:S(2)}) %copy-start.4) | copy-done | bytes 3145752
  33.0 0.0 copy-start.1
  33.0 12.5 %maxsim.1 = f32[64,128]{1,0:T(8,128)} custom-call(s32[96]{0:T(128)S(1)} %copy-done.5, s32[1,128]{1,0:T(1,128)S(1)} %copy-done.7, s32[1,128]{1,0:T(1,128)S(1)} %copy-done.8, bf16[2048,128]{1,0:T(8,128)(2,1)S(1)} %bitcast.9, bf16[96,128,128]{2,1,0:T(8,128)(2,1)S(1)} %copy-done.4, s32[8,128]{1,0:T(8,128)S(1)} %copy-done.6), custom_call_target="tpu_custom_call" | custom-call | flops 6442450944 | bytes 3145728 | tf_op jit(solution)/shard_map/maxsim/pallas_call | solution.py:217
  45.5 0.0 copy-start.2
  45.5 0.0 copy-start.3
  45.5 9.4 %all-to-all-start.1 = ((f32[32,2,128]{2,1,0:T(2,128)}), f32[32,2,128]{2,1,0:T(2,128)S(1)}, u32[]{:S(2)}, u32[]{:S(2)}) async-start(f32[32,2,128]{2,1,0:T(2,128)} %bitcast.4), calls=%async_computation.1 | async-start | bytes 65536 | tf_op jit(solution)/shard_map/all_to_all | solution.py:286
  54.8 0.0 copy-done.1
  54.8 3.1 %probe_7.1 = f32[16,128]{1,0:T(8,128)S(1)} custom-call(bf16[512,128]{1,0:T(8,128)(2,1)S(1)} %bitcast.12, bf16[32768,128]{1,0:T(8,128)(2,1)} %c_ref.3, f32[16,128]{1,0:T(8,128)S(1)} %probe_0.1.refs_0_), custom_call_target="tpu_custom_call" | custom-call | flops 1073741824 | bytes 1048576 | tf_op jit(solution)/shard_map/probe_7/pallas_call | solution.py:110
  58.0 5.6 %all-to-all-done.1 = f32[32,2,128]{2,1,0:T(2,128)S(1)} async-done(((f32[32,2,128]{2,1,0:T(2,128)}), f32[32,2,128]{2,1,0:T(2,128)S(1)}, u32[]{:S(2)}, u32[]{:S(2)}) %all-to-all-start.1) | async-done | bytes 32800 | tf_op jit(solution)/shard_map/all_to_all | solution.py:286
  63.6 14.3 %all_to_all.29 = f32[8,80,128]{2,1,0:T(8,128)S(1)} all-to-all(f32[8,80,128]{2,1,0:T(8,128)S(1)} %broadcast_in_dim.5), channel_id=1, replica_groups=mesh['shard'=32,'cent'=8] {'cent'}, dimensions={0} | all-to-all | bytes 655360 | tf_op jit(solution)/shard_map/all_to_all | solution.py:289
  77.9 0.0 copy-done.2
  77.9 0.0 copy-done.3
  77.9 0.8 %finish.1 = (f32[16,4,32]{2,1,0:T(4,128)}, f32[16,32]{1,0:T(8,128)}) custom-call(f32[640,128]{1,0:T(8,128)S(1)} %bitcast.8, s32[16,128]{1,0:T(8,128)S(1)} %copy-done.2, s32[16,128]{1,0:T(8,128)S(1)} %copy-done.3), custom_call_target="tpu_custom_call" | custom-call | tf_op jit(solution)/shard_map/finish/pallas_call | solution.py:256
  (2 shorter events, 0.0 us)
Async XLA Ops:
  2.3 28.8 %all-to-all-start = ((bf16[32,64,128]{2,1,0:T(8,128)(2,1)}), bf16[32,64,128]{2,1,0:T(8,128)(2,1)S(1)}, u32[]{:S(2)}, u32[]{:S(2)}) async-start(bf16[32,64,128]{2,1,0:T(8,128)(2,1)} %broadcast_in_dim.4), calls=%async_computation | async-start | bytes 1048576 | tf_op jit(solution)/shard_map/all_to_all | solution.py:278
  15.9 0.9 %copy-start = (bf16[16,32,128]{2,1,0:T(8,128)(2,1)S(1)}, bf16[16,32,128]{2,1,0:T(8,128)(2,1)}, u32[]{:S(2)}) copy-start(bf16[16,32,128]{2,1,0:T(8,128)(2,1)} %param.6) | copy-start | bytes 393220
  16.8 14.2 %copy-start.5 = (s32[96]{0:T(128)S(1)}, s32[96]{0:T(128)}, u32[]{:S(2)}) copy-start(s32[96]{0:T(128)} %count_ref.1) | copy-start | bytes 1156
  16.8 14.2 %copy-start.6 = (s32[8,128]{1,0:T(8,128)S(1)}, s32[8,128]{1,0:T(8,128)}, u32[]{:S(2)}) copy-start(s32[8,128]{1,0:T(8,128)} %get-tuple-element.22.place_ref) | copy-start | bytes 12292
  16.8 14.2 %copy-start.7 = (s32[1,128]{1,0:T(1,128)S(1)}, s32[1,128]{1,0:T(1,128)}, u32[]{:S(2)}) copy-start(s32[1,128]{1,0:T(1,128)} %get-tuple-element.19.order_ref) | copy-start | bytes 1540
  16.8 14.2 %copy-start.8 = (s32[1,128]{1,0:T(1,128)S(1)}, s32[1,128]{1,0:T(1,128)}, u32[]{:S(2)}) copy-start(s32[1,128]{1,0:T(1,128)} %get-tuple-element.20.tiles_ref) | copy-start | bytes 1540
  31.1 1.9 %copy-start.4 = (bf16[96,128,128]{2,1,0:T(8,128)(2,1)S(1)}, bf16[96,128,128]{2,1,0:T(8,128)(2,1)}, u32[]{:S(2)}) copy-start(bf16[96,128,128]{2,1,0:T(8,128)(2,1)} %p_ref.1) | copy-start | bytes 9437188
  33.0 21.9 %copy-start.1 = (bf16[16,32,128]{2,1,0:T(8,128)(2,1)S(1)}, bf16[16,32,128]{2,1,0:T(8,128)(2,1)}, u32[]{:S(2)}) copy-start(bf16[16,32,128]{2,1,0:T(8,128)(2,1)} %param.6) | copy-start | bytes 393220
  45.5 32.4 %copy-start.2 = (s32[16,128]{1,0:T(8,128)S(1)}, s32[16,128]{1,0:T(8,128)}, u32[]{:S(2)}) copy-start(s32[16,128]{1,0:T(8,128)} %get-tuple-element.26.shard_ref) | copy-start | bytes 24580
  45.5 32.4 %copy-start.3 = (s32[16,128]{1,0:T(8,128)S(1)}, s32[16,128]{1,0:T(8,128)}, u32[]{:S(2)}) copy-start(s32[16,128]{1,0:T(8,128)} %get-tuple-element.27.local_ref) | copy-start | bytes 24580
  45.5 18.1 %all-to-all-start.1 = ((f32[32,2,128]{2,1,0:T(2,128)}), f32[32,2,128]{2,1,0:T(2,128)S(1)}, u32[]{:S(2)}, u32[]{:S(2)}) async-start(f32[32,2,128]{2,1,0:T(2,128)} %bitcast.4), calls=%async_computation.1 | async-start | bytes 65536 | tf_op jit(solution)/shard_map/all_to_all | solution.py:286

commit v7 on v6

--- a/solution.py
+++ b/solution.py
@@ -118,7 +118,7 @@
         out_specs=pl.BlockSpec((rows, LANES), lambda i: (0, 0)),
         out_shape=jax.ShapeDtypeStruct((rows, LANES), jnp.float32),
         scratch_shapes=[pltpu.VMEM((sum(streams(LEVELS)), 8, nq), jnp.float32)],
-        compiler_params=pltpu.CompilerParams(vmem_limit_bytes=24 * MIB),
+        compiler_params=pltpu.CompilerParams(vmem_limit_bytes=58 * MIB),
         cost_estimate=pl.CostEstimate(
             flops=4 * nq * total * dim, bytes_accessed=2 * total * dim, transcendentals=0
         ),
@@ -281,6 +281,7 @@
     lists = probe(tokens, centroids, (), 0, FIRST)
     shard_index, local_index, places, order, tiles = prepare(counts, home, candidates)
     gathered, lists, places, order, tiles = lax.optimization_barrier((gathered, lists, places, order, tiles))
+    gathered = pltpu.with_memory_space_constraint(gathered, pltpu.HBM)
     table = maxsim(counts, order, tiles, gathered, passages, places, nt)
     table, lists = lax.optimization_barrier((table, lists))
     returned = lax.all_to_all(table, "shard", 0, 0, tiled=True)

time: 79.2 us -> 78.5 us (level)
  local copies, waits for them, and re-layouts: 4.47 us -> 1.69 us
  Pallas kernels: 32.2 us -> 34.7 us
    unnamed x18 -> x14, local copies, waits for them, and re-layouts: 2.81 us -> 0.03 us
    pallas_call x2, Pallas kernels: 17.3 us -> 18.7 us  [probe(): pl.pallas_call(probe_kernel, grid=(steps,), in_specs=[pl.BlockSpec((nq, d...]
    pallas_call x1, Pallas kernels: 12.5 us -> 13.5 us  [maxsim(): pl.pallas_call(functools.partial(maxsim_kernel, width=width, tokens=token...]
  transfers between devices with their start and end apart: 2 -> 2, of which waited for: 1 -> 1; matrix products, arithmetic and copies ran while one was open for 0% -> 0% of each run, Pallas kernels for 24% -> 26%
where the time goes in v7:
time: 78.5 us; the launch traced here: 78 us
  Pallas kernels  34.7 us (44%)
  starting transfers between devices  20.9 us (27%)
  blocking collectives  14.3 us (18%)
  waiting for transfers between devices  5.05 us (6%)
  local copies, waits for them, and re-layouts  1.69 us (2%)
    pallas_call x2, Pallas kernels, probe(): pl.pallas_call(probe_kernel, grid=(steps,), in_specs=[pl.BlockSpec((nq, d...  18.7 us
    all_to_all x1, blocking collectives, body(): received = lax.all_to_all(final, 'cent', 0, 0, tiled=True)  14.3 us
    pallas_call x1, Pallas kernels, maxsim(): pl.pallas_call(functools.partial(maxsim_kernel, width=width, tokens=token...  13.5 us
    all_to_all x1, starting transfers between devices, body(): gathered = lax.all_to_all(spread(own, shards), 'shard', 0, 0, tiled=True)  12.2 us
    all_to_all x1, starting transfers between devices, body(): returned = lax.all_to_all(table, 'shard', 0, 0, tiled=True)  8.74 us
    all_to_all x1, waiting for transfers between devices, body(): returned = lax.all_to_all(table, 'shard', 0, 0, tiled=True)  5.04 us
    pallas_call x1, Pallas kernels, prepare(): pl.pallas_call(prepare_kernel, out_shape=[index, index, jax.ShapeDtypeStr...  1.61 us
  transfers between devices with their start and end apart: 2, of which 1 were waited for; matrix products, arithmetic and copies ran while one was open for 0% of the time, Pallas kernels for 26%

profile of v7, /device:TPU:1, one launch (start us, length us, event | category | flops | bytes accessed | tf_op | source)
XLA Modules:
  0.0 78.0 jit_solution(13936223931452626752)
XLA Ops:
  0.6 0.7 constant_dynamic-slice_fusion
  1.4 0.9 %broadcast_in_dim.4 = bf16[32,64,128]{2,1,0:T(8,128)(2,1)} broadcast(bf16[64,128]{1,0:T(8,128)(2,1)S(1)} %constant_dynamic-slice_fusion), dimensions={1,2} | broadcast | bytes 540672 | tf_op jit(solution)/shard_map/broadcast_in_dim | solution.py:268
  2.3 12.2 %all-to-all-start = ((bf16[32,64,128]{2,1,0:T(8,128)(2,1)}), bf16[32,64,128]{2,1,0:T(8,128)(2,1)}, u32[]{:S(2)}, u32[]{:S(2)}) async-start(bf16[32,64,128]{2,1,0:T(8,128)(2,1)} %broadcast_in_dim.4), calls=%async_computation | async-start | bytes 1048576 | tf_op jit(solution)/shard_map/all_to_all | solution.py:278
  14.4 1.6 %prepare.1 = (s32[16,128]{1,0:T(8,128)}, s32[16,128]{1,0:T(8,128)}, s32[8,128]{1,0:T(8,128)}, s32[1,128]{1,0:T(1,128)}, s32[1,128]{1,0:T(1,128)}) custom-call(s32[1,96]{1,0:T(1,128)} %bitcast.9, s32[24,128]{1,0:T(8,128)} %bitcast.15, s32[16,32]{1,0:T(8,128)} %cand_ref.1), custom_call_target="tpu_custom_call" | custom-call | flops 100000000 | bytes 100000 | tf_op jit(solution)/shard_map/prepare/pallas_call | solution.py:160
  16.1 0.0 copy-start.2
  16.1 0.0 copy-start.3
  16.1 0.0 copy-start.4
  16.1 0.0 copy-start.5
  16.1 0.0 copy-start.6
  16.1 15.0 %probe_0.1.refs_0_ = f32[16,128]{1,0:T(8,128)} custom-call(bf16[512,128]{1,0:T(8,128)(2,1)} %bitcast.11, bf16[32768,128]{1,0:T(8,128)(2,1)} %c_ref.3), custom_call_target="tpu_custom_call" | custom-call | flops 7516192768 | bytes 7340032 | tf_op jit(solution)/shard_map/probe_0/pallas_call | solution.py:110
  31.1 0.0 all-to-all-done
  31.1 0.0 copy-done.2
  31.1 0.0 copy-done.3
  31.1 0.0 copy-done.4
  31.1 0.0 copy-done.5
  31.1 0.0 copy-done.6
  31.1 13.5 %maxsim.1 = f32[64,128]{1,0:T(8,128)} custom-call(s32[96]{0:T(128)S(1)} %copy-done.3, s32[1,128]{1,0:T(1,128)S(1)} %copy-done.5, s32[1,128]{1,0:T(1,128)S(1)} %copy-done.6, bf16[2048,128]{1,0:T(8,128)(2,1)} %bitcast.1.g_ref, bf16[96,128,128]{2,1,0:T(8,128)(2,1)S(1)} %copy-done.2, s32[8,128]{1,0:T(8,128)S(1)} %copy-done.4), custom_call_target="tpu_custom_call" | custom-call | flops 6442450944 | bytes 3145728 | tf_op jit(solution)/shard_map/maxsim/pallas_call | solution.py:217
  44.7 0.0 copy-start
  44.7 0.0 copy-start.1
  44.7 8.7 %all-to-all-start.1 = ((f32[32,2,128]{2,1,0:T(2,128)}), f32[32,2,128]{2,1,0:T(2,128)S(1)}, u32[]{:S(2)}, u32[]{:S(2)}) async-start(f32[32,2,128]{2,1,0:T(2,128)} %bitcast.4), calls=%async_computation.1 | async-start | bytes 65536 | tf_op jit(solution)/shard_map/all_to_all | solution.py:287
  53.4 3.7 %probe_7.1 = f32[16,128]{1,0:T(8,128)} custom-call(bf16[512,128]{1,0:T(8,128)(2,1)} %bitcast.12, bf16[32768,128]{1,0:T(8,128)(2,1)} %c_ref.3, f32[16,128]{1,0:T(8,128)} %probe_0.1.refs_0_), custom_call_target="tpu_custom_call" | custom-call | flops 1073741824 | bytes 1048576 | tf_op jit(solution)/shard_map/probe_7/pallas_call | solution.py:110
  57.1 5.0 %all-to-all-done.1 = f32[32,2,128]{2,1,0:T(2,128)S(1)} async-done(((f32[32,2,128]{2,1,0:T(2,128)}), f32[32,2,128]{2,1,0:T(2,128)S(1)}, u32[]{:S(2)}, u32[]{:S(2)}) %all-to-all-start.1) | async-done | bytes 32800 | tf_op jit(solution)/shard_map/all_to_all | solution.py:287
  62.2 0.7 pad_maximum_fusion
  62.9 14.3 %all_to_all.29 = f32[8,80,128]{2,1,0:T(8,128)S(1)} all-to-all(f32[8,80,128]{2,1,0:T(8,128)S(1)} %broadcast_in_dim.5), channel_id=1, replica_groups=mesh['shard'=32,'cent'=8] {'cent'}, dimensions={0} | all-to-all | bytes 655360 | tf_op jit(solution)/shard_map/all_to_all | solution.py:290
  77.2 0.0 copy-done
  77.2 0.0 copy-done.1
  77.2 0.8 %finish.1 = (f32[16,4,32]{2,1,0:T(4,128)}, f32[16,32]{1,0:T(8,128)}) custom-call(f32[640,128]{1,0:T(8,128)S(1)} %bitcast.8, s32[16,128]{1,0:T(8,128)S(1)} %copy-done, s32[16,128]{1,0:T(8,128)S(1)} %copy-done.1), custom_call_target="tpu_custom_call" | custom-call | tf_op jit(solution)/shard_map/finish/pallas_call | solution.py:256
  (1 shorter events, 0.0 us)
Async XLA Ops:
  2.3 28.8 %all-to-all-start = ((bf16[32,64,128]{2,1,0:T(8,128)(2,1)}), bf16[32,64,128]{2,1,0:T(8,128)(2,1)}, u32[]{:S(2)}, u32[]{:S(2)}) async-start(bf16[32,64,128]{2,1,0:T(8,128)(2,1)} %broadcast_in_dim.4), calls=%async_computation | async-start | bytes 1048576 | tf_op jit(solution)/shard_map/all_to_all | solution.py:278
  16.1 15.0 %copy-start.2 = (bf16[96,128,128]{2,1,0:T(8,128)(2,1)S(1)}, bf16[96,128,128]{2,1,0:T(8,128)(2,1)}, u32[]{:S(2)}) copy-start(bf16[96,128,128]{2,1,0:T(8,128)(2,1)} %p_ref.1) | copy-start | bytes 9437188
  16.1 15.0 %copy-start.3 = (s32[96]{0:T(128)S(1)}, s32[96]{0:T(128)}, u32[]{:S(2)}) copy-start(s32[96]{0:T(128)} %count_ref.1) | copy-start | bytes 1156
  16.1 15.0 %copy-start.4 = (s32[8,128]{1,0:T(8,128)S(1)}, s32[8,128]{1,0:T(8,128)}, u32[]{:S(2)}) copy-start(s32[8,128]{1,0:T(8,128)} %get-tuple-element.22.place_ref) | copy-start | bytes 12292
  16.1 15.0 %copy-start.5 = (s32[1,128]{1,0:T(1,128)S(1)}, s32[1,128]{1,0:T(1,128)}, u32[]{:S(2)}) copy-start(s32[1,128]{1,0:T(1,128)} %get-tuple-element.19.order_ref) | copy-start | bytes 1540
  16.1 15.0 %copy-start.6 = (s32[1,128]{1,0:T(1,128)S(1)}, s32[1,128]{1,0:T(1,128)}, u32[]{:S(2)}) copy-start(s32[1,128]{1,0:T(1,128)} %get-tuple-element.20.tiles_ref) | copy-start | bytes 1540
  44.7 32.5 %copy-start = (s32[16,128]{1,0:T(8,128)S(1)}, s32[16,128]{1,0:T(8,128)}, u32[]{:S(2)}) copy-start(s32[16,128]{1,0:T(8,128)} %get-tuple-element.26.shard_ref) | copy-start | bytes 24580
  44.7 32.5 %copy-start.1 = (s32[16,128]{1,0:T(8,128)S(1)}, s32[16,128]{1,0:T(8,128)}, u32[]{:S(2)}) copy-start(s32[16,128]{1,0:T(8,128)} %get-tuple-element.27.local_ref) | copy-start | bytes 24580
  44.7 17.5 %all-to-all-start.1 = ((f32[32,2,128]{2,1,0:T(2,128)}), f32[32,2,128]{2,1,0:T(2,128)S(1)}, u32[]{:S(2)}, u32[]{:S(2)}) async-start(f32[32,2,128]{2,1,0:T(2,128)} %bitcast.4), calls=%async_computation.1 | async-start | bytes 65536 | tf_op jit(solution)/shard_map/all_to_all | solution.py:287

commit v8 on v7

--- a/solution.py
+++ b/solution.py
@@ -14,7 +14,7 @@
 GROUP = 16
 ROWS = 32
 PER = 16
-FIRST = 7
+FIRST = 6
 
 
 def insert(running, x):
@@ -166,10 +166,9 @@
     )(counts.reshape(1, -1), home.reshape(-1, LANES), candidates)
 
 
-def maxsim_kernel(count_ref, order_ref, tiles_ref, g_ref, p_ref, place_ref, o_ref, best_ref, lhs_ref, *, width, tokens):
+def maxsim_kernel(count_ref, order_ref, tiles_ref, g_ref, p_ref, best_ref, lhs_ref, *, width):
     count, length, dim = p_ref.shape
     columns = g_ref.shape[0]
-    best_ref[count:, :] = jnp.zeros((best_ref.shape[0] - count, columns), jnp.float32)
 
     def one(g, carry):
         at = pl.multiple_of(g * PER, PER)
@@ -195,11 +194,34 @@
         return carry
 
     lax.fori_loop(0, count // PER, one, 0)
+
+
+def maxsim(counts, order, tiles, gathered, passages, width=512):
+    columns, dim = gathered.shape
+    count, length, _ = passages.shape
+    vmem = pl.BlockSpec(memory_space=pltpu.VMEM)
+    smem = pl.BlockSpec(memory_space=pltpu.SMEM)
+    return pl.pallas_call(
+        functools.partial(maxsim_kernel, width=width),
+        in_specs=[smem, smem, smem, vmem, vmem],
+        out_specs=vmem,
+        out_shape=jax.ShapeDtypeStruct((count, columns), jnp.float32),
+        scratch_shapes=[pltpu.VMEM((PER * length, dim), jnp.bfloat16)],
+        compiler_params=pltpu.CompilerParams(vmem_limit_bytes=40 * MIB),
+        cost_estimate=pl.CostEstimate(
+            flops=2 * columns * count * length * dim, bytes_accessed=2 * passages.size, transcendentals=0
+        ),
+        name="maxsim",
+    )(counts, order, tiles, gathered, passages)
+
+
+def total_kernel(best_ref, place_ref, o_ref, *, tokens):
+    count, columns = best_ref.shape
     nq = o_ref.shape[0]
-    owner = lax.broadcasted_iota(jnp.int32, (nq, columns), 1) // tokens
+    owner = lax.shift_right_logical(lax.broadcasted_iota(jnp.int32, (nq, columns), 1), tokens.bit_length() - 1)
     pick = (owner == lax.broadcasted_iota(jnp.int32, (nq, columns), 0)).astype(jnp.bfloat16)
-    rest = best_ref[...]
-    total = jnp.zeros((nq, best_ref.shape[0]), jnp.float32)
+    rest = jnp.concatenate([best_ref[...], jnp.zeros((LANES - count, columns), jnp.float32)], axis=0)
+    total = jnp.zeros((nq, LANES), jnp.float32)
     for _ in range(3):
         part = rest.astype(jnp.bfloat16)
         rest = rest - part.astype(jnp.float32)
@@ -208,24 +230,15 @@
     o_ref[...] = jnp.take_along_axis(total, place, axis=1)
 
 
-def maxsim(counts, order, tiles, gathered, passages, places, tokens, width=512):
-    columns, dim = gathered.shape
-    count, length, _ = passages.shape
-    nq = columns // tokens
-    vmem = pl.BlockSpec(memory_space=pltpu.VMEM)
-    smem = pl.BlockSpec(memory_space=pltpu.SMEM)
-    return pl.pallas_call(
-        functools.partial(maxsim_kernel, width=width, tokens=tokens),
-        in_specs=[smem, smem, smem, vmem, vmem, vmem],
-        out_specs=vmem,
+def total_scores(best, places, tokens):
+    nq = best.shape[1] // tokens
+    return pl.pallas_call(
+        functools.partial(total_kernel, tokens=tokens),
         out_shape=jax.ShapeDtypeStruct((nq, LANES), jnp.float32),
-        scratch_shapes=[pltpu.VMEM((LANES, columns), jnp.float32), pltpu.VMEM((PER * length, dim), jnp.bfloat16)],
-        compiler_params=pltpu.CompilerParams(vmem_limit_bytes=40 * MIB),
-        cost_estimate=pl.CostEstimate(
-            flops=2 * columns * count * length * dim, bytes_accessed=2 * passages.size, transcendentals=0
-        ),
-        name="maxsim",
-    )(counts, order, tiles, gathered, passages, places)
+        compiler_params=pltpu.CompilerParams(vmem_limit_bytes=16 * MIB),
+        cost_estimate=pl.CostEstimate(flops=10**8, bytes_accessed=best.size * 4, transcendentals=0),
+        name="total",
+    )(best, places)
 
 
 def finish_kernel(r_ref, shard_ref, local_ref, probe_ref, score_ref, *, shards, cents):
@@ -282,7 +295,8 @@
     shard_index, local_index, places, order, tiles = prepare(counts, home, candidates)
     gathered, lists, places, order, tiles = lax.optimization_barrier((gathered, lists, places, order, tiles))
     gathered = pltpu.with_memory_space_constraint(gathered, pltpu.HBM)
-    table = maxsim(counts, order, tiles, gathered, passages, places, nt)
+    best = maxsim(counts, order, tiles, gathered, passages)
+    table = total_scores(best, places, nt)
     table, lists = lax.optimization_barrier((table, lists))
     returned = lax.all_to_all(table, "shard", 0, 0, tiled=True)
     lists = probe(tokens, centroids, (lists,), FIRST, blocks - FIRST)

time: 78.5 us -> 76.1 us (0.969)
  waiting for transfers between devices: 5.05 us -> 3.18 us
    all_to_all x1, waiting for transfers between devices: 5.04 us -> 3.18 us  [body(): returned = lax.all_to_all(table, 'shard', 0, 0, tiled=True)]
    pallas_call x1 -> x2, Pallas kernels: 13.5 us -> 12.9 us  [the longest x1 11.6 us: maxsim(): pl.pallas_call(functools.partial(maxsim_kernel, width=width), in_specs=[s...]
  transfers between devices with their start and end apart: 2 -> 2, of which waited for: 1 -> 1; matrix products, arithmetic and copies ran while one was open for 0% -> 0% of each run, Pallas kernels for 26% -> 27%
where the time goes in v8:
time: 76.1 us; the launch traced here: 75.4 us
  Pallas kernels  34 us (45%)
  starting transfers between devices  20.8 us (27%)
  blocking collectives  14.3 us (19%)
  waiting for transfers between devices  3.18 us (4%)
  local copies, waits for them, and re-layouts  1.7 us (2%)
    pallas_call x2, Pallas kernels, probe(): pl.pallas_call(probe_kernel, grid=(steps,), in_specs=[pl.BlockSpec((nq, d...  18.7 us
    all_to_all x1, blocking collectives, body(): received = lax.all_to_all(final, 'cent', 0, 0, tiled=True)  14.3 us
    all_to_all x1, starting transfers between devices, body(): gathered = lax.all_to_all(spread(own, shards), 'shard', 0, 0, tiled=True)  12.2 us
    pallas_call x1, Pallas kernels, maxsim(): pl.pallas_call(functools.partial(maxsim_kernel, width=width), in_specs=[s...  11.6 us
    all_to_all x1, starting transfers between devices, body(): returned = lax.all_to_all(table, 'shard', 0, 0, tiled=True)  8.61 us
    all_to_all x1, waiting for transfers between devices, body(): returned = lax.all_to_all(table, 'shard', 0, 0, tiled=True)  3.18 us
    pallas_call x1, Pallas kernels, prepare(): pl.pallas_call(prepare_kernel, out_shape=[index, index, jax.ShapeDtypeStr...  1.61 us
  transfers between devices with their start and end apart: 2, of which 1 were waited for; matrix products, arithmetic and copies ran while one was open for 0% of the time, Pallas kernels for 27%

profile of v8, /device:TPU:1, one launch (start us, length us, event | category | flops | bytes accessed | tf_op | source)
XLA Modules:
  0.0 75.4 jit_solution(8566528186033862044)
XLA Ops:
  0.6 0.7 constant_dynamic-slice_fusion
  1.4 0.9 %broadcast_in_dim.4 = bf16[32,64,128]{2,1,0:T(8,128)(2,1)} broadcast(bf16[64,128]{1,0:T(8,128)(2,1)S(1)} %constant_dynamic-slice_fusion), dimensions={1,2} | broadcast | bytes 540672 | tf_op jit(solution)/shard_map/broadcast_in_dim | solution.py:281
  2.3 12.2 %all-to-all-start = ((bf16[32,64,128]{2,1,0:T(8,128)(2,1)}), bf16[32,64,128]{2,1,0:T(8,128)(2,1)}, u32[]{:S(2)}, u32[]{:S(2)}) async-start(bf16[32,64,128]{2,1,0:T(8,128)(2,1)} %broadcast_in_dim.4), calls=%async_computation | async-start | bytes 1048576 | tf_op jit(solution)/shard_map/all_to_all | solution.py:291
  14.4 1.6 %prepare.1 = (s32[16,128]{1,0:T(8,128)}, s32[16,128]{1,0:T(8,128)}, s32[8,128]{1,0:T(8,128)}, s32[1,128]{1,0:T(1,128)}, s32[1,128]{1,0:T(1,128)}) custom-call(s32[1,96]{1,0:T(1,128)} %bitcast.9, s32[24,128]{1,0:T(8,128)} %bitcast.15, s32[16,32]{1,0:T(8,128)} %cand_ref.1), custom_call_target="tpu_custom_call" | custom-call | flops 100000000 | bytes 100000 | tf_op jit(solution)/shard_map/prepare/pallas_call | solution.py:160
  16.1 0.0 copy-start.3
  16.1 0.0 copy-start.4
  16.1 0.0 copy-start.5
  16.1 0.0 copy-start.6
  16.1 13.1 %probe_0.1.refs_0_ = f32[16,128]{1,0:T(8,128)} custom-call(bf16[512,128]{1,0:T(8,128)(2,1)} %bitcast.11, bf16[32768,128]{1,0:T(8,128)(2,1)} %c_ref.3), custom_call_target="tpu_custom_call" | custom-call | flops 6442450944 | bytes 6291456 | tf_op jit(solution)/shard_map/probe_0/pallas_call | solution.py:110
  29.2 0.0 all-to-all-done
  29.2 0.0 copy-done.3
  29.2 0.0 copy-done.4
  29.2 0.0 copy-done.5
  29.2 0.0 copy-done.6
  29.2 0.0 copy-start.2
  29.3 11.6 %maxsim.1.best_ref = f32[96,2048]{1,0:T(8,128)S(1)} custom-call(s32[96]{0:T(128)S(1)} %copy-done.4, s32[1,128]{1,0:T(1,128)S(1)} %copy-done.5, s32[1,128]{1,0:T(1,128)S(1)} %copy-done.6, bf16[2048,128]{1,0:T(8,128)(2,1)} %bitcast.1.g_ref, bf16[96,128,128]{2,1,0:T(8,128)(2,1)S(1)} %copy-done.3), custom_call_target="tpu_custom_call" | custom-call | flops 6442450944 | bytes 3145728 | tf_op jit(solution)/shard_map/maxsim/pallas_call | solution.py:204
  40.9 0.0 copy-done.2
  40.9 0.0 copy-start
  40.9 0.0 copy-start.1
  40.9 1.3 %total.1 = f32[64,128]{1,0:T(8,128)} custom-call(f32[96,2048]{1,0:T(8,128)S(1)} %maxsim.1.best_ref, s32[8,128]{1,0:T(8,128)S(1)} %copy-done.2), custom_call_target="tpu_custom_call" | custom-call | flops 100000000 | bytes 786432 | tf_op jit(solution)/shard_map/total/pallas_call | solution.py:235
  42.2 8.6 %all-to-all-start.1 = ((f32[32,2,128]{2,1,0:T(2,128)}), f32[32,2,128]{2,1,0:T(2,128)S(1)}, u32[]{:S(2)}, u32[]{:S(2)}) async-start(f32[32,2,128]{2,1,0:T(2,128)} %bitcast.4), calls=%async_computation.1 | async-start | bytes 65536 | tf_op jit(solution)/shard_map/all_to_all | solution.py:301
  50.8 5.6 %probe_6.1 = f32[16,128]{1,0:T(8,128)} custom-call(bf16[512,128]{1,0:T(8,128)(2,1)} %bitcast.12, bf16[32768,128]{1,0:T(8,128)(2,1)} %c_ref.3, f32[16,128]{1,0:T(8,128)} %probe_0.1.refs_0_), custom_call_target="tpu_custom_call" | custom-call | flops 2147483648 | bytes 2097152 | tf_op jit(solution)/shard_map/probe_6/pallas_call | solution.py:110
  56.4 3.2 %all-to-all-done.1 = f32[32,2,128]{2,1,0:T(2,128)S(1)} async-done(((f32[32,2,128]{2,1,0:T(2,128)}), f32[32,2,128]{2,1,0:T(2,128)S(1)}, u32[]{:S(2)}, u32[]{:S(2)}) %all-to-all-start.1) | async-done | bytes 32800 | tf_op jit(solution)/shard_map/all_to_all | solution.py:301
  59.6 0.7 pad_maximum_fusion
  60.3 14.3 %all_to_all.29 = f32[8,80,128]{2,1,0:T(8,128)S(1)} all-to-all(f32[8,80,128]{2,1,0:T(8,128)S(1)} %broadcast_in_dim.5), channel_id=1, replica_groups=mesh['shard'=32,'cent'=8] {'cent'}, dimensions={0} | all-to-all | bytes 655360 | tf_op jit(solution)/shard_map/all_to_all | solution.py:304
  74.6 0.0 copy-done
  74.6 0.0 copy-done.1
  74.6 0.8 %finish.1 = (f32[16,4,32]{2,1,0:T(4,128)}, f32[16,32]{1,0:T(8,128)}) custom-call(f32[640,128]{1,0:T(8,128)S(1)} %bitcast.8, s32[16,128]{1,0:T(8,128)S(1)} %copy-done, s32[16,128]{1,0:T(8,128)S(1)} %copy-done.1), custom_call_target="tpu_custom_call" | custom-call | tf_op jit(solution)/shard_map/finish/pallas_call | solution.py:269
  (1 shorter events, 0.0 us)
Async XLA Ops:
  2.3 26.9 %all-to-all-start = ((bf16[32,64,128]{2,1,0:T(8,128)(2,1)}), bf16[32,64,128]{2,1,0:T(8,128)(2,1)}, u32[]{:S(2)}, u32[]{:S(2)}) async-start(bf16[32,64,128]{2,1,0:T(8,128)(2,1)} %broadcast_in_dim.4), calls=%async_computation | async-start | bytes 1048576 | tf_op jit(solution)/shard_map/all_to_all | solution.py:291
  16.1 13.2 %copy-start.3 = (bf16[96,128,128]{2,1,0:T(8,128)(2,1)S(1)}, bf16[96,128,128]{2,1,0:T(8,128)(2,1)}, u32[]{:S(2)}) copy-start(bf16[96,128,128]{2,1,0:T(8,128)(2,1)} %p_ref.1) | copy-start | bytes 9437188
  16.1 13.2 %copy-start.4 = (s32[96]{0:T(128)S(1)}, s32[96]{0:T(128)}, u32[]{:S(2)}) copy-start(s32[96]{0:T(128)} %count_ref.1) | copy-start | bytes 1156
  16.1 13.2 %copy-start.5 = (s32[1,128]{1,0:T(1,128)S(1)}, s32[1,128]{1,0:T(1,128)}, u32[]{:S(2)}) copy-start(s32[1,128]{1,0:T(1,128)} %get-tuple-element.19.order_ref) | copy-start | bytes 1540
  16.1 13.2 %copy-start.6 = (s32[1,128]{1,0:T(1,128)S(1)}, s32[1,128]{1,0:T(1,128)}, u32[]{:S(2)}) copy-start(s32[1,128]{1,0:T(1,128)} %get-tuple-element.20.tiles_ref) | copy-start | bytes 1540
  29.2 11.6 %copy-start.2 = (s32[8,128]{1,0:T(8,128)S(1)}, s32[8,128]{1,0:T(8,128)}, u32[]{:S(2)}) copy-start(s32[8,128]{1,0:T(8,128)} %get-tuple-element.22.place_ref) | copy-start | bytes 12292
  40.9 33.7 %copy-start = (s32[16,128]{1,0:T(8,128)S(1)}, s32[16,128]{1,0:T(8,128)}, u32[]{:S(2)}) copy-start(s32[16,128]{1,0:T(8,128)} %get-tuple-element.26.shard_ref) | copy-start | bytes 24580
  40.9 33.7 %copy-start.1 = (s32[16,128]{1,0:T(8,128)S(1)}, s32[16,128]{1,0:T(8,128)}, u32[]{:S(2)}) copy-start(s32[16,128]{1,0:T(8,128)} %get-tuple-element.27.local_ref) | copy-start | bytes 24580
  42.2 17.4 %all-to-all-start.1 = ((f32[32,2,128]{2,1,0:T(2,128)}), f32[32,2,128]{2,1,0:T(2,128)S(1)}, u32[]{:S(2)}, u32[]{:S(2)}) async-start(f32[32,2,128]{2,1,0:T(2,128)} %bitcast.4), calls=%async_computation.1 | async-start | bytes 65536 | tf_op jit(solution)/shard_map/all_to_all | solution.py:301

commit v9 on v7

--- a/solution.py
+++ b/solution.py
@@ -14,7 +14,7 @@
 GROUP = 16
 ROWS = 32
 PER = 16
-FIRST = 7
+FIRST = 5
 
 
 def insert(running, x):
@@ -166,10 +166,17 @@
     )(counts.reshape(1, -1), home.reshape(-1, LANES), candidates)
 
 
-def maxsim_kernel(count_ref, order_ref, tiles_ref, g_ref, p_ref, place_ref, o_ref, best_ref, lhs_ref, *, width, tokens):
+def maxsim_kernel(
+    count_ref, order_ref, tiles_ref, sent_ref, p_ref, place_ref, o_ref, best_ref, lhs_ref, g_ref, *, width, tokens, mine
+):
     count, length, dim = p_ref.shape
     columns = g_ref.shape[0]
-    best_ref[count:, :] = jnp.zeros((best_ref.shape[0] - count, columns), jnp.float32)
+    nq = o_ref.shape[0]
+    shards, eights = nq // mine, tokens // 8
+    for shard in range(shards):
+        for k in range(mine * eights):
+            to, at_row = (k * shards + shard) * 8, (shard * mine * eights + k) * 8
+            g_ref[to : to + 8, :] = sent_ref[at_row : at_row + 8, :]
 
     def one(g, carry):
         at = pl.multiple_of(g * PER, PER)
@@ -195,31 +202,43 @@
         return carry
 
     lax.fori_loop(0, count // PER, one, 0)
-    nq = o_ref.shape[0]
-    owner = lax.broadcasted_iota(jnp.int32, (nq, columns), 1) // tokens
-    pick = (owner == lax.broadcasted_iota(jnp.int32, (nq, columns), 0)).astype(jnp.bfloat16)
-    rest = best_ref[...]
-    total = jnp.zeros((nq, best_ref.shape[0]), jnp.float32)
+    wide = shards * 8
+    rest = jnp.concatenate(
+        [sum(best_ref[:, (j * eights + k) * wide : (j * eights + k + 1) * wide] for k in range(eights)) for j in range(mine)],
+        axis=1,
+    )
+    column = lax.broadcasted_iota(jnp.int32, (nq, mine * wide), 1)
+    owner = lax.shift_right_logical(column % wide, 3) * mine + column // wide
+    pick = (owner == lax.broadcasted_iota(jnp.int32, (nq, mine * wide), 0)).astype(jnp.bfloat16)
+    parts = []
     for _ in range(3):
-        part = rest.astype(jnp.bfloat16)
-        rest = rest - part.astype(jnp.float32)
-        total += lax.dot_general(pick, part, (((1,), (1,)), ((), ())), preferred_element_type=jnp.float32)
-    place = jnp.broadcast_to(place_ref[0:1, :], total.shape)
-    o_ref[...] = jnp.take_along_axis(total, place, axis=1)
-
-
-def maxsim(counts, order, tiles, gathered, passages, places, tokens, width=512):
+        parts.append(rest.astype(jnp.bfloat16))
+        rest = rest - parts[-1].astype(jnp.float32)
+    sums = lax.dot_general(
+        jnp.concatenate(parts, axis=0), pick, (((1,), (1,)), ((), ())), preferred_element_type=jnp.float32
+    )
+    sums = sums[:count] + sums[count : 2 * count] + sums[2 * count :]
+    sums = jnp.concatenate([sums, jnp.zeros((LANES - count, nq), jnp.float32)], axis=0)
+    place = jnp.broadcast_to(place_ref[0:1, :], o_ref.shape)
+    o_ref[...] = jnp.take_along_axis(sums.T, place, axis=1)
+
+
+def maxsim(counts, order, tiles, gathered, passages, places, tokens, mine, width=512):
     columns, dim = gathered.shape
     count, length, _ = passages.shape
     nq = columns // tokens
     vmem = pl.BlockSpec(memory_space=pltpu.VMEM)
     smem = pl.BlockSpec(memory_space=pltpu.SMEM)
     return pl.pallas_call(
-        functools.partial(maxsim_kernel, width=width, tokens=tokens),
+        functools.partial(maxsim_kernel, width=width, tokens=tokens, mine=mine),
         in_specs=[smem, smem, smem, vmem, vmem, vmem],
         out_specs=vmem,
         out_shape=jax.ShapeDtypeStruct((nq, LANES), jnp.float32),
-        scratch_shapes=[pltpu.VMEM((LANES, columns), jnp.float32), pltpu.VMEM((PER * length, dim), jnp.bfloat16)],
+        scratch_shapes=[
+            pltpu.VMEM((count, columns), jnp.float32),
+            pltpu.VMEM((PER * length, dim), jnp.bfloat16),
+            pltpu.VMEM(gathered.shape, gathered.dtype),
+        ],
         compiler_params=pltpu.CompilerParams(vmem_limit_bytes=40 * MIB),
         cost_estimate=pl.CostEstimate(
             flops=2 * columns * count * length * dim, bytes_accessed=2 * passages.size, transcendentals=0
@@ -282,7 +301,7 @@
     shard_index, local_index, places, order, tiles = prepare(counts, home, candidates)
     gathered, lists, places, order, tiles = lax.optimization_barrier((gathered, lists, places, order, tiles))
     gathered = pltpu.with_memory_space_constraint(gathered, pltpu.HBM)
-    table = maxsim(counts, order, tiles, gathered, passages, places, nt)
+    table = maxsim(counts, order, tiles, gathered, passages, places, nt, mine)
     table, lists = lax.optimization_barrier((table, lists))
     returned = lax.all_to_all(table, "shard", 0, 0, tiled=True)
     lists = probe(tokens, centroids, (lists,), FIRST, blocks - FIRST)

time: 78.5 us -> 74.3 us (0.946)
  waiting for transfers between devices: 5.05 us -> 2.69 us
  Pallas kernels: 34.7 us -> 33.8 us
  starting transfers between devices: 20.9 us -> 20.1 us
    all_to_all x1, waiting for transfers between devices: 5.04 us -> 1.34 us  [body(): returned = lax.all_to_all(table, 'shard', 0, 0, tiled=True)]
    all_to_all x1, waiting for transfers between devices: 0.01 us -> 1.35 us  [body(): gathered = lax.all_to_all(spread(own, shards), 'shard', 0, 0, tiled=True)]
    pallas_call x1, Pallas kernels: 13.5 us -> 12.7 us  [maxsim(): pl.pallas_call(functools.partial(maxsim_kernel, width=width, tokens=token...]
    all_to_all x1, starting transfers between devices: 8.74 us -> 7.94 us  [body(): returned = lax.all_to_all(table, 'shard', 0, 0, tiled=True)]
  transfers between devices with their start and end apart: 2 -> 2, of which waited for: 1 -> 2; matrix products, arithmetic and copies ran while one was open for 0% -> 0% of each run, Pallas kernels for 26% -> 27%
where the time goes in v9:
time: 74.3 us; the launch traced here: 74 us
  Pallas kernels  33.8 us (45%)
  starting transfers between devices  20.1 us (27%)
  blocking collectives  14.3 us (19%)
  waiting for transfers between devices  2.69 us (4%)
  local copies, waits for them, and re-layouts  1.69 us (2%)
    pallas_call x2, Pallas kernels, probe(): pl.pallas_call(probe_kernel, grid=(steps,), in_specs=[pl.BlockSpec((nq, d...  18.7 us
    all_to_all x1, blocking collectives, body(): received = lax.all_to_all(final, 'cent', 0, 0, tiled=True)  14.3 us
    pallas_call x1, Pallas kernels, maxsim(): pl.pallas_call(functools.partial(maxsim_kernel, width=width, tokens=token...  12.7 us
    all_to_all x1, starting transfers between devices, body(): gathered = lax.all_to_all(spread(own, shards), 'shard', 0, 0, tiled=True)  12.2 us
    all_to_all x1, starting transfers between devices, body(): returned = lax.all_to_all(table, 'shard', 0, 0, tiled=True)  7.94 us
    pallas_call x1, Pallas kernels, prepare(): pl.pallas_call(prepare_kernel, out_shape=[index, index, jax.ShapeDtypeStr...  1.61 us
  transfers between devices with their start and end apart: 2, of which 2 were waited for; matrix products, arithmetic and copies ran while one was open for 0% of the time, Pallas kernels for 27%

profile of v9, /device:TPU:1, one launch (start us, length us, event | category | flops | bytes accessed | tf_op | source)
XLA Modules:
  0.0 74.0 jit_solution(15006841578169452034)
XLA Ops:
  0.6 0.7 constant_dynamic-slice_fusion
  1.4 0.9 %broadcast_in_dim.4 = bf16[32,64,128]{2,1,0:T(8,128)(2,1)} broadcast(bf16[64,128]{1,0:T(8,128)(2,1)S(1)} %constant_dynamic-slice_fusion), dimensions={1,2} | broadcast | bytes 540672 | tf_op jit(solution)/shard_map/broadcast_in_dim | solution.py:287
  2.3 12.2 %all-to-all-start = ((bf16[32,64,128]{2,1,0:T(8,128)(2,1)}), bf16[32,64,128]{2,1,0:T(8,128)(2,1)}, u32[]{:S(2)}, u32[]{:S(2)}) async-start(bf16[32,64,128]{2,1,0:T(8,128)(2,1)} %broadcast_in_dim.4), calls=%async_computation | async-start | bytes 1048576 | tf_op jit(solution)/shard_map/all_to_all | solution.py:297
  14.4 1.6 %prepare.1 = (s32[16,128]{1,0:T(8,128)}, s32[16,128]{1,0:T(8,128)}, s32[8,128]{1,0:T(8,128)}, s32[1,128]{1,0:T(1,128)}, s32[1,128]{1,0:T(1,128)}) custom-call(s32[1,96]{1,0:T(1,128)} %bitcast.9, s32[24,128]{1,0:T(8,128)} %bitcast.15, s32[16,32]{1,0:T(8,128)} %cand_ref.1), custom_call_target="tpu_custom_call" | custom-call | flops 100000000 | bytes 100000 | tf_op jit(solution)/shard_map/prepare/pallas_call | solution.py:160
  16.1 0.0 copy-start.2
  16.1 0.0 copy-start.3
  16.1 0.0 copy-start.4
  16.1 0.0 copy-start.5
  16.1 0.0 copy-start.6
  16.1 11.3 %probe_0.1.refs_0_ = f32[16,128]{1,0:T(8,128)} custom-call(bf16[512,128]{1,0:T(8,128)(2,1)} %bitcast.12, bf16[32768,128]{1,0:T(8,128)(2,1)} %c_ref.3), custom_call_target="tpu_custom_call" | custom-call | flops 5368709120 | bytes 5242880 | tf_op jit(solution)/shard_map/probe_0/pallas_call | solution.py:110
  27.4 1.4 %all-to-all-done = bf16[32,64,128]{2,1,0:T(8,128)(2,1)} async-done(((bf16[32,64,128]{2,1,0:T(8,128)(2,1)}), bf16[32,64,128]{2,1,0:T(8,128)(2,1)}, u32[]{:S(2)}, u32[]{:S(2)}) %all-to-all-start) | async-done | bytes 524320 | tf_op jit(solution)/shard_map/all_to_all | solution.py:297
  28.7 0.0 copy-done.2
  28.7 0.0 copy-done.3
  28.7 0.0 copy-done.4
  28.7 0.0 copy-done.5
  28.8 0.0 copy-done.6
  28.8 12.7 %maxsim.1 = f32[64,128]{1,0:T(8,128)} custom-call(s32[96]{0:T(128)S(1)} %copy-done.3, s32[1,128]{1,0:T(1,128)S(1)} %copy-done.5, s32[1,128]{1,0:T(1,128)S(1)} %copy-done.6, bf16[2048,128]{1,0:T(8,128)(2,1)} %bitcast.1.sent_ref, bf16[96,128,128]{2,1,0:T(8,128)(2,1)S(1)} %copy-done.2, s32[8,128]{1,0:T(8,128)S(1)} %copy-done.4), custom_call_target="tpu_custom_call" | custom-call | flops 6442450944 | bytes 3145728 | tf_op jit(solution)/shard_map/maxsim/pallas_call | solution.py:232
  41.5 0.0 copy-start
  41.5 0.0 copy-start.1
  41.5 7.9 %all-to-all-start.1 = ((f32[32,2,128]{2,1,0:T(2,128)}), f32[32,2,128]{2,1,0:T(2,128)S(1)}, u32[]{:S(2)}, u32[]{:S(2)}) async-start(f32[32,2,128]{2,1,0:T(2,128)} %bitcast.4), calls=%async_computation.1 | async-start | bytes 65536 | tf_op jit(solution)/shard_map/all_to_all | solution.py:306
  49.4 7.4 %probe_5.1 = f32[16,128]{1,0:T(8,128)} custom-call(bf16[512,128]{1,0:T(8,128)(2,1)} %bitcast.13, bf16[32768,128]{1,0:T(8,128)(2,1)} %c_ref.3, f32[16,128]{1,0:T(8,128)} %probe_0.1.refs_0_), custom_call_target="tpu_custom_call" | custom-call | flops 3221225472 | bytes 3145728 | tf_op jit(solution)/shard_map/probe_5/pallas_call | solution.py:110
  56.8 1.3 %all-to-all-done.1 = f32[32,2,128]{2,1,0:T(2,128)S(1)} async-done(((f32[32,2,128]{2,1,0:T(2,128)}), f32[32,2,128]{2,1,0:T(2,128)S(1)}, u32[]{:S(2)}, u32[]{:S(2)}) %all-to-all-start.1) | async-done | bytes 32800 | tf_op jit(solution)/shard_map/all_to_all | solution.py:306
  58.2 0.7 pad_maximum_fusion
  58.9 14.3 %all_to_all.29 = f32[8,80,128]{2,1,0:T(8,128)S(1)} all-to-all(f32[8,80,128]{2,1,0:T(8,128)S(1)} %broadcast_in_dim.5), channel_id=1, replica_groups=mesh['shard'=32,'cent'=8] {'cent'}, dimensions={0} | all-to-all | bytes 655360 | tf_op jit(solution)/shard_map/all_to_all | solution.py:309
  73.2 0.0 copy-done
  73.2 0.0 copy-done.1
  73.2 0.8 %finish.1 = (f32[16,4,32]{2,1,0:T(4,128)}, f32[16,32]{1,0:T(8,128)}) custom-call(f32[640,128]{1,0:T(8,128)S(1)} %bitcast.8, s32[16,128]{1,0:T(8,128)S(1)} %copy-done, s32[16,128]{1,0:T(8,128)S(1)} %copy-done.1), custom_call_target="tpu_custom_call" | custom-call | tf_op jit(solution)/shard_map/finish/pallas_call | solution.py:275
  (1 shorter events, 0.0 us)
Async XLA Ops:
  2.3 26.5 %all-to-all-start = ((bf16[32,64,128]{2,1,0:T(8,128)(2,1)}), bf16[32,64,128]{2,1,0:T(8,128)(2,1)}, u32[]{:S(2)}, u32[]{:S(2)}) async-start(bf16[32,64,128]{2,1,0:T(8,128)(2,1)} %broadcast_in_dim.4), calls=%async_computation | async-start | bytes 1048576 | tf_op jit(solution)/shard_map/all_to_all | solution.py:297
  16.1 12.7 %copy-start.2 = (bf16[96,128,128]{2,1,0:T(8,128)(2,1)S(1)}, bf16[96,128,128]{2,1,0:T(8,128)(2,1)}, u32[]{:S(2)}) copy-start(bf16[96,128,128]{2,1,0:T(8,128)(2,1)} %p_ref.1) | copy-start | bytes 9437188
  16.1 12.7 %copy-start.3 = (s32[96]{0:T(128)S(1)}, s32[96]{0:T(128)}, u32[]{:S(2)}) copy-start(s32[96]{0:T(128)} %count_ref.1) | copy-start | bytes 1156
  16.1 12.7 %copy-start.4 = (s32[8,128]{1,0:T(8,128)S(1)}, s32[8,128]{1,0:T(8,128)}, u32[]{:S(2)}) copy-start(s32[8,128]{1,0:T(8,128)} %get-tuple-element.22.place_ref) | copy-start | bytes 12292
  16.1 12.7 %copy-start.5 = (s32[1,128]{1,0:T(1,128)S(1)}, s32[1,128]{1,0:T(1,128)}, u32[]{:S(2)}) copy-start(s32[1,128]{1,0:T(1,128)} %get-tuple-element.19.order_ref) | copy-start | bytes 1540
  16.1 12.7 %copy-start.6 = (s32[1,128]{1,0:T(1,128)S(1)}, s32[1,128]{1,0:T(1,128)}, u32[]{:S(2)}) copy-start(s32[1,128]{1,0:T(1,128)} %get-tuple-element.20.tiles_ref) | copy-start | bytes 1540
  41.5 31.7 %copy-start = (s32[16,128]{1,0:T(8,128)S(1)}, s32[16,128]{1,0:T(8,128)}, u32[]{:S(2)}) copy-start(s32[16,128]{1,0:T(8,128)} %get-tuple-element.26.shard_ref) | copy-start | bytes 24580
  41.5 31.7 %copy-start.1 = (s32[16,128]{1,0:T(8,128)S(1)}, s32[16,128]{1,0:T(8,128)}, u32[]{:S(2)}) copy-start(s32[16,128]{1,0:T(8,128)} %get-tuple-element.27.local_ref) | copy-start | bytes 24580
  41.5 16.7 %all-to-all-start.1 = ((f32[32,2,128]{2,1,0:T(2,128)}), f32[32,2,128]{2,1,0:T(2,128)S(1)}, u32[]{:S(2)}, u32[]{:S(2)}) async-start(f32[32,2,128]{2,1,0:T(2,128)} %bitcast.4), calls=%async_computation.1 | async-start | bytes 65536 | tf_op jit(solution)/shard_map/all_to_all | solution.py:306

commit v10 on v9

--- a/solution.py
+++ b/solution.py
@@ -14,7 +14,7 @@
 GROUP = 16
 ROWS = 32
 PER = 16
-FIRST = 5
+FIRST = 6
 
 
 def insert(running, x):

time: 74.3 us -> 76.1 us (1.024)
  starting transfers between devices: 20.1 us -> 21.4 us
    all_to_all x1, waiting for transfers between devices: 1.34 us -> 3.18 us  [body(): returned = lax.all_to_all(table, 'shard', 0, 0, tiled=True)]
    all_to_all x1, waiting for transfers between devices: 1.35 us -> 0.01 us  [body(): gathered = lax.all_to_all(spread(own, shards), 'shard', 0, 0, tiled=True)]
    all_to_all x1, starting transfers between devices: 7.94 us -> 9.28 us  [body(): returned = lax.all_to_all(table, 'shard', 0, 0, tiled=True)]
  transfers between devices with their start and end apart: 2 -> 2, of which waited for: 2 -> 1; matrix products, arithmetic and copies ran while one was open for 0% -> 0% of each run, Pallas kernels for 27% -> 27%
where the time goes in v10:
time: 76.1 us; the launch traced here: 75.3 us
  Pallas kernels  33.3 us (44%)
  starting transfers between devices  21.4 us (28%)
  blocking collectives  14.3 us (19%)
  waiting for transfers between devices  3.18 us (4%)
  local copies, waits for them, and re-layouts  1.69 us (2%)
    pallas_call x2, Pallas kernels, probe(): pl.pallas_call(probe_kernel, grid=(steps,), in_specs=[pl.BlockSpec((nq, d...  18.7 us
    all_to_all x1, blocking collectives, body(): received = lax.all_to_all(final, 'cent', 0, 0, tiled=True)  14.3 us
    all_to_all x1, starting transfers between devices, body(): gathered = lax.all_to_all(spread(own, shards), 'shard', 0, 0, tiled=True)  12.2 us
    pallas_call x1, Pallas kernels, maxsim(): pl.pallas_call(functools.partial(maxsim_kernel, width=width, tokens=token...  12.1 us
    all_to_all x1, starting transfers between devices, body(): returned = lax.all_to_all(table, 'shard', 0, 0, tiled=True)  9.28 us
    all_to_all x1, waiting for transfers between devices, body(): returned = lax.all_to_all(table, 'shard', 0, 0, tiled=True)  3.18 us
    pallas_call x1, Pallas kernels, prepare(): pl.pallas_call(prepare_kernel, out_shape=[index, index, jax.ShapeDtypeStr...  1.61 us
  transfers between devices with their start and end apart: 2, of which 1 were waited for; matrix products, arithmetic and copies ran while one was open for 0% of the time, Pallas kernels for 27%

profile of v10, /device:TPU:1, one launch (start us, length us, event | category | flops | bytes accessed | tf_op | source)
XLA Modules:
  0.0 75.3 jit_solution(15210722518118760886)
XLA Ops:
  0.6 0.7 constant_dynamic-slice_fusion
  1.4 0.9 %broadcast_in_dim.4 = bf16[32,64,128]{2,1,0:T(8,128)(2,1)} broadcast(bf16[64,128]{1,0:T(8,128)(2,1)S(1)} %constant_dynamic-slice_fusion), dimensions={1,2} | broadcast | bytes 540672 | tf_op jit(solution)/shard_map/broadcast_in_dim | solution.py:287
  2.3 12.2 %all-to-all-start = ((bf16[32,64,128]{2,1,0:T(8,128)(2,1)}), bf16[32,64,128]{2,1,0:T(8,128)(2,1)}, u32[]{:S(2)}, u32[]{:S(2)}) async-start(bf16[32,64,128]{2,1,0:T(8,128)(2,1)} %broadcast_in_dim.4), calls=%async_computation | async-start | bytes 1048576 | tf_op jit(solution)/shard_map/all_to_all | solution.py:297
  14.4 1.6 %prepare.1 = (s32[16,128]{1,0:T(8,128)}, s32[16,128]{1,0:T(8,128)}, s32[8,128]{1,0:T(8,128)}, s32[1,128]{1,0:T(1,128)}, s32[1,128]{1,0:T(1,128)}) custom-call(s32[1,96]{1,0:T(1,128)} %bitcast.9, s32[24,128]{1,0:T(8,128)} %bitcast.15, s32[16,32]{1,0:T(8,128)} %cand_ref.1), custom_call_target="tpu_custom_call" | custom-call | flops 100000000 | bytes 100000 | tf_op jit(solution)/shard_map/prepare/pallas_call | solution.py:160
  16.1 0.0 copy-start.2
  16.1 0.0 copy-start.3
  16.1 0.0 copy-start.4
  16.1 0.0 copy-start.5
  16.1 0.0 copy-start.6
  16.1 13.1 %probe_0.1.refs_0_ = f32[16,128]{1,0:T(8,128)} custom-call(bf16[512,128]{1,0:T(8,128)(2,1)} %bitcast.11, bf16[32768,128]{1,0:T(8,128)(2,1)} %c_ref.3), custom_call_target="tpu_custom_call" | custom-call | flops 6442450944 | bytes 6291456 | tf_op jit(solution)/shard_map/probe_0/pallas_call | solution.py:110
  29.2 0.0 all-to-all-done
  29.2 0.0 copy-done.2
  29.2 0.0 copy-done.3
  29.2 0.0 copy-done.4
  29.3 0.0 copy-done.5
  29.3 0.0 copy-done.6
  29.3 12.1 %maxsim.1 = f32[64,128]{1,0:T(8,128)} custom-call(s32[96]{0:T(128)S(1)} %copy-done.3, s32[1,128]{1,0:T(1,128)S(1)} %copy-done.5, s32[1,128]{1,0:T(1,128)S(1)} %copy-done.6, bf16[2048,128]{1,0:T(8,128)(2,1)} %bitcast.1.sent_ref, bf16[96,128,128]{2,1,0:T(8,128)(2,1)S(1)} %copy-done.2, s32[8,128]{1,0:T(8,128)S(1)} %copy-done.4), custom_call_target="tpu_custom_call" | custom-call | flops 6442450944 | bytes 3145728 | tf_op jit(solution)/shard_map/maxsim/pallas_call | solution.py:232
  41.4 0.0 copy-start
  41.4 0.0 copy-start.1
  41.4 9.3 %all-to-all-start.1 = ((f32[32,2,128]{2,1,0:T(2,128)}), f32[32,2,128]{2,1,0:T(2,128)S(1)}, u32[]{:S(2)}, u32[]{:S(2)}) async-start(f32[32,2,128]{2,1,0:T(2,128)} %bitcast.4), calls=%async_computation.1 | async-start | bytes 65536 | tf_op jit(solution)/shard_map/all_to_all | solution.py:306
  50.7 5.6 %probe_6.1 = f32[16,128]{1,0:T(8,128)} custom-call(bf16[512,128]{1,0:T(8,128)(2,1)} %bitcast.12, bf16[32768,128]{1,0:T(8,128)(2,1)} %c_ref.3, f32[16,128]{1,0:T(8,128)} %probe_0.1.refs_0_), custom_call_target="tpu_custom_call" | custom-call | flops 2147483648 | bytes 2097152 | tf_op jit(solution)/shard_map/probe_6/pallas_call | solution.py:110
  56.3 3.2 %all-to-all-done.1 = f32[32,2,128]{2,1,0:T(2,128)S(1)} async-done(((f32[32,2,128]{2,1,0:T(2,128)}), f32[32,2,128]{2,1,0:T(2,128)S(1)}, u32[]{:S(2)}, u32[]{:S(2)}) %all-to-all-start.1) | async-done | bytes 32800 | tf_op jit(solution)/shard_map/all_to_all | solution.py:306
  59.5 0.7 pad_maximum_fusion
  60.2 14.3 %all_to_all.29 = f32[8,80,128]{2,1,0:T(8,128)S(1)} all-to-all(f32[8,80,128]{2,1,0:T(8,128)S(1)} %broadcast_in_dim.5), channel_id=1, replica_groups=mesh['shard'=32,'cent'=8] {'cent'}, dimensions={0} | all-to-all | bytes 655360 | tf_op jit(solution)/shard_map/all_to_all | solution.py:309
  74.5 0.0 copy-done
  74.5 0.0 copy-done.1
  74.5 0.8 %finish.1 = (f32[16,4,32]{2,1,0:T(4,128)}, f32[16,32]{1,0:T(8,128)}) custom-call(f32[640,128]{1,0:T(8,128)S(1)} %bitcast.8, s32[16,128]{1,0:T(8,128)S(1)} %copy-done, s32[16,128]{1,0:T(8,128)S(1)} %copy-done.1), custom_call_target="tpu_custom_call" | custom-call | tf_op jit(solution)/shard_map/finish/pallas_call | solution.py:275
  (1 shorter events, 0.0 us)
Async XLA Ops:
  2.3 27.0 %all-to-all-start = ((bf16[32,64,128]{2,1,0:T(8,128)(2,1)}), bf16[32,64,128]{2,1,0:T(8,128)(2,1)}, u32[]{:S(2)}, u32[]{:S(2)}) async-start(bf16[32,64,128]{2,1,0:T(8,128)(2,1)} %broadcast_in_dim.4), calls=%async_computation | async-start | bytes 1048576 | tf_op jit(solution)/shard_map/all_to_all | solution.py:297
  16.1 13.2 %copy-start.2 = (bf16[96,128,128]{2,1,0:T(8,128)(2,1)S(1)}, bf16[96,128,128]{2,1,0:T(8,128)(2,1)}, u32[]{:S(2)}) copy-start(bf16[96,128,128]{2,1,0:T(8,128)(2,1)} %p_ref.1) | copy-start | bytes 9437188
  16.1 13.2 %copy-start.3 = (s32[96]{0:T(128)S(1)}, s32[96]{0:T(128)}, u32[]{:S(2)}) copy-start(s32[96]{0:T(128)} %count_ref.1) | copy-start | bytes 1156
  16.1 13.2 %copy-start.4 = (s32[8,128]{1,0:T(8,128)S(1)}, s32[8,128]{1,0:T(8,128)}, u32[]{:S(2)}) copy-start(s32[8,128]{1,0:T(8,128)} %get-tuple-element.22.place_ref) | copy-start | bytes 12292
  16.1 13.2 %copy-start.5 = (s32[1,128]{1,0:T(1,128)S(1)}, s32[1,128]{1,0:T(1,128)}, u32[]{:S(2)}) copy-start(s32[1,128]{1,0:T(1,128)} %get-tuple-element.19.order_ref) | copy-start | bytes 1540
  16.1 13.2 %copy-start.6 = (s32[1,128]{1,0:T(1,128)S(1)}, s32[1,128]{1,0:T(1,128)}, u32[]{:S(2)}) copy-start(s32[1,128]{1,0:T(1,128)} %get-tuple-element.20.tiles_ref) | copy-start | bytes 1540
  41.4 33.1 %copy-start = (s32[16,128]{1,0:T(8,128)S(1)}, s32[16,128]{1,0:T(8,128)}, u32[]{:S(2)}) copy-start(s32[16,128]{1,0:T(8,128)} %get-tuple-element.26.shard_ref) | copy-start | bytes 24580
  41.4 33.1 %copy-start.1 = (s32[16,128]{1,0:T(8,128)S(1)}, s32[16,128]{1,0:T(8,128)}, u32[]{:S(2)}) copy-start(s32[16,128]{1,0:T(8,128)} %get-tuple-element.27.local_ref) | copy-start | bytes 24580
  41.4 18.1 %all-to-all-start.1 = ((f32[32,2,128]{2,1,0:T(2,128)}), f32[32,2,128]{2,1,0:T(2,128)S(1)}, u32[]{:S(2)}, u32[]{:S(2)}) async-start(f32[32,2,128]{2,1,0:T(2,128)} %bitcast.4), calls=%async_computation.1 | async-start | bytes 65536 | tf_op jit(solution)/shard_map/all_to_all | solution.py:306
